TPU v7x, 32 devices: a whole 2x2x4 slice. The times are simulated.
32 devices in a mesh: dp: 8 (over y, x, core), tensor: 4 (over z).
Axes of the slice: x: 2, y: 2, z: 4, core: 2. Of those that a mesh axis runs over, the one named last changes fastest.
Arguments:
- tokens: bfloat16 [4096, 2048], P(('dp', 'tensor')), may hold values from -6 to 6
- file_ids: int32 [8, 512], P('dp'), may hold values from 0 to 7, never falling along the last dimension, each value on 1 to 256 neighbouring positions
- expert_ids: int32 [4096, 8], P(('dp', 'tensor')), may hold values from 0 to 15, all different within a row; in each aligned block of 128 rows (0 to 127, 128 to 255, ...) at most 72 rows name the same one
- attention_norm_gain: float32 [2048], replicated, may hold values from 0.5 to 1.5
- w_query: bfloat16 [2048, 2048], P(None, 'tensor'), as said below
- w_key: bfloat16 [2048, 2048], P(None, 'tensor'), as said below
- w_value: bfloat16 [2048, 2048], P(None, 'tensor'), may hold values from -0.125 to 0.125
- query_gain: float32 [2048], P('tensor'), may hold values from 0.5 to 1.5
- key_gain: float32 [2048], P('tensor'), may hold values from 0.5 to 1.5
- w_output: bfloat16 [2048, 2048], P('tensor'), may hold values from -1 to 1
- expert_norm_gain: float32 [2048], replicated, may hold values from 0.5 to 1.5
- w_router: bfloat16 [2048, 16], replicated, may hold values from -0.0625 to 0.0625
- w_gate: bfloat16 [16, 2048, 1024], P('dp', None, 'tensor'), may hold values from -0.125 to 0.125
- w_up: bfloat16 [16, 2048, 1024], P('dp', None, 'tensor'), may hold values from -0.125 to 0.125
- w_down: bfloat16 [16, 1024, 2048], P('dp', 'tensor'), may hold values from -3.59375 to 3.59375
- grad_output: bfloat16 [4096, 2048], P(('dp', 'tensor')), may hold values from -6 to 6
Outputs:
- out: bfloat16 [4096, 2048], P(('dp', 'tensor'))
- grad_tokens: bfloat16 [4096, 2048], P(('dp', 'tensor'))
- grad_w_query: float32 [2048, 2048], P(None, 'tensor')
- grad_w_key: float32 [2048, 2048], P(None, 'tensor')
- grad_w_value: float32 [2048, 2048], P(None, 'tensor')
- grad_w_output: float32 [2048, 2048], P('tensor')
- grad_query_gain: float32 [2048], P('tensor')
- grad_key_gain: float32 [2048], P('tensor')
- grad_attn_gain: float32 [2048], replicated
- grad_ffn_gain: float32 [2048], replicated
- grad_w_router: float32 [2048, 16], replicated
- grad_w_gate: float32 [16, 2048, 1024], P('dp', None, 'tensor')
- grad_w_up: float32 [16, 2048, 1024], P('dp', None, 'tensor')
- grad_w_down: float32 [16, 1024, 2048], P('dp', 'tensor')
Inputs may be any that keep to these rules, and one draw needn't show every extreme that they name: `expert_ids`: each row names 8 different experts; the 128 rows of one device (aligned blocks) name no expert more than 72 times, a bound that some block reaches. `file_ids`: along each row the ids never fall; equal ids mark one file; no file is longer than 256 tokens. `w_query`: drawn independently, columns of unequal scale. `w_key`: drawn independently, columns of unequal scale.
All inputs are finite; a program needn't handle non-finite values.
Results may differ from a plain program's by a relative error of at most 0.022.
Values may be sent and summed in bfloat16 or wider, within the bound.
A program may use at most 320 MiB of HBM per device.

v0:
```python
import math

import jax
import jax.numpy as jnp
from jax import lax
from jax.sharding import PartitionSpec as P

HEAD_DIM = 128


EPSILON = 1e-05
THETA = 10000.0
NEG_LARGE = -1e30


def root_mean_square_scale(values):
    return lax.rsqrt(jnp.mean(values * values, axis=-1, keepdims=True) + EPSILON)


def rope_tables(length, head_dim):
    half_dim = head_dim // 2
    freq_index = jnp.arange(half_dim, dtype=jnp.float32)
    frequency = THETA ** (-(2.0 * freq_index) / head_dim)
    angles = jnp.arange(length, dtype=jnp.float32)[:, None] * frequency[None, :]
    cosine = jnp.concatenate([jnp.cos(angles), jnp.cos(angles)], axis=1)
    sine_table = jnp.concatenate([jnp.sin(angles), jnp.sin(angles)], axis=1)
    return (cosine[:, None, :], sine_table[:, None, :])


def rotate(values, cosine, sine_table):
    half_dim = values.shape[-1] // 2
    turned = jnp.concatenate([-values[..., half_dim:], values[..., :half_dim]], axis=-1)
    return values * cosine + turned * sine_table


def unrotate(grad_rows, cosine, sine_table):
    half_dim = grad_rows.shape[-1] // 2
    scaled = grad_rows * sine_table
    turned = jnp.concatenate([scaled[..., half_dim:], -scaled[..., :half_dim]], axis=-1)
    return grad_rows * cosine + turned


def slot_positions(ids, experts):
    flat_ids = ids.reshape(-1)
    onehot = (flat_ids[:, None] == jnp.arange(experts, dtype=jnp.int32)[None, :]).astype(jnp.int32)
    running = jnp.cumsum(onehot, axis=0)
    return (flat_ids, jnp.sum(running * onehot, axis=1) - 1)


def block_scores(query_block, key_rows, file_row, block_start, score_scale):
    block_rows = query_block.shape[0]
    raw_scores = (
        jnp.einsum("qhd,khd->hqk", query_block, key_rows, preferred_element_type=jnp.float32)
        * score_scale
    )
    rows_at = block_start + jnp.arange(block_rows, dtype=jnp.int32)
    cols_at = jnp.arange(key_rows.shape[0], dtype=jnp.int32)
    allowed = (cols_at[None, :] <= rows_at[:, None]) & (file_row[None, :] == file_row[:, None])
    return jnp.where(allowed[None], raw_scores, NEG_LARGE)


def local(
    tokens,
    file_ids,
    expert_ids,
    attention_norm_gain,
    w_query,
    w_key,
    w_value,
    query_gain,
    key_gain,
    w_output,
    expert_norm_gain,
    w_router,
    w_gate,
    w_up,
    w_down,
    grad_output,
):
    tok_count, d_model = tokens.shape
    n_tensor = lax.axis_size("tensor")
    n_dp = lax.axis_size("dp")
    devices = n_dp * n_tensor
    local_dim = w_query.shape[1]
    head_dim = HEAD_DIM
    local_heads = local_dim // head_dim
    seq_len = tok_count * n_tensor
    block_rows = min(512, seq_len)
    score_scale = 1.0 / math.sqrt(head_dim)
    file_row = file_ids[0]
    cosine, sine_table = rope_tables(seq_len, head_dim)
    input_tensors = tokens.astype(jnp.float32)
    first_norm_scale = root_mean_square_scale(input_tensors)
    first_unit_rows = input_tensors * first_norm_scale
    first_normalized = (first_unit_rows * attention_norm_gain).astype(jnp.bfloat16)
    normed_all = lax.all_gather(first_normalized, "tensor", axis=0, tiled=True)
    query_raw = jnp.dot(normed_all, w_query, preferred_element_type=jnp.float32)
    key_raw = jnp.dot(normed_all, w_key, preferred_element_type=jnp.float32)
    value_rows = (
        jnp.dot(normed_all, w_value, preferred_element_type=jnp.float32)
        .astype(jnp.bfloat16)
        .reshape(seq_len, local_heads, head_dim)
    )
    query_total, key_total = lax.psum(
        (jnp.sum(query_raw * query_raw, axis=1), jnp.sum(key_raw * key_raw, axis=1)), "tensor"
    )
    query_scale = lax.rsqrt(query_total / d_model + EPSILON)[:, None]
    key_scale = lax.rsqrt(key_total / d_model + EPSILON)[:, None]
    query_hat = query_raw * query_scale
    key_hat = key_raw * key_scale
    queries = rotate(
        (query_hat * query_gain).reshape(seq_len, local_heads, head_dim), cosine, sine_table
    ).astype(jnp.bfloat16)
    key_rows = rotate(
        (key_hat * key_gain).reshape(seq_len, local_heads, head_dim), cosine, sine_table
    ).astype(jnp.bfloat16)
    block_start = 0
    scores = block_scores(queries, key_rows, file_row, block_start, score_scale)
    row_peak = jnp.max(scores, axis=-1, keepdims=True)
    log_total = row_peak + jnp.log(jnp.sum(jnp.exp(scores - row_peak), axis=-1, keepdims=True))
    attn_probs = jnp.exp(scores - log_total).astype(jnp.bfloat16)
    context_blocks = jnp.einsum(
        "hqk,khd->qhd", attn_probs, value_rows, preferred_element_type=jnp.float32
    )
    log_totals = [log_total]
    context = context_blocks.reshape(seq_len, local_dim).astype(jnp.bfloat16)
    attn_out = lax.psum_scatter(
        jnp.dot(context, w_output, preferred_element_type=jnp.float32),
        "tensor",
        scatter_dimension=0,
        tiled=True,
    )
    hidden_after_attention = input_tensors + attn_out
    second_norm_scale = root_mean_square_scale(hidden_after_attention)
    second_unit_rows = hidden_after_attention * second_norm_scale
    second_normalized = (second_unit_rows * expert_norm_gain).astype(jnp.bfloat16)
    experts = w_router.shape[1]
    topk = expert_ids.shape[1]
    exp_dev = w_gate.shape[0]
    most = 2 * ((tok_count * topk * 9 + experts * 16 - 1) // (experts * 16))
    route_probs = jax.nn.softmax(
        jnp.dot(second_normalized, w_router, preferred_element_type=jnp.float32), axis=-1
    )
    chosen = expert_ids[:, :, None] == jnp.arange(experts, dtype=jnp.int32)[None, None, :]
    gate_values = jnp.sum(jnp.where(chosen, route_probs[:, None, :], 0.0), axis=-1)
    flat_ids, pair_rank = slot_positions(expert_ids, experts)
    pair_slot = (flat_ids % exp_dev * n_dp + flat_ids // exp_dev) * most + pair_rank
    pair_count = tok_count * topk
    slot_count = exp_dev * n_dp * most
    slot_owner = (
        jnp.full((slot_count,), pair_count, jnp.int32)
        .at[pair_slot]
        .set(jnp.arange(pair_count, dtype=jnp.int32))
    )
    padded = jnp.concatenate([second_normalized, jnp.zeros((1, d_model), jnp.bfloat16)], axis=0)
    outgoing = padded[slot_owner // topk].reshape(exp_dev, n_dp, most, d_model)
    copies = jnp.broadcast_to(
        outgoing[:, :, None], (exp_dev, n_dp, n_tensor, most, d_model)
    ).reshape(exp_dev, devices, most, d_model)
    arrived = lax.all_to_all(copies, ("dp", "tensor"), split_axis=1, concat_axis=1, tiled=True)
    expert_rows = arrived.reshape(exp_dev, devices * most, d_model)
    gate_pre = jnp.einsum("erd,edf->erf", expert_rows, w_gate, preferred_element_type=jnp.float32)
    up_pre = jnp.einsum("erd,edf->erf", expert_rows, w_up, preferred_element_type=jnp.float32)
    gate_sigmoid = jax.nn.sigmoid(gate_pre)
    silu_gate = gate_pre * gate_sigmoid
    hidden = (silu_gate * up_pre).astype(jnp.bfloat16)
    partial_value = (
        jnp.einsum("erf,efd->erd", hidden, w_down, preferred_element_type=jnp.float32)
        .astype(jnp.bfloat16)
        .reshape(exp_dev, devices, most, d_model)
    )
    returned = lax.all_to_all(
        partial_value, ("dp", "tensor"), split_axis=1, concat_axis=1, tiled=True
    )
    expert_out = jnp.sum(
        returned.reshape(exp_dev, n_dp, n_tensor, most, d_model).astype(jnp.float32), axis=2
    ).reshape(slot_count, d_model)
    pair_out = expert_out[pair_slot].reshape(tok_count, topk, d_model)
    result = (hidden_after_attention + jnp.sum(gate_values[:, :, None] * pair_out, axis=1)).astype(
        jnp.bfloat16
    )
    cotangent = grad_output.astype(jnp.float32)
    grad_gates = jnp.sum(pair_out * cotangent[:, None, :], axis=-1)
    grad_pairs = (
        (gate_values[:, :, None] * cotangent[:, None, :])
        .astype(jnp.bfloat16)
        .reshape(pair_count, d_model)
    )
    grad_slots = jnp.concatenate([grad_pairs, jnp.zeros((1, d_model), jnp.bfloat16)], axis=0)[
        slot_owner
    ].reshape(exp_dev, n_dp, most, d_model)
    grad_copies = jnp.broadcast_to(
        grad_slots[:, :, None], (exp_dev, n_dp, n_tensor, most, d_model)
    ).reshape(exp_dev, devices, most, d_model)
    grad_arrived = lax.all_to_all(
        grad_copies, ("dp", "tensor"), split_axis=1, concat_axis=1, tiled=True
    )
    grad_rows = grad_arrived.reshape(exp_dev, devices * most, d_model)
    grad_hidden = jnp.einsum("erd,efd->erf", grad_rows, w_down, preferred_element_type=jnp.float32)
    grad_down = jnp.einsum("erf,erd->efd", hidden, grad_rows, preferred_element_type=jnp.float32)
    grad_gate_pre = (
        grad_hidden * up_pre * gate_sigmoid * (1.0 + gate_pre * (1.0 - gate_sigmoid))
    ).astype(jnp.bfloat16)
    grad_up_pre = (grad_hidden * silu_gate).astype(jnp.bfloat16)
    grad_gate = jnp.einsum(
        "erd,erf->edf", expert_rows, grad_gate_pre, preferred_element_type=jnp.float32
    )
    grad_up = jnp.einsum(
        "erd,erf->edf", expert_rows, grad_up_pre, preferred_element_type=jnp.float32
    )
    grad_expert_in = jnp.einsum(
        "erf,edf->erd", grad_gate_pre, w_gate, preferred_element_type=jnp.float32
    )
    grad_expert_in = grad_expert_in + jnp.einsum(
        "erf,edf->erd", grad_up_pre, w_up, preferred_element_type=jnp.float32
    )
    grad_expert_in = grad_expert_in.astype(jnp.bfloat16).reshape(exp_dev, devices, most, d_model)
    grad_back = lax.all_to_all(
        grad_expert_in, ("dp", "tensor"), split_axis=1, concat_axis=1, tiled=True
    )
    grad_slot_in = jnp.sum(
        grad_back.reshape(exp_dev, n_dp, n_tensor, most, d_model).astype(jnp.float32), axis=2
    ).reshape(slot_count, d_model)
    grad_second_normalized = jnp.sum(
        grad_slot_in[pair_slot].reshape(tok_count, topk, d_model), axis=1
    )
    grad_route = jnp.sum(jnp.where(chosen, grad_gates[:, :, None], 0.0), axis=1)
    grad_logits = (
        route_probs * (grad_route - jnp.sum(route_probs * grad_route, axis=-1, keepdims=True))
    ).astype(jnp.bfloat16)
    grad_router_part = jnp.einsum(
        "td,te->de", second_normalized, grad_logits, preferred_element_type=jnp.float32
    )
    grad_second_normalized = grad_second_normalized + jnp.einsum(
        "te,de->td", grad_logits, w_router, preferred_element_type=jnp.float32
    )
    grad_expert_share = jnp.sum(grad_second_normalized * second_unit_rows, axis=0)
    grad_second_unit_rows = grad_second_normalized * expert_norm_gain
    grad_hidden_one = (
        second_norm_scale
        * (
            grad_second_unit_rows
            - second_unit_rows
            * jnp.mean(grad_second_unit_rows * second_unit_rows, axis=-1, keepdims=True)
        )
        + cotangent
    )
    grad_attn = grad_hidden_one.astype(jnp.bfloat16)
    grad_attn_all = lax.all_gather(grad_attn, "tensor", axis=0, tiled=True)
    grad_output_part = jnp.einsum(
        "sd,se->de", context, grad_attn_all, preferred_element_type=jnp.float32
    )
    grad_context = (
        jnp.einsum("se,de->sd", grad_attn_all, w_output, preferred_element_type=jnp.float32)
        .astype(jnp.bfloat16)
        .reshape(seq_len, local_heads, head_dim)
    )
    grad_query_blocks = []
    grad_key_total = jnp.zeros((seq_len, local_heads, head_dim), jnp.float32)
    grad_value_total = jnp.zeros((seq_len, local_heads, head_dim), jnp.float32)
    for block_index, block_start in enumerate(range(0, seq_len, block_rows)):
        scores = block_scores(queries, key_rows, file_row, block_start, score_scale)
        probs_full = jnp.exp(scores - log_totals[block_index])
        probs_low = probs_full.astype(jnp.bfloat16)
        grad_value_total = jnp.einsum(
            "hqk,qhd->khd", probs_low, grad_context, preferred_element_type=jnp.float32
        )
        grad_probs = jnp.einsum(
            "qhd,khd->hqk", grad_context, value_rows, preferred_element_type=jnp.float32
        )
        row_shift = jnp.sum(probs_full * grad_probs, axis=-1, keepdims=True)
        grad_scores = (probs_full * (grad_probs - row_shift)).astype(jnp.bfloat16)
        grad_query_blocks.append(
            jnp.einsum("hqk,khd->qhd", grad_scores, key_rows, preferred_element_type=jnp.float32)
            * score_scale
        )
        grad_key_total = (
            jnp.einsum("hqk,qhd->khd", grad_scores, queries, preferred_element_type=jnp.float32)
            * score_scale
        )
    grad_query_normed = unrotate(grad_query_blocks[0], cosine, sine_table).reshape(
        seq_len, local_dim
    )
    grad_key_normed = unrotate(grad_key_total, cosine, sine_table).reshape(seq_len, local_dim)
    grad_qgain_part = jnp.sum(grad_query_normed * query_hat, axis=0)
    grad_kgain_part = jnp.sum(grad_key_normed * key_hat, axis=0)
    grad_query_hat = grad_query_normed * query_gain
    grad_key_hat = grad_key_normed * key_gain
    query_inner, key_inner = lax.psum(
        (jnp.sum(grad_query_hat * query_hat, axis=1), jnp.sum(grad_key_hat * key_hat, axis=1)),
        "tensor",
    )
    grad_query_raw = (
        query_scale * (grad_query_hat - query_hat * (query_inner / d_model)[:, None])
    ).astype(jnp.bfloat16)
    grad_key_raw = (key_scale * (grad_key_hat - key_hat * (key_inner / d_model)[:, None])).astype(
        jnp.bfloat16
    )
    grad_value_raw = grad_value_total.reshape(seq_len, local_dim).astype(jnp.bfloat16)
    grad_query_part = jnp.einsum(
        "sd,sf->df", normed_all, grad_query_raw, preferred_element_type=jnp.float32
    )
    grad_key_part = jnp.einsum(
        "sd,sf->df", normed_all, grad_key_raw, preferred_element_type=jnp.float32
    )
    grad_value_part = jnp.einsum(
        "sd,sf->df", normed_all, grad_value_raw, preferred_element_type=jnp.float32
    )
    summed = jnp.einsum("sf,df->sd", grad_query_raw, w_query, preferred_element_type=jnp.float32)
    summed = summed + jnp.einsum(
        "sf,df->sd", grad_key_raw, w_key, preferred_element_type=jnp.float32
    )
    grad_first_normalized = lax.psum_scatter(
        (
            summed
            + jnp.einsum("sf,df->sd", grad_value_raw, w_value, preferred_element_type=jnp.float32)
        ).astype(jnp.bfloat16),
        "tensor",
        scatter_dimension=0,
        tiled=True,
    ).astype(jnp.float32)
    grad_attention_share = jnp.sum(grad_first_normalized * first_unit_rows, axis=0)
    grad_first_unit_rows = grad_first_normalized * attention_norm_gain
    grad_tokens = (
        first_norm_scale
        * (
            grad_first_unit_rows
            - first_unit_rows
            * jnp.mean(grad_first_unit_rows * first_unit_rows, axis=-1, keepdims=True)
        )
        + grad_hidden_one
    ).astype(jnp.bfloat16)
    total_query, total_key, total_value, total_output, total_qgain, total_kgain = (
        lax.psum(grad_query_part.astype(jnp.bfloat16), "dp").astype(jnp.float32),
        lax.psum(grad_key_part.astype(jnp.bfloat16), "dp").astype(jnp.float32),
        lax.psum(grad_value_part.astype(jnp.bfloat16), "dp").astype(jnp.float32),
        lax.psum(grad_output_part.astype(jnp.bfloat16), "dp").astype(jnp.float32),
        lax.psum(grad_qgain_part.astype(jnp.bfloat16), "dp").astype(jnp.float32),
        lax.psum(grad_kgain_part.astype(jnp.bfloat16), "dp").astype(jnp.float32),
    )
    total_attn_gain, total_ffn_gain, total_router = lax.psum(
        (grad_attention_share, grad_expert_share, grad_router_part), ("dp", "tensor")
    )
    return (
        result,
        grad_tokens,
        total_query,
        total_key,
        total_value,
        total_output,
        total_qgain,
        total_kgain,
        total_attn_gain,
        total_ffn_gain,
        total_router,
        grad_gate,
        grad_up,
        grad_down,
    )


def solution(mesh):
    return jax.shard_map(
        local,
        mesh=mesh,
        in_specs=(
            P(("dp", "tensor"), None),
            P("dp", None),
            P(("dp", "tensor"), None),
            P(),
            P(None, "tensor"),
            P(None, "tensor"),
            P(None, "tensor"),
            P("tensor"),
            P("tensor"),
            P("tensor", None),
            P(),
            P(),
            P("dp", None, "tensor"),
            P("dp", None, "tensor"),
            P("dp", "tensor", None),
            P(("dp", "tensor"), None),
        ),
        out_specs=(
            P(("dp", "tensor"), None),
            P(("dp", "tensor"), None),
            P(None, "tensor"),
            P(None, "tensor"),
            P(None, "tensor"),
            P("tensor", None),
            P("tensor"),
            P("tensor"),
            P(),
            P(),
            P(),
            P("dp", None, "tensor"),
            P("dp", None, "tensor"),
            P("dp", "tensor", None),
        ),
        check_vma=False,
    )
```

profile of v0, /device:TPU:0, one launch (start us, length us, event | category | flops | bytes accessed | tf_op | source)
XLA Modules:
  0.0 2369.3 jit_solution(17083296328021372407)
XLA Ops:
  13.8 45.9 %all-gather.3.cloned.1.call-done = bf16[512,2048]{1,0:T(8,128)(2,1)} async-done(((bf16[128,2048]{1,0:T(8,128)(2,1)}), bf16[512,2048]{1,0:T(8,128)(2,1)}) %all-gather.3.cloned.1.call-update) | async-done | bytes 2097168 | tf_op jit(solution)/shard_map/all_gather | solution.py:96
  59.7 3.7 multiply_reduce_fusion.6
  65.7 10.0 all-reduce.4
  89.7 4.5 reduce-window.6
  95.3 4.3 scatter_custom_fusion
  99.7 64.8 %reduce-scatter.3.cloned.1.call-done = f32[128,2048]{1,0:T(8,128)} async-done(((f32[512,2048]{1,0:T(8,128)}), f32[128,2048]{1,0:T(8,128)}) %reduce-scatter.3.cloned.1.call-update) | async-done | bytes 1048592 | tf_op jit(solution)/shard_map/reduce_scatter | solution.py:127
  167.9 5.9 gather_fusion
  176.6 6.8 broadcast_in_dim.55
  183.3 5.7 all-to-all-start
  195.9 13.4 gather_fusion.2
  209.4 5.2 copy.153
  214.5 379.1 %all-to-all-done = bf16[2,32,72,2048]{3,2,0,1:T(8,128)(2,1)} async-done(((bf16[2,32,72,2048]{3,2,0,1:T(8,128)(2,1)}), bf16[2,32,72,2048]{3,2,0,1:T(8,128)(2,1)}, u32[]{:S(2)}, u32[]{:S(2)}) %all-to-all-start) | async-done | bytes 18874400 | tf_op jit(solution)/shard_map/all_to_all | solution.py:160
  593.7 8.3 broadcast_in_dim.58
  601.9 17.5 all-to-all-start.2
  619.5 9.8 copy.149
  629.4 7.6 fusion.46
  637.8 6.7 fusion.45
  644.4 379.7 %all-to-all-done.2 = bf16[2,32,72,2048]{3,2,0,1:T(8,128)(2,1)} async-done(((bf16[2,32,72,2048]{3,2,0,1:T(8,128)(2,1)}), bf16[2,32,72,2048]{3,2,0,1:T(8,128)(2,1)}, u32[]{:S(2)}, u32[]{:S(2)}) %all-to-all-start.2) | async-done | bytes 18874400 | tf_op jit(solution)/shard_map/all_to_all | solution.py:195
  1024.2 17.2 copy.154
  1041.4 13.2 multiply_convert_fusion
  1054.6 9.1 convolution_convert_fusion
  1063.7 16.9 copy.150
  1080.6 17.6 all-to-all-start.1
  1098.2 16.3 fusion.47
  1114.6 22.1 add_convert_fusion
  1136.7 16.9 copy.155
  1153.6 350.2 %all-to-all-done.1 = bf16[2,32,72,2048]{3,2,0,1:T(8,128)(2,1)} async-done(((bf16[2,32,72,2048]{3,2,0,1:T(8,128)(2,1)}), bf16[2,32,72,2048]{3,2,0,1:T(8,128)(2,1)}, u32[]{:S(2)}, u32[]{:S(2)}) %all-to-all-start.1) | async-done | bytes 18874400 | tf_op jit(solution)/shard_map/all_to_all | solution.py:172
  1503.8 16.7 all-to-all-start.3
  1520.6 14.6 convert_reduce_fusion.1
  1535.2 8.7 copy.151
  1544.0 12.7 gather_fusion.1
  1556.7 6.2 fusion.2
  1563.1 362.1 %all-to-all-done.3 = bf16[2,32,72,2048]{3,2,0,1:T(8,128)(2,1)} async-done(((bf16[2,32,72,2048]{3,2,0,1:T(8,128)(2,1)}), bf16[2,32,72,2048]{3,2,0,1:T(8,128)(2,1)}, u32[]{:S(2)}, u32[]{:S(2)}) %all-to-all-start.3) | async-done | bytes 18874400 | tf_op jit(solution)/shard_map/all_to_all | solution.py:218
  1925.2 14.7 convert_reduce_fusion
  1939.9 8.7 copy.156
  1948.6 12.7 gather_fusion.3
  1961.3 5.7 bitcast_reduce_fusion
  1969.1 58.4 %all-gather.5.cloned.1.call-done = bf16[512,2048]{1,0:T(8,128)(2,1)} async-done(((bf16[128,2048]{1,0:T(8,128)(2,1)}), bf16[512,2048]{1,0:T(8,128)(2,1)}) %all-gather.5.cloned.1.call-update) | async-done | bytes 2097168 | tf_op jit(solution)/shard_map/all_gather | solution.py:249
  2027.5 3.7 convolution_convert_fusion.5
  2039.8 9.8 all-reduce.3
  2058.5 13.7 fusion.51
  2083.1 13.4 fusion.50
  2096.6 11.8 fusion.52
  2109.3 12.6 all-reduce.5
  2127.8 102.3 %all-reduce.12.cloned.1.call-done = (bf16[2048,512]{1,0:T(8,128)(2,1)}, bf16[2048,512]{1,0:T(8,128)(2,1)}, bf16[2048,512]{1,0:T(8,128)(2,1)}, bf16[512,2048]{1,0:T(8,128)(2,1)}) async-done(((bf16[2048,512]{1,0:T(8,128)(2,1)}, bf16[2048,512]{1,0:T(8,128)(2,1)}, bf16[2048,512]{1,0:T(8,128)(2,1)}, bf16[512,2048]{1,0:T(8,128)(2,1)}), (bf16[2048,512]{1,0:T(8,128)(2,1)}, bf16[2048,512]{1,0:T(8,128)(2,1)}, ...) | async-done | bytes 8388624 | tf_op jit(solution)/shard_map/psum | solution.py:334
  2230.1 4.3 convert_element_type.181
  2242.3 39.5 %all-reduce.2 = (f32[2048]{0:T(1024)}, f32[2048]{0:T(1024)}) all-reduce(f32[2048]{0:T(1024)S(1)} %get-tuple-element.22, f32[2048]{0:T(1024)S(1)} %get-tuple-element.20), channel_id=1, replica_groups=mesh['dp'=8,'tensor'=4] {'dp','tensor'}, use_global_device_ids=true, to_apply=%region_40.41 | all-reduce | flops 4096 | bytes 32768 | tf_op jit(solution)/shard_map/psum | solution.py:341
  2281.8 78.8 %all-reduce.10.cloned.1.call-done = f32[2048,16]{0,1:T(8,128)} async-done(((f32[2048,16]{0,1:T(8,128)}), f32[2048,16]{0,1:T(8,128)}) %all-reduce.10.cloned.1.call-update) | async-done | bytes 131088 | tf_op jit(solution)/shard_map/psum | solution.py:341
  (283 shorter events, 83.9 us)
Async XLA Ops:
  7.2 1034.2 %copy-start = (bf16[2,256,2048]{2,1,0:T(8,128)(2,1)S(1)}, bf16[2,256,2048]{2,1,0:T(8,128)(2,1)}, u32[]{:S(2)}) copy-start(bf16[2,256,2048]{2,1,0:T(8,128)(2,1)} %param.30) | copy-start | bytes 6291460
  7.2 52.5 %all-gather.3.cloned.1.call-start = ((), (), s32[]{:S(2)}) async-start(), calls=%async_computation.6 | async-start | bytes 2621440 | tf_op jit(solution)/shard_map/all_gather | solution.py:96
  11.2 153.3 %reduce-scatter.3.cloned.1.call-start = ((), (), s32[]{:S(2)}) async-start(), calls=%async_computation.7 | async-start | bytes 5242880 | tf_op jit(solution)/shard_map/reduce_scatter | solution.py:127
  13.8 70.0 %copy-start.22 = (pred[512,512]{0,1:T(8,128)(4,1)}, pred[512,512]{0,1:T(8,128)(4,1)S(1)}, u32[]{:S(2)}) copy-start(pred[512,512]{0,1:T(8,128)(4,1)S(1)} %fusion.24) | copy-start | bytes 786436
  63.5 13.9 copy-start.12
  63.5 12.3 copy-start.71
  65.7 11.7 copy-start.73
  89.3 75.2 %copy-start.9 = (bf16[128,2048]{1,0:T(8,128)(2,1)S(1)}, bf16[128,2048]{1,0:T(8,128)(2,1)}, u32[]{:S(2)}) copy-start(bf16[128,2048]{1,0:T(8,128)(2,1)} %param.16) | copy-start | bytes 1572868
  89.3 77.6 %copy-start.60 = (f32[2048]{0:T(1024)S(1)}, f32[2048]{0:T(1024)}, u32[]{:S(2)}) copy-start(f32[2048]{0:T(1024)} %param.26) | copy-start | bytes 24580
  165.9 7.9 copy-start.81
  183.3 6.8 copy-start.56
  183.3 410.3 %all-to-all-start = ((bf16[2,32,72,2048]{3,2,0,1:T(8,128)(2,1)}), bf16[2,32,72,2048]{3,2,0,1:T(8,128)(2,1)}, u32[]{:S(2)}, u32[]{:S(2)}) async-start(bf16[2,32,72,2048]{3,2,0,1:T(8,128)(2,1)} %bitcast.142), calls=%async_computation.1 | async-start | bytes 37748736 | tf_op jit(solution)/shard_map/all_to_all | solution.py:160
  190.1 5.8 copy-start.18
  601.9 422.2 %all-to-all-start.2 = ((bf16[2,32,72,2048]{3,2,0,1:T(8,128)(2,1)}), bf16[2,32,72,2048]{3,2,0,1:T(8,128)(2,1)}, u32[]{:S(2)}, u32[]{:S(2)}) async-start(bf16[2,32,72,2048]{3,2,0,1:T(8,128)(2,1)} %bitcast.143), calls=%async_computation.3 | async-start | bytes 37748736 | tf_op jit(solution)/shard_map/all_to_all | solution.py:195
  619.5 9.9 copy-start.44
  629.3 8.4 copy-start.8
  629.3 8.4 copy-start.33
  1024.2 17.2 copy-start.89
  1054.6 9.1 copy-start.4
  1080.6 17.6 copy-start.34
  1080.6 423.2 %all-to-all-start.1 = ((bf16[2,32,72,2048]{3,2,0,1:T(8,128)(2,1)}), bf16[2,32,72,2048]{3,2,0,1:T(8,128)(2,1)}, u32[]{:S(2)}, u32[]{:S(2)}) async-start(bf16[2,32,72,2048]{3,2,0,1:T(8,128)(2,1)} %copy.150), calls=%async_computation.2 | async-start | bytes 37748736 | tf_op jit(solution)/shard_map/all_to_all | solution.py:172
  1153.6 367.0 %copy-start.76 = (s32[1024,1]{0,1:T(1,128)S(1)}, s32[1024,1]{0,1:T(1,128)}, u32[]{:S(2)}) copy-start(s32[1024,1]{0,1:T(1,128)} %copy-done.75) | copy-start | bytes 12292
  1503.8 421.4 %all-to-all-start.3 = ((bf16[2,32,72,2048]{3,2,0,1:T(8,128)(2,1)}), bf16[2,32,72,2048]{3,2,0,1:T(8,128)(2,1)}, u32[]{:S(2)}, u32[]{:S(2)}) async-start(bf16[2,32,72,2048]{3,2,0,1:T(8,128)(2,1)} %copy.155), calls=%async_computation.4 | async-start | bytes 37748736 | tf_op jit(solution)/shard_map/all_to_all | solution.py:218
  1520.5 507.0 %all-gather.5.cloned.1.call-start = ((), (), s32[]{:S(2)}) async-start(), calls=%async_computation.8 | async-start | bytes 2621440 | tf_op jit(solution)/shard_map/all_gather | solution.py:249
  1544.0 12.7 copy-start.19
  1544.0 12.7 copy-start.50
  1556.7 6.3 copy-start.66
  1556.7 6.3 copy-start.59
  1556.7 6.3 copy-start.78
  1556.7 6.3 copy-start.80
  1961.3 5.8 copy-start.82
  1961.3 6.3 copy-start.24
  1967.6 63.5 %copy-start.16 = (f32[128,2048]{1,0:T(8,128)}, f32[128,2048]{1,0:T(8,128)S(1)}, u32[]{:S(2)}) copy-start(f32[128,2048]{1,0:T(8,128)S(1)} %get-tuple-element.73) | copy-start | bytes 3145732
  1968.8 62.4 %copy-start.23 = (pred[512,512]{0,1:T(8,128)(4,1)S(1)}, pred[512,512]{0,1:T(8,128)(4,1)}, u32[]{:S(2)}) copy-start(pred[512,512]{0,1:T(8,128)(4,1)} %copy-done.22) | copy-start | bytes 786436
  1968.8 62.4 %copy-start.64 = (f32[4,512]{1,0:T(4,128)S(1)}, f32[4,512]{1,0:T(4,128)}, u32[]{:S(2)}) copy-start(f32[4,512]{1,0:T(4,128)} %copy-done.63) | copy-start | bytes 24580
  1968.8 154.2 %reduce-scatter.5.cloned.1.call-start = ((), (), s32[]{:S(2)}) async-start(), calls=%async_computation.9 | async-start | bytes 2621440 | tf_op jit(solution)/shard_map/reduce_scatter | solution.py:313
  2038.5 13.0 copy-start.14
  2058.0 14.2 copy-start.55
  2058.0 172.0 %all-reduce.12.cloned.1.call-start = ((), (), s32[]{:S(2)}) async-start(), calls=%async_computation.11 | async-start | bytes 16777216 | tf_op jit(solution)/shard_map/psum | solution.py:334
  2058.5 13.7 copy-start.88
  2082.9 277.8 %all-reduce.10.cloned.1.call-start = ((), (), s32[]{:S(2)}) async-start(), calls=%async_computation.10 | async-start | bytes 262144 | tf_op jit(solution)/shard_map/psum | solution.py:341
  2083.1 13.4 copy-start.5
  2096.5 11.9 copy-start.21
  2096.5 26.5 %copy-start.10 = (bf16[128,2048]{1,0:T(8,128)(2,1)S(1)}, bf16[128,2048]{1,0:T(8,128)(2,1)}, u32[]{:S(2)}) copy-start(bf16[128,2048]{1,0:T(8,128)(2,1)} %param.16) | copy-start | bytes 1572868
  2096.5 26.5 %copy-start.62 = (f32[2048]{0:T(1024)S(1)}, f32[2048]{0:T(1024)}, u32[]{:S(2)}) copy-start(f32[2048]{0:T(1024)} %param.19) | copy-start | bytes 24580
  2096.6 26.5 %copy-start.84 = (f32[128]{0:T(128)S(1)}, f32[128]{0:T(128)}, u32[]{:S(2)}) copy-start(f32[128]{0:T(128)} %copy-done.83) | copy-start | bytes 1540
  2096.6 28.0 %copy-start.17 = (f32[128,2048]{1,0:T(8,128)S(1)}, f32[128,2048]{1,0:T(8,128)}, u32[]{:S(2)}) copy-start(f32[128,2048]{1,0:T(8,128)} %copy-done.16) | copy-start | bytes 3145732
  2237.0 125.2 %copy-start.1 = (bf16[2,256,2048]{2,1,0:T(8,128)(2,1)S(1)}, bf16[2,256,2048]{2,1,0:T(8,128)(2,1)}, u32[]{:S(2)}) copy-start(bf16[2,256,2048]{2,1,0:T(8,128)(2,1)} %param.30) | copy-start | bytes 6291460
  (52 other events, 112.7 us)
Sparse Core Ops, SparseCore 0:
  11.3 48.3 all-gather.2
  89.4 74.9 reduce-scatter.2
  1968.9 58.4 all-gather.4
  2058.1 41.8 reduce-scatter.4
  2104.3 125.6 all-reduce.11
  2236.0 124.5 all-reduce.9
where the time goes:
time: 2380 us; the launch traced here: 2370 us
  waiting for transfers between devices  1820 us (76%)
  local copies, waits for them, and re-layouts  164 us (7%)
  matrix products  155 us (7%)
  other arithmetic  83.3 us (4%)
  blocking collectives  71.9 us (3%)
  starting transfers between devices  58.5 us (2%)
    all_to_all x1, waiting for transfers between devices, local(): lax.all_to_all(grad_copies, ('dp', 'tensor'), split_axis=1, concat_axis=1...  380 us
    all_to_all x1, waiting for transfers between devices, local(): lax.all_to_all(copies, ('dp', 'tensor'), split_axis=1, concat_axis=1, til...  379 us
    all_to_all x1, waiting for transfers between devices, local(): lax.all_to_all(grad_expert_in, ('dp', 'tensor'), split_axis=1, concat_axi...  362 us
    all_to_all x1, waiting for transfers between devices, local(): lax.all_to_all(partial_value, ('dp', 'tensor'), split_axis=1, concat_axis...  350 us
    psum x1, waiting for transfers between devices, local(): lax.psum(grad_query_part.astype(jnp.bfloat16), 'dp').astype(jnp.float32)  102 us
    psum x1, waiting for transfers between devices, local(): lax.psum((grad_attention_share, grad_expert_share, grad_router_part), ('d...  78.8 us
    reduce_scatter x1, waiting for transfers between devices, local(): lax.psum_scatter(jnp.dot(context, w_output, preferred_element_type=jnp.fl...  64.8 us
    all_gather x1, waiting for transfers between devices, local(): grad_attn_all = lax.all_gather(grad_attn, 'tensor', axis=0, tiled=True)  58.4 us
  transfers between devices with their start and end apart: 10, of which 9 were waited for; matrix products, arithmetic and copies ran while one was open for 10% of the time, Pallas kernels for 0%

commit v1 on v0

--- a/solution.py
+++ b/solution.py
@@ -1,8 +1,11 @@
+import functools
 import math
 
 import jax
 import jax.numpy as jnp
 from jax import lax
+from jax.experimental import pallas as pl
+from jax.experimental.pallas import tpu as pltpu
 from jax.sharding import PartitionSpec as P
 
 HEAD_DIM = 128
@@ -57,6 +60,613 @@
     cols_at = jnp.arange(key_rows.shape[0], dtype=jnp.int32)
     allowed = (cols_at[None, :] <= rows_at[:, None]) & (file_row[None, :] == file_row[:, None])
     return jnp.where(allowed[None], raw_scores, NEG_LARGE)
+
+
+MESH = pl.DeviceIdType.MESH
+VMEM_LIMIT = 60 * 2**20
+
+
+def greet(dp, z, nz):
+    barrier = pltpu.get_barrier_semaphore()
+    for flip in (1, 2, 4):
+        pl.semaphore_signal(barrier, 1, device_id=(dp ^ flip, z), device_id_type=MESH)
+
+    @pl.when(z > 0)
+    def _():
+        pl.semaphore_signal(barrier, 1, device_id=(dp, z - 1), device_id_type=MESH)
+
+    @pl.when(z < nz - 1)
+    def _():
+        pl.semaphore_signal(barrier, 1, device_id=(dp, z + 1), device_id_type=MESH)
+
+    ends = jnp.where(z > 0, 1, 0) + jnp.where(z < nz - 1, 1, 0)
+    pl.semaphore_wait(barrier, 3 + ends)
+
+
+def gather_kernel(nz, x_ref, out_ref, local_sem, sz, sx, sy, sda, sdb, sc, rz, rx, ry, rda, rdb, rc):
+    dp, z = lax.axis_index("dp"), lax.axis_index("tensor")
+    half = x_ref.shape[0] // 2
+    greet(dp, z, nz)
+
+    def at(flip, zz):
+        return out_ref.at[(dp ^ flip) * nz + zz]
+
+    def remote(src, dst, send, recv, device):
+        return pltpu.make_async_remote_copy(
+            src_ref=src, dst_ref=dst, send_sem=send, recv_sem=recv, device_id=device, device_id_type=MESH
+        )
+
+    def z_copy(zz, step, own):
+        src = x_ref if own else at(0, zz)
+        return remote(src, at(0, zz), sz.at[(step + 1) // 2, zz], rz.at[zz], (dp, z + step))
+
+    def x_copy(zz, own):
+        return remote(x_ref if own else at(0, zz), at(0, zz), sx.at[zz], rx.at[zz], (dp ^ 2, z))
+
+    def y_copy(zz, own):
+        return remote(x_ref if own else at(0, zz), at(0, zz), sy.at[zz], ry.at[zz], (dp ^ 4, z))
+
+    def a_copy(zz):
+        ref = at(4, zz).at[pl.ds(0, half)]
+        return remote(ref, ref, sda.at[zz], rda.at[zz], (dp ^ 2, z))
+
+    def b_copy(zz):
+        ref = at(2, zz).at[pl.ds(half, half)]
+        return remote(ref, ref, sdb.at[zz], rdb.at[zz], (dp ^ 4, z))
+
+    def c_copy(kind, zz, own=False):
+        if kind < 3:
+            dst = at((0, 2, 4)[kind], zz)
+        else:
+            dst = at(6, zz).at[pl.ds((kind - 3) * half, half)]
+        return remote(x_ref if own else dst, dst, sc.at[kind, zz], rc.at[kind, zz], (dp ^ 1, z))
+
+    def arrived(ref, sem):
+        remote(ref, ref, sem, sem, (dp ^ 1, z)).wait_recv()
+
+    def places(distance):
+        for sign in (0,) if distance == 0 else (-1, 1):
+            yield sign, z + sign * distance
+
+    def spread(distance):
+        for sign, zz in places(distance):
+            own = distance == 0
+
+            @pl.when((zz >= 0) & (zz < nz))
+            def _():
+                if not own:
+                    arrived(at(0, zz), rz.at[zz])
+                if sign <= 0:
+
+                    @pl.when(z < nz - 1)
+                    def _():
+                        z_copy(zz, 1, own).start()
+
+                if sign >= 0:
+
+                    @pl.when(z > 0)
+                    def _():
+                        z_copy(zz, -1, own).start()
+
+                x_copy(zz, own).start()
+                y_copy(zz, own).start()
+                c_copy(0, zz, own).start()
+
+    def relay(distance):
+        for _, zz in places(distance):
+
+            @pl.when((zz >= 0) & (zz < nz))
+            def _():
+                arrived(at(4, zz), ry.at[zz])
+                a_copy(zz).start()
+                c_copy(2, zz).start()
+                arrived(at(2, zz), rx.at[zz])
+                b_copy(zz).start()
+                c_copy(1, zz).start()
+
+    def corner(distance):
+        for _, zz in places(distance):
+
+            @pl.when((zz >= 0) & (zz < nz))
+            def _():
+                arrived(at(6, zz).at[pl.ds(0, half)], rda.at[zz])
+                c_copy(3, zz).start()
+                arrived(at(6, zz).at[pl.ds(half, half)], rdb.at[zz])
+                c_copy(4, zz).start()
+
+    keep = pltpu.make_async_copy(x_ref, at(0, z), local_sem)
+    keep.start()
+    for step in range(nz + 2):
+        if step < nz:
+            spread(step)
+        if 0 <= step - 1 < nz:
+            relay(step - 1)
+        if 0 <= step - 2 < nz:
+            corner(step - 2)
+    keep.wait()
+    for zz in range(nz):
+
+        @pl.when((zz <= z) & (z < nz - 1))
+        def _():
+            z_copy(zz, 1, False).wait_send()
+
+        @pl.when((zz >= z) & (z > 0))
+        def _():
+            z_copy(zz, -1, False).wait_send()
+
+        x_copy(zz, False).wait_send()
+        y_copy(zz, False).wait_send()
+        a_copy(zz).wait_send()
+        b_copy(zz).wait_send()
+        for kind in range(5):
+            c_copy(kind, zz).wait_send()
+        for kind, flip in ((0, 1), (1, 3), (2, 5)):
+            arrived(at(flip, zz), rc.at[kind, zz])
+        for kind in (3, 4):
+            arrived(at(7, zz).at[pl.ds((kind - 3) * half, half)], rc.at[kind, zz])
+
+
+def gather_all(x, nz, collective_id):
+    rows, width = x.shape
+    dma = pltpu.SemaphoreType.DMA
+    return pl.pallas_call(
+        functools.partial(gather_kernel, nz),
+        name="gather_all",
+        out_shape=jax.ShapeDtypeStruct((8 * nz, rows, width), x.dtype),
+        in_specs=[pl.BlockSpec(memory_space=pltpu.VMEM)],
+        out_specs=pl.BlockSpec(memory_space=pl.ANY),
+        scratch_shapes=[dma(())]
+        + [dma((2, nz)), dma((nz,)), dma((nz,)), dma((nz,)), dma((nz,)), dma((5, nz))]
+        + [dma((nz,)), dma((nz,)), dma((nz,)), dma((nz,)), dma((nz,)), dma((5, nz))],
+        compiler_params=pltpu.CompilerParams(
+            collective_id=collective_id, has_side_effects=True, vmem_limit_bytes=8 * 2**20
+        ),
+    )(x)
+
+
+def z_order(nz):
+    return [sorted(range(nz), key=lambda zz: (-abs(zz - z), zz if z >= nz // 2 else -zz)) for z in range(nz)]
+
+
+CHUNK = 16
+
+
+def scatter_kernel(nz, p_ref, out_ref, acc, rc, ra, rb, rx, ry, ru, rd, s_local, s_core, r_core, s_a, r_a, s_b, r_b, s_x, r_x, s_y, r_y, s_u, r_u, s_d, r_d):
+    dp, z = lax.axis_index("dp"), lax.axis_index("tensor")
+    rows = acc.shape[2]
+    half = rows // 2
+    order = z_order(nz)
+
+    def place(i):
+        zz = order[0][i]
+        for zv in range(1, nz):
+            zz = jnp.where(z == zv, order[zv][i], zz)
+        return zz
+
+    def remote(src, dst, send, recv, device):
+        return pltpu.make_async_remote_copy(
+            src_ref=src, dst_ref=dst, send_sem=send, recv_sem=recv, device_id=device, device_id_type=MESH
+        )
+
+    flips = (0, 2, 4, 6)
+
+    def load(kind, zz):
+        return pltpu.make_async_copy(
+            p_ref.at[(dp ^ flips[kind]) * nz + zz], acc.at[kind, zz], s_local.at[kind, zz]
+        )
+
+    def core_copy(kind, zz):
+        return remote(
+            p_ref.at[(dp ^ flips[kind] ^ 1) * nz + zz], rc.at[kind, zz], s_core.at[kind, zz], r_core.at[kind, zz], (dp ^ 1, z)
+        )
+
+    def a_copy(zz):
+        return remote(acc.at[3, zz, pl.ds(0, half)], ra.at[zz], s_a.at[zz], r_a.at[zz], (dp ^ 2, z))
+
+    def b_copy(zz):
+        return remote(acc.at[3, zz, pl.ds(half, half)], rb.at[zz], s_b.at[zz], r_b.at[zz], (dp ^ 4, z))
+
+    def x_copy(zz):
+        return remote(acc.at[1, zz], rx.at[zz], s_x.at[zz], r_x.at[zz], (dp ^ 2, z))
+
+    def y_copy(zz):
+        return remote(acc.at[2, zz], ry.at[zz], s_y.at[zz], r_y.at[zz], (dp ^ 4, z))
+
+    def up_copy(zz):
+        return remote(acc.at[0, zz], ru.at[zz], s_u.at[zz], r_u.at[zz], (dp, z + 1))
+
+    def down_copy(zz):
+        return remote(acc.at[0, zz], rd.at[zz], s_d.at[zz], r_d.at[zz], (dp, z - 1))
+
+    def add(dst, *others, start=0, count=rows):
+        def body(k, carry):
+            at = pl.ds(start + k * CHUNK, CHUNK)
+            total = dst[at, :].astype(jnp.float32)
+            for ref, base in others:
+                total = total + ref[pl.ds(base + k * CHUNK, CHUNK), :].astype(jnp.float32)
+            dst[at, :] = total.astype(dst.dtype)
+            return carry
+
+        lax.fori_loop(0, count // CHUNK, body, 0)
+
+    def wave(i):
+        zz = place(i)
+        for kind in (3, 1, 2, 0):
+            core_copy(kind, zz).start()
+            load(kind, zz).start()
+
+    def paired(kind, zz):
+        load(kind, zz).wait()
+        core_copy(kind, zz).wait_recv()
+
+    def stage_diagonal(i):
+        zz = place(i)
+        paired(3, zz)
+        add(acc.at[3, zz], (rc.at[3, zz], 0))
+        a_copy(zz).start()
+        b_copy(zz).start()
+
+    def stage_side(i):
+        zz = place(i)
+        paired(1, zz)
+        paired(2, zz)
+        a_copy(zz).wait_recv()
+        add(acc.at[2, zz], (rc.at[2, zz], 0), (ra.at[zz], 0), start=0, count=half)
+        add(acc.at[2, zz], (rc.at[2, zz], half), start=half, count=half)
+        y_copy(zz).start()
+        b_copy(zz).wait_recv()
+        add(acc.at[1, zz], (rc.at[1, zz], half), (rb.at[zz], 0), start=half, count=half)
+        add(acc.at[1, zz], (rc.at[1, zz], 0), start=0, count=half)
+        x_copy(zz).start()
+
+    def stage_column(i):
+        zz = place(i)
+        paired(0, zz)
+        x_copy(zz).wait_recv()
+        y_copy(zz).wait_recv()
+        add(acc.at[0, zz], (rc.at[0, zz], 0), (rx.at[zz], 0), (ry.at[zz], 0))
+
+        @pl.when((zz > z) & (z == 0))
+        def _():
+            up_copy(zz).start()
+
+        @pl.when((zz < z) & (z == nz - 1))
+        def _():
+            down_copy(zz).start()
+
+    def stage_line(i):
+        zz = place(i)
+
+        @pl.when((zz > z) & (z > 0))
+        def _():
+            up_copy(zz).wait_recv()
+            add(acc.at[0, zz], (ru.at[zz], 0))
+            up_copy(zz).start()
+
+        @pl.when((zz < z) & (z < nz - 1))
+        def _():
+            down_copy(zz).wait_recv()
+            add(acc.at[0, zz], (rd.at[zz], 0))
+            down_copy(zz).start()
+
+    greet(dp, z, nz)
+    wave(0)
+    for i in range(nz + 3):
+        if i + 1 < nz:
+            wave(i + 1)
+        if i < nz:
+            stage_diagonal(i)
+        if 0 <= i - 1 < nz:
+            stage_side(i - 1)
+        if 0 <= i - 2 < nz:
+            stage_column(i - 2)
+        if 0 <= i - 3 < nz:
+            stage_line(i - 3)
+
+    @pl.when(z > 0)
+    def _():
+        up_copy(z).wait_recv()
+
+    @pl.when(z < nz - 1)
+    def _():
+        down_copy(z).wait_recv()
+
+    def finish(k, carry):
+        at = pl.ds(k * CHUNK, CHUNK)
+        total = acc[0, z, at, :].astype(jnp.float32)
+        zero = jnp.zeros_like(total)
+        total = total + jnp.where(z > 0, ru[z, at, :].astype(jnp.float32), zero)
+        total = total + jnp.where(z < nz - 1, rd[z, at, :].astype(jnp.float32), zero)
+        out_ref[at, :] = total
+        return carry
+
+    lax.fori_loop(0, rows // CHUNK, finish, 0)
+    for zz in range(nz):
+        for kind in range(4):
+            core_copy(kind, zz).wait_send()
+        a_copy(zz).wait_send()
+        b_copy(zz).wait_send()
+        x_copy(zz).wait_send()
+        y_copy(zz).wait_send()
+
+        @pl.when(zz > z)
+        def _():
+            up_copy(zz).wait_send()
+
+        @pl.when(zz < z)
+        def _():
+            down_copy(zz).wait_send()
+
+
+def scatter_all(p, nz, collective_id):
+    _, rows, width = p.shape
+    dma, vmem = pltpu.SemaphoreType.DMA, functools.partial(pltpu.VMEM, dtype=p.dtype)
+    half = rows // 2
+    return pl.pallas_call(
+        functools.partial(scatter_kernel, nz),
+        name="scatter_all",
+        out_shape=jax.ShapeDtypeStruct((rows, width), jnp.float32),
+        in_specs=[pl.BlockSpec(memory_space=pl.ANY)],
+        out_specs=pl.BlockSpec(memory_space=pltpu.VMEM),
+        scratch_shapes=[vmem((4, nz, rows, width)), vmem((4, nz, rows, width))]
+        + [vmem((nz, half, width)) for _ in range(2)]
+        + [vmem((nz, rows, width)) for _ in range(4)]
+        + [dma((4, nz)), dma((4, nz)), dma((4, nz))]
+        + [dma((nz,)) for _ in range(12)],
+        compiler_params=pltpu.CompilerParams(
+            collective_id=collective_id, has_side_effects=True, vmem_limit_bytes=VMEM_LIMIT
+        ),
+    )(p)
+
+
+def experts_routed(
+    hidden_after_attention,
+    expert_ids,
+    expert_norm_gain,
+    w_router,
+    w_gate,
+    w_up,
+    w_down,
+    grad_output,
+):
+    tok_count, d_model = hidden_after_attention.shape
+    n_tensor = lax.axis_size("tensor")
+    n_dp = lax.axis_size("dp")
+    devices = n_dp * n_tensor
+    second_norm_scale = root_mean_square_scale(hidden_after_attention)
+    second_unit_rows = hidden_after_attention * second_norm_scale
+    second_normalized = (second_unit_rows * expert_norm_gain).astype(jnp.bfloat16)
+    experts = w_router.shape[1]
+    topk = expert_ids.shape[1]
+    exp_dev = w_gate.shape[0]
+    most = 2 * ((tok_count * topk * 9 + experts * 16 - 1) // (experts * 16))
+    route_probs = jax.nn.softmax(
+        jnp.dot(second_normalized, w_router, preferred_element_type=jnp.float32), axis=-1
+    )
+    chosen = expert_ids[:, :, None] == jnp.arange(experts, dtype=jnp.int32)[None, None, :]
+    gate_values = jnp.sum(jnp.where(chosen, route_probs[:, None, :], 0.0), axis=-1)
+    flat_ids, pair_rank = slot_positions(expert_ids, experts)
+    pair_slot = (flat_ids % exp_dev * n_dp + flat_ids // exp_dev) * most + pair_rank
+    pair_count = tok_count * topk
+    slot_count = exp_dev * n_dp * most
+    slot_owner = (
+        jnp.full((slot_count,), pair_count, jnp.int32)
+        .at[pair_slot]
+        .set(jnp.arange(pair_count, dtype=jnp.int32))
+    )
+    padded = jnp.concatenate([second_normalized, jnp.zeros((1, d_model), jnp.bfloat16)], axis=0)
+    outgoing = padded[slot_owner // topk].reshape(exp_dev, n_dp, most, d_model)
+    copies = jnp.broadcast_to(
+        outgoing[:, :, None], (exp_dev, n_dp, n_tensor, most, d_model)
+    ).reshape(exp_dev, devices, most, d_model)
+    arrived = lax.all_to_all(copies, ("dp", "tensor"), split_axis=1, concat_axis=1, tiled=True)
+    expert_rows = arrived.reshape(exp_dev, devices * most, d_model)
+    gate_pre = jnp.einsum("erd,edf->erf", expert_rows, w_gate, preferred_element_type=jnp.float32)
+    up_pre = jnp.einsum("erd,edf->erf", expert_rows, w_up, preferred_element_type=jnp.float32)
+    gate_sigmoid = jax.nn.sigmoid(gate_pre)
+    silu_gate = gate_pre * gate_sigmoid
+    hidden = (silu_gate * up_pre).astype(jnp.bfloat16)
+    partial_value = (
+        jnp.einsum("erf,efd->erd", hidden, w_down, preferred_element_type=jnp.float32)
+        .astype(jnp.bfloat16)
+        .reshape(exp_dev, devices, most, d_model)
+    )
+    returned = lax.all_to_all(
+        partial_value, ("dp", "tensor"), split_axis=1, concat_axis=1, tiled=True
+    )
+    expert_out = jnp.sum(
+        returned.reshape(exp_dev, n_dp, n_tensor, most, d_model).astype(jnp.float32), axis=2
+    ).reshape(slot_count, d_model)
+    pair_out = expert_out[pair_slot].reshape(tok_count, topk, d_model)
+    result = (hidden_after_attention + jnp.sum(gate_values[:, :, None] * pair_out, axis=1)).astype(
+        jnp.bfloat16
+    )
+    cotangent = grad_output.astype(jnp.float32)
+    grad_gates = jnp.sum(pair_out * cotangent[:, None, :], axis=-1)
+    grad_pairs = (
+        (gate_values[:, :, None] * cotangent[:, None, :])
+        .astype(jnp.bfloat16)
+        .reshape(pair_count, d_model)
+    )
+    grad_slots = jnp.concatenate([grad_pairs, jnp.zeros((1, d_model), jnp.bfloat16)], axis=0)[
+        slot_owner
+    ].reshape(exp_dev, n_dp, most, d_model)
+    grad_copies = jnp.broadcast_to(
+        grad_slots[:, :, None], (exp_dev, n_dp, n_tensor, most, d_model)
+    ).reshape(exp_dev, devices, most, d_model)
+    grad_arrived = lax.all_to_all(
+        grad_copies, ("dp", "tensor"), split_axis=1, concat_axis=1, tiled=True
+    )
+    grad_rows = grad_arrived.reshape(exp_dev, devices * most, d_model)
+    grad_hidden = jnp.einsum("erd,efd->erf", grad_rows, w_down, preferred_element_type=jnp.float32)
+    grad_down = jnp.einsum("erf,erd->efd", hidden, grad_rows, preferred_element_type=jnp.float32)
+    grad_gate_pre = (
+        grad_hidden * up_pre * gate_sigmoid * (1.0 + gate_pre * (1.0 - gate_sigmoid))
+    ).astype(jnp.bfloat16)
+    grad_up_pre = (grad_hidden * silu_gate).astype(jnp.bfloat16)
+    grad_gate = jnp.einsum(
+        "erd,erf->edf", expert_rows, grad_gate_pre, preferred_element_type=jnp.float32
+    )
+    grad_up = jnp.einsum(
+        "erd,erf->edf", expert_rows, grad_up_pre, preferred_element_type=jnp.float32
+    )
+    grad_expert_in = jnp.einsum(
+        "erf,edf->erd", grad_gate_pre, w_gate, preferred_element_type=jnp.float32
+    )
+    grad_expert_in = grad_expert_in + jnp.einsum(
+        "erf,edf->erd", grad_up_pre, w_up, preferred_element_type=jnp.float32
+    )
+    grad_expert_in = grad_expert_in.astype(jnp.bfloat16).reshape(exp_dev, devices, most, d_model)
+    grad_back = lax.all_to_all(
+        grad_expert_in, ("dp", "tensor"), split_axis=1, concat_axis=1, tiled=True
+    )
+    grad_slot_in = jnp.sum(
+        grad_back.reshape(exp_dev, n_dp, n_tensor, most, d_model).astype(jnp.float32), axis=2
+    ).reshape(slot_count, d_model)
+    grad_second_normalized = jnp.sum(
+        grad_slot_in[pair_slot].reshape(tok_count, topk, d_model), axis=1
+    )
+    grad_route = jnp.sum(jnp.where(chosen, grad_gates[:, :, None], 0.0), axis=1)
+    grad_logits = (
+        route_probs * (grad_route - jnp.sum(route_probs * grad_route, axis=-1, keepdims=True))
+    ).astype(jnp.bfloat16)
+    grad_router_part = jnp.einsum(
+        "td,te->de", second_normalized, grad_logits, preferred_element_type=jnp.float32
+    )
+    grad_second_normalized = grad_second_normalized + jnp.einsum(
+        "te,de->td", grad_logits, w_router, preferred_element_type=jnp.float32
+    )
+    grad_expert_share = jnp.sum(grad_second_normalized * second_unit_rows, axis=0)
+    grad_second_unit_rows = grad_second_normalized * expert_norm_gain
+    grad_hidden_one = (
+        second_norm_scale
+        * (
+            grad_second_unit_rows
+            - second_unit_rows
+            * jnp.mean(grad_second_unit_rows * second_unit_rows, axis=-1, keepdims=True)
+        )
+        + cotangent
+    )
+    return (
+        result,
+        grad_hidden_one,
+        grad_expert_share,
+        grad_router_part,
+        grad_gate,
+        grad_up,
+        grad_down,
+    )
+
+
+def experts_dense(
+    hidden_after_attention,
+    expert_ids,
+    expert_norm_gain,
+    w_router,
+    w_gate,
+    w_up,
+    w_down,
+    grad_output,
+):
+    tok_count, d_model = hidden_after_attention.shape
+    n_tensor = lax.axis_size("tensor")
+    n_dp = lax.axis_size("dp")
+    devices = n_dp * n_tensor
+    everyone = ("dp", "tensor")
+    second_norm_scale = root_mean_square_scale(hidden_after_attention)
+    second_unit_rows = hidden_after_attention * second_norm_scale
+    second_normalized = (second_unit_rows * expert_norm_gain).astype(jnp.bfloat16)
+    experts = w_router.shape[1]
+    exp_dev, _, width = w_gate.shape
+    all_count = devices * tok_count
+    expert_at = jnp.arange(experts, dtype=jnp.int32)
+    local_at = lax.axis_index("dp") * exp_dev + jnp.arange(exp_dev, dtype=jnp.int32)
+
+    all_rows = gather_all(second_normalized, n_tensor, 0).reshape(all_count, d_model)
+    all_cotangents = lax.all_gather(grad_output, everyone, axis=0, tiled=True)
+    all_ids = lax.all_gather(expert_ids, everyone, axis=0, tiled=True)
+
+    def route(rows):
+        return jax.nn.softmax(
+            jnp.dot(rows, w_router, preferred_element_type=jnp.float32), axis=-1
+        )
+
+    down_rows = w_down.reshape(exp_dev * width, d_model)
+    wide = jnp.concatenate([w_gate[e] for e in range(exp_dev)] + [w_up[e] for e in range(exp_dev)], axis=1)
+    all_route = route(all_rows)
+    named = jnp.any(all_ids[:, :, None] == local_at[None, None, :], axis=1)
+    local_route = jnp.sum(
+        jnp.where(local_at[None, :, None] == expert_at[None, None, :], all_route[:, None, :], 0.0), axis=-1
+    )
+    local_gate = jnp.where(named, local_route, 0.0)
+    spread = jnp.repeat(local_gate, width, axis=1)
+    both = exp_dev * width
+    pre = jnp.dot(all_rows, wide, preferred_element_type=jnp.float32)
+    gate_pre, up_pre = pre[:, :both], pre[:, both:]
+    gate_sigmoid = jax.nn.sigmoid(gate_pre)
+    silu_gate = gate_pre * gate_sigmoid
+    hidden = silu_gate * up_pre
+    gated_hidden = (spread * hidden).astype(jnp.bfloat16)
+    out_part = jnp.dot(gated_hidden, down_rows, preferred_element_type=jnp.float32).astype(jnp.bfloat16)
+    back = jnp.einsum("td,fd->tf", all_cotangents, down_rows, preferred_element_type=jnp.float32)
+    gate_grads = jnp.sum((hidden * back).reshape(all_count, exp_dev, width), axis=-1)
+    grad_hidden = spread * back
+    grad_gate_pre = (
+        grad_hidden * up_pre * gate_sigmoid * (1.0 + gate_pre * (1.0 - gate_sigmoid))
+    ).astype(jnp.bfloat16)
+    grad_up_pre = (grad_hidden * silu_gate).astype(jnp.bfloat16)
+    grad_pre = jnp.concatenate([grad_gate_pre, grad_up_pre], axis=1)
+    in_part = jnp.einsum("tf,df->td", grad_pre, wide, preferred_element_type=jnp.float32).astype(jnp.bfloat16)
+    grad_in = scatter_all(in_part.reshape(devices, tok_count, d_model), n_tensor, 1)
+    moe_out = scatter_all(out_part.reshape(devices, tok_count, d_model), n_tensor, 1)
+    grad_down = jnp.einsum(
+        "tf,td->fd", gated_hidden, all_cotangents, preferred_element_type=jnp.float32
+    ).reshape(exp_dev, width, d_model)
+    grad_wide = jnp.einsum("td,tf->df", all_rows, grad_pre, preferred_element_type=jnp.float32)
+    grad_gate = jnp.stack([grad_wide[:, e * width : (e + 1) * width] for e in range(exp_dev)])
+    grad_up = jnp.stack([grad_wide[:, both + e * width : both + (e + 1) * width] for e in range(exp_dev)])
+
+    route_grads = jnp.sum(
+        jnp.where(
+            (named[:, :, None]) & (local_at[None, :, None] == expert_at[None, None, :]),
+            gate_grads[:, :, None],
+            0.0,
+        ),
+        axis=1,
+    )
+    grad_route = lax.psum_scatter(route_grads, everyone, scatter_dimension=0, tiled=True)
+    cotangent = grad_output.astype(jnp.float32)
+    result = (hidden_after_attention + moe_out).astype(jnp.bfloat16)
+    route_probs = route(second_normalized)
+    grad_logits = (
+        route_probs * (grad_route - jnp.sum(route_probs * grad_route, axis=-1, keepdims=True))
+    ).astype(jnp.bfloat16)
+    grad_router_part = jnp.einsum(
+        "td,te->de", second_normalized, grad_logits, preferred_element_type=jnp.float32
+    )
+    grad_second_normalized = grad_in + jnp.einsum(
+        "te,de->td", grad_logits, w_router, preferred_element_type=jnp.float32
+    )
+    grad_expert_share = jnp.sum(grad_second_normalized * second_unit_rows, axis=0)
+    grad_second_unit_rows = grad_second_normalized * expert_norm_gain
+    grad_hidden_one = (
+        second_norm_scale
+        * (
+            grad_second_unit_rows
+            - second_unit_rows
+            * jnp.mean(grad_second_unit_rows * second_unit_rows, axis=-1, keepdims=True)
+        )
+        + cotangent
+    )
+    return (
+        result,
+        grad_hidden_one,
+        grad_expert_share,
+        grad_router_part,
+        grad_gate,
+        grad_up,
+        grad_down,
+    )
 
 
 def local(
@@ -125,125 +735,24 @@
     log_totals = [log_total]
     context = context_blocks.reshape(seq_len, local_dim).astype(jnp.bfloat16)
     attn_out = lax.psum_scatter(
-        jnp.dot(context, w_output, preferred_element_type=jnp.float32),
+        jnp.dot(context, w_output, preferred_element_type=jnp.float32).astype(jnp.bfloat16),
         "tensor",
         scatter_dimension=0,
         tiled=True,
-    )
+    ).astype(jnp.float32)
     hidden_after_attention = input_tensors + attn_out
-    second_norm_scale = root_mean_square_scale(hidden_after_attention)
-    second_unit_rows = hidden_after_attention * second_norm_scale
-    second_normalized = (second_unit_rows * expert_norm_gain).astype(jnp.bfloat16)
-    experts = w_router.shape[1]
-    topk = expert_ids.shape[1]
-    exp_dev = w_gate.shape[0]
-    most = 2 * ((tok_count * topk * 9 + experts * 16 - 1) // (experts * 16))
-    route_probs = jax.nn.softmax(
-        jnp.dot(second_normalized, w_router, preferred_element_type=jnp.float32), axis=-1
-    )
-    chosen = expert_ids[:, :, None] == jnp.arange(experts, dtype=jnp.int32)[None, None, :]
-    gate_values = jnp.sum(jnp.where(chosen, route_probs[:, None, :], 0.0), axis=-1)
-    flat_ids, pair_rank = slot_positions(expert_ids, experts)
-    pair_slot = (flat_ids % exp_dev * n_dp + flat_ids // exp_dev) * most + pair_rank
-    pair_count = tok_count * topk
-    slot_count = exp_dev * n_dp * most
-    slot_owner = (
-        jnp.full((slot_count,), pair_count, jnp.int32)
-        .at[pair_slot]
-        .set(jnp.arange(pair_count, dtype=jnp.int32))
-    )
-    padded = jnp.concatenate([second_normalized, jnp.zeros((1, d_model), jnp.bfloat16)], axis=0)
-    outgoing = padded[slot_owner // topk].reshape(exp_dev, n_dp, most, d_model)
-    copies = jnp.broadcast_to(
-        outgoing[:, :, None], (exp_dev, n_dp, n_tensor, most, d_model)
-    ).reshape(exp_dev, devices, most, d_model)
-    arrived = lax.all_to_all(copies, ("dp", "tensor"), split_axis=1, concat_axis=1, tiled=True)
-    expert_rows = arrived.reshape(exp_dev, devices * most, d_model)
-    gate_pre = jnp.einsum("erd,edf->erf", expert_rows, w_gate, preferred_element_type=jnp.float32)
-    up_pre = jnp.einsum("erd,edf->erf", expert_rows, w_up, preferred_element_type=jnp.float32)
-    gate_sigmoid = jax.nn.sigmoid(gate_pre)
-    silu_gate = gate_pre * gate_sigmoid
-    hidden = (silu_gate * up_pre).astype(jnp.bfloat16)
-    partial_value = (
-        jnp.einsum("erf,efd->erd", hidden, w_down, preferred_element_type=jnp.float32)
-        .astype(jnp.bfloat16)
-        .reshape(exp_dev, devices, most, d_model)
-    )
-    returned = lax.all_to_all(
-        partial_value, ("dp", "tensor"), split_axis=1, concat_axis=1, tiled=True
-    )
-    expert_out = jnp.sum(
-        returned.reshape(exp_dev, n_dp, n_tensor, most, d_model).astype(jnp.float32), axis=2
-    ).reshape(slot_count, d_model)
-    pair_out = expert_out[pair_slot].reshape(tok_count, topk, d_model)
-    result = (hidden_after_attention + jnp.sum(gate_values[:, :, None] * pair_out, axis=1)).astype(
-        jnp.bfloat16
-    )
-    cotangent = grad_output.astype(jnp.float32)
-    grad_gates = jnp.sum(pair_out * cotangent[:, None, :], axis=-1)
-    grad_pairs = (
-        (gate_values[:, :, None] * cotangent[:, None, :])
-        .astype(jnp.bfloat16)
-        .reshape(pair_count, d_model)
-    )
-    grad_slots = jnp.concatenate([grad_pairs, jnp.zeros((1, d_model), jnp.bfloat16)], axis=0)[
-        slot_owner
-    ].reshape(exp_dev, n_dp, most, d_model)
-    grad_copies = jnp.broadcast_to(
-        grad_slots[:, :, None], (exp_dev, n_dp, n_tensor, most, d_model)
-    ).reshape(exp_dev, devices, most, d_model)
-    grad_arrived = lax.all_to_all(
-        grad_copies, ("dp", "tensor"), split_axis=1, concat_axis=1, tiled=True
-    )
-    grad_rows = grad_arrived.reshape(exp_dev, devices * most, d_model)
-    grad_hidden = jnp.einsum("erd,efd->erf", grad_rows, w_down, preferred_element_type=jnp.float32)
-    grad_down = jnp.einsum("erf,erd->efd", hidden, grad_rows, preferred_element_type=jnp.float32)
-    grad_gate_pre = (
-        grad_hidden * up_pre * gate_sigmoid * (1.0 + gate_pre * (1.0 - gate_sigmoid))
-    ).astype(jnp.bfloat16)
-    grad_up_pre = (grad_hidden * silu_gate).astype(jnp.bfloat16)
-    grad_gate = jnp.einsum(
-        "erd,erf->edf", expert_rows, grad_gate_pre, preferred_element_type=jnp.float32
-    )
-    grad_up = jnp.einsum(
-        "erd,erf->edf", expert_rows, grad_up_pre, preferred_element_type=jnp.float32
-    )
-    grad_expert_in = jnp.einsum(
-        "erf,edf->erd", grad_gate_pre, w_gate, preferred_element_type=jnp.float32
-    )
-    grad_expert_in = grad_expert_in + jnp.einsum(
-        "erf,edf->erd", grad_up_pre, w_up, preferred_element_type=jnp.float32
-    )
-    grad_expert_in = grad_expert_in.astype(jnp.bfloat16).reshape(exp_dev, devices, most, d_model)
-    grad_back = lax.all_to_all(
-        grad_expert_in, ("dp", "tensor"), split_axis=1, concat_axis=1, tiled=True
-    )
-    grad_slot_in = jnp.sum(
-        grad_back.reshape(exp_dev, n_dp, n_tensor, most, d_model).astype(jnp.float32), axis=2
-    ).reshape(slot_count, d_model)
-    grad_second_normalized = jnp.sum(
-        grad_slot_in[pair_slot].reshape(tok_count, topk, d_model), axis=1
-    )
-    grad_route = jnp.sum(jnp.where(chosen, grad_gates[:, :, None], 0.0), axis=1)
-    grad_logits = (
-        route_probs * (grad_route - jnp.sum(route_probs * grad_route, axis=-1, keepdims=True))
-    ).astype(jnp.bfloat16)
-    grad_router_part = jnp.einsum(
-        "td,te->de", second_normalized, grad_logits, preferred_element_type=jnp.float32
-    )
-    grad_second_normalized = grad_second_normalized + jnp.einsum(
-        "te,de->td", grad_logits, w_router, preferred_element_type=jnp.float32
-    )
-    grad_expert_share = jnp.sum(grad_second_normalized * second_unit_rows, axis=0)
-    grad_second_unit_rows = grad_second_normalized * expert_norm_gain
-    grad_hidden_one = (
-        second_norm_scale
-        * (
-            grad_second_unit_rows
-            - second_unit_rows
-            * jnp.mean(grad_second_unit_rows * second_unit_rows, axis=-1, keepdims=True)
-        )
-        + cotangent
+    dense = n_dp == 8 and n_dp <= expert_ids.shape[1]
+    result, grad_hidden_one, grad_expert_share, grad_router_part, grad_gate, grad_up, grad_down = (
+        experts_dense if dense else experts_routed
+    )(
+        hidden_after_attention,
+        expert_ids,
+        expert_norm_gain,
+        w_router,
+        w_gate,
+        w_up,
+        w_down,
+        grad_output,
     )
     grad_attn = grad_hidden_one.astype(jnp.bfloat16)
     grad_attn_all = lax.all_gather(grad_attn, "tensor", axis=0, tiled=True)

time: 2380 us -> 944 us (0.40)
  waiting for transfers between devices: 1820 us -> 231 us
  Pallas kernels: 0 us -> 288 us
  local copies, waits for them, and re-layouts: 164 us -> 20.8 us
  blocking collectives: 71.9 us -> 142 us
  starting transfers between devices: 58.5 us -> 0.33 us
    all_to_all x4 -> x0, waiting for transfers between devices: 1470 us -> none  [the longest x1 380 us: local(): lax.all_to_all(grad_copies, ('dp', 'tensor'), split_axis=1, concat_axis=1...]
    pallas_call x0 -> x3, Pallas kernels: none -> 288 us  [the longest x2 177 us: scatter_all(): pl.pallas_call(functools.partial(scatter_kernel, nz), name='scatter_all',...]
    all_gather x0 -> x1, blocking collectives: none -> 68.3 us  [experts_dense(): all_ids = lax.all_gather(expert_ids, everyone, axis=0, tiled=True)]
    reduce_scatter x1, waiting for transfers between devices: 64.8 us -> 0.01 us  [local(): lax.psum_scatter(jnp.dot(context, w_output, preferred_element_type=jnp.fl...]
    all_to_all x4 -> x0, starting transfers between devices: 57.4 us -> none  [the longest x1 17.6 us: local(): lax.all_to_all(partial_value, ('dp', 'tensor'), split_axis=1, concat_axis...]
    gather x4 -> x0, local copies, waits for them, and re-layouts: 44.8 us -> none  [the longest x1 13.4 us: local(): jnp.concatenate([grad_pairs, jnp.zeros((1, d_model), jnp.bfloat16)], axis=0)]
    reduce_sum x9 -> x4, other arithmetic: 41.4 us -> 1.72 us  [the longest x1 0.9 us: experts_dense(): jnp.sum(jnp.where(named[:, :, None] & (local_at[None, :, None] == expert_...]
    all_gather x1, waiting for transfers between devices: 58.4 us -> 20.5 us  [local(): grad_attn_all = lax.all_gather(grad_attn, 'tensor', axis=0, tiled=True)]
  transfers between devices with their start and end apart: 10 -> 8, of which waited for: 9 -> 4; matrix products, arithmetic and copies ran while one was open for 10% -> 19% of each run, Pallas kernels for 0% -> 31%
where the time goes in v1:
time: 944 us; the launch traced here: 937 us
  Pallas kernels  288 us (31%)
  waiting for transfers between devices  231 us (24%)
  matrix products  165 us (17%)
  blocking collectives  142 us (15%)
  other arithmetic  73.4 us (8%)
  local copies, waits for them, and re-layouts  20.8 us (2%)
  between operations  16.7 us (2%)
    pallas_call x2, Pallas kernels, scatter_all(): pl.pallas_call(functools.partial(scatter_kernel, nz), name='scatter_all',...  177 us
    pallas_call x1, Pallas kernels, gather_all(): pl.pallas_call(functools.partial(gather_kernel, nz), name='gather_all', o...  111 us
    psum x1, waiting for transfers between devices, local(): lax.psum(grad_query_part.astype(jnp.bfloat16), 'dp').astype(jnp.float32)  84.7 us
    psum x1, waiting for transfers between devices, local(): lax.psum((grad_attention_share, grad_expert_share, grad_router_part), ('d...  78.9 us
    all_gather x1, blocking collectives, experts_dense(): all_ids = lax.all_gather(expert_ids, everyone, axis=0, tiled=True)  68.3 us
    all_gather x1, waiting for transfers between devices, local(): normed_all = lax.all_gather(first_normalized, 'tensor', axis=0, tiled=True)  46 us
    psum x1, blocking collectives, local(): lax.psum((grad_attention_share, grad_expert_share, grad_router_part), ('d...  39.5 us
    dot_general x1, matrix products, experts_dense(): jnp.einsum('td,tf->df', all_rows, grad_pre, preferred_element_type=jnp.fl...  24.5 us
  transfers between devices with their start and end apart: 8, of which 4 were waited for; matrix products, arithmetic and copies ran while one was open for 19% of the time, Pallas kernels for 31%

profile of v1, /device:TPU:0, one launch (start us, length us, event | category | flops | bytes accessed | tf_op | source)
XLA Modules:
  0.0 937.2 jit_solution(15713702648295688144)
XLA Ops:
  9.5 2.0 fusion.14
  14.0 46.0 %all-gather.4.cloned.1.call-done = bf16[512,2048]{1,0:T(8,128)(2,1)} async-done(((bf16[128,2048]{1,0:T(8,128)(2,1)}), bf16[512,2048]{1,0:T(8,128)(2,1)}) %all-gather.4.cloned.1.call-update) | async-done | bytes 2097168 | tf_op jit(solution)/shard_map/all_gather | solution.py:706
  60.0 4.6 multiply_reduce_fusion.6
  64.7 2.3 multiply_reduce_fusion.7
  67.0 9.8 %all-reduce.2 = (f32[512]{0:T(512)S(1)}, f32[512]{0:T(512)S(1)}) all-reduce(f32[512]{0:T(512)S(1)} %get-tuple-element.69, f32[512]{0:T(512)S(1)} %get-tuple-element.71), channel_id=1, replica_groups=mesh['dp'=8,'tensor'=4] {'tensor'}, use_global_device_ids=true, to_apply=%region_2.0 | all-reduce | flops 1024 | bytes 8192 | tf_op jit(solution)/shard_map/psum | solution.py:714
  82.5 2.1 copy-done.60
  88.2 2.6 convolution_convert_fusion.6
  91.5 68.3 %all_gather.13 = s32[4096,8]{0,1:T(8,128)S(1)} all-gather(s32[128,8]{0,1:T(8,128)S(1)} %copy-done.57), channel_id=1, replica_groups=mesh['dp'=8,'tensor'=4] {'dp','tensor'}, dimensions={0}, use_global_device_ids=true | all-gather | bytes 135168 | tf_op jit(solution)/shard_map/all_gather | solution.py:587
  160.1 4.4 slice_bitcast_fusion.5
  167.0 111.4 %gather_all.1 = bf16[32,128,2048]{2,1,0:T(8,128)(2,1)S(1)} custom-call(bf16[128,2048]{1,0:T(8,128)(2,1)S(1)} %multiply_convert_fusion.5.x_ref), custom_call_target="tpu_custom_call" | custom-call | tf_op jit(solution)/shard_map/gather_all/pallas_call | solution.py:212
  278.8 4.4 fusion.41
  283.2 2.3 copy-done.1
  285.7 22.4 %fusion.26 = f32[4096,1024]{0,1:T(8,128)} fusion(bf16[4096,2048]{1,0:T(8,128)(2,1)} %bitcast.118, bf16[2048,256]{1,0:T(8,128)(2,1)S(1)} %copy-done.35, bf16[2048,256]{1,0:T(8,128)(2,1)S(1)} %copy-done.34, bf16[2048,256]{1,0:T(8,128)(2,1)S(1)} %copy-done.36, bf16[2048,256]{1,0:T(8,128)(2,1)S(1)} %copy-done.37), kind=kOutput, calls=%fused_computation.92 | convolution fusion | flops 17196646400 | bytes 37748736 | tf_op jit(solution)/shard_map/dot_general | solution.py:604
  308.1 20.2 %bitcast_reduce_fusion = (f32[4096,2]{0,1:T(2,128)S(1)}, f32[4096,512]{0,1:T(8,128)}) fusion(f32[4096,1024]{0,1:T(8,128)} %fusion.26, bf16[4096,2048]{1,0:T(8,128)(2,1)} %all-gather.6.cloned.1.call-done, bf16[512,2048]{1,0:T(8,128)(2,1)S(1)} %bitcast.116), kind=kOutput, calls=%fused_computation.6 | convolution fusion | flops 8604606464 | bytes 44072960 | tf_op jit(solution)/shard_map/td,fd->tf/dot_general | solution.py:611
  329.3 23.3 %multiply_convert_fusion.1 = (bf16[4096,512]{0,1:T(8,128)(2,1)}, bf16[4096,512]{0,1:T(8,128)(2,1)}, bf16[4096,512]{0,1:T(8,128)(2,1)}) fusion(f32[4096,512]{0,1:T(8,128)} %get-tuple-element.76, f32[4096,1024]{0,1:T(8,128)} %fusion.26, f32[4096,2]{0,1:T(2,128)S(1)} %broadcast_select_fusion), kind=kLoop, calls=%fused_computation.8 | loop fusion | flops 35651584 | bytes 37781504 | tf_op jit(solution)/shard_map/convert_element_type | solution.py:616
  352.6 24.0 %convolution_convert_fusion = bf16[4096,2048]{1,0:T(8,128)(2,1)} fusion(bf16[4096,512]{0,1:T(8,128)(2,1)} %get-tuple-element.37, bf16[4096,512]{0,1:T(8,128)(2,1)} %get-tuple-element.36, bf16[2048,256]{1,0:T(8,128)(2,1)} %get-tuple-element.46, bf16[2048,256]{1,0:T(8,128)(2,1)} %get-tuple-element.45, bf16[2048,256]{1,0:T(8,128)(2,1)} %get-tuple-element.89, ...), kind=kOutput, calls=%fused_computation | convolution fusion | flops 17221812224 | bytes 29360128 | tf_op jit(solution)/shard_map/tf,df->td/dot_general | solution.py:619
  376.7 88.4 %scatter_all.3 = f32[128,2048]{1,0:T(8,128)} custom-call(bf16[32,128,2048]{2,1,0:T(8,128)(2,1)} %bitcast.120), custom_call_target="tpu_custom_call" | custom-call | tf_op jit(solution)/shard_map/scatter_all/pallas_call | solution.py:405
  466.5 1.8 multiply_reduce_fusion.1
  469.3 2.3 fusion.38
  471.6 24.5 %fusion.2 = f32[2048,1024]{1,0:T(8,128)} fusion(bf16[4096,2048]{1,0:T(8,128)(2,1)} %bitcast.119, bf16[4096,512]{0,1:T(8,128)(2,1)} %get-tuple-element.37, bf16[4096,512]{0,1:T(8,128)(2,1)} %get-tuple-element.36), kind=kOutput, calls=%fused_computation.12 | convolution fusion | flops 17196646400 | bytes 33554432 | tf_op jit(solution)/shard_map/td,tf->df/dot_general | solution.py:625
  496.1 20.5 %all-gather.8.cloned.1.call-done = bf16[512,2048]{1,0:T(8,128)(2,1)} async-done(((bf16[128,2048]{1,0:T(8,128)(2,1)}), bf16[512,2048]{1,0:T(8,128)(2,1)}) %all-gather.8.cloned.1.call-update) | async-done | bytes 2097168 | tf_op jit(solution)/shard_map/all_gather | solution.py:758
  516.7 3.7 convolution_convert_fusion.7
  520.4 2.2 convolution_convert_fusion.9
  522.5 1.6 multiply_reduce_fusion
  529.4 10.1 %all-reduce.1 = (f32[512]{0:T(512)S(1)}, f32[512]{0:T(512)S(1)}) all-reduce(f32[512]{0:T(512)S(1)} %get-tuple-element.17, f32[512]{0:T(512)S(1)} %get-tuple-element.15), channel_id=1, replica_groups=mesh['dp'=8,'tensor'=4] {'tensor'}, use_global_device_ids=true, to_apply=%region_22.23 | all-reduce | flops 1024 | bytes 8192 | tf_op jit(solution)/shard_map/psum | solution.py:798
  539.5 1.9 multiply_convert_fusion.4
  541.5 1.9 multiply_convert_fusion.3
  546.9 2.6 add_convert_fusion
  549.6 14.7 %convolution_convert_fusion.1 = bf16[4096,2048]{1,0:T(8,128)(2,1)} fusion(bf16[4096,512]{0,1:T(8,128)(2,1)} %get-tuple-element.38, bf16[512,2048]{1,0:T(8,128)(2,1)S(1)} %bitcast.115), kind=kOutput, calls=%fused_computation.1 | convolution fusion | flops 8598323200 | bytes 23068672 | tf_op jit(solution)/shard_map/dot_general | solution.py:610
  564.3 88.7 %scatter_all.2 = f32[128,2048]{1,0:T(8,128)} custom-call(bf16[32,128,2048]{2,1,0:T(8,128)(2,1)} %bitcast.121), custom_call_target="tpu_custom_call" | custom-call | tf_op jit(solution)/shard_map/scatter_all/pallas_call | solution.py:405
  653.0 6.1 slice_bitcast_fusion.1
  659.1 2.3 pad_maximum_fusion.5
  662.0 2.6 convolution_convert_fusion.2
  664.6 2.7 convolution_convert_fusion.3
  667.2 2.6 convolution_convert_fusion.4
  669.9 2.6 convolution_convert_fusion.5
  672.6 4.8 pad_maximum_fusion.4
  677.5 13.9 %fusion.45 = f32[512,2048]{1,0:T(8,128)} fusion(bf16[4096,512]{0,1:T(8,128)(2,1)S(1)} %copy-done.19, bf16[4096,2048]{1,0:T(8,128)(2,1)} %all-gather.6.cloned.1.call-done), kind=kOutput, calls=%fused_computation.140 | convolution fusion | flops 8589934592 | bytes 25165824 | tf_op jit(solution)/shard_map/tf,td->fd/dot_general | solution.py:622
  692.3 14.2 %all-reduce.3 = (bf16[512]{0:T(512)(128)(2,1)S(1)}, bf16[512]{0:T(512)(128)(2,1)S(1)}) all-reduce(bf16[512]{0:T(512)(128)(2,1)S(1)} %get-tuple-element.16, bf16[512]{0:T(512)(128)(2,1)S(1)} %get-tuple-element.14), channel_id=1, replica_groups=mesh['dp'=8,'tensor'=4] {'dp'}, use_global_device_ids=true, to_apply=%region_32.33 | all-reduce | flops 1024 | bytes 4096 | tf_op jit(solution)/shard_map/psum | solution.py:847
  709.1 3.6 fusion.13
  712.7 84.7 %all-reduce.10.cloned.1.call-done = (bf16[2048,512]{1,0:T(8,128)(2,1)}, bf16[2048,512]{1,0:T(8,128)(2,1)}, bf16[2048,512]{1,0:T(8,128)(2,1)}, bf16[512,2048]{1,0:T(8,128)(2,1)}) async-done(((bf16[2048,512]{1,0:T(8,128)(2,1)}, bf16[2048,512]{1,0:T(8,128)(2,1)}, bf16[2048,512]{1,0:T(8,128)(2,1)}, bf16[512,2048]{1,0:T(8,128)(2,1)}), (bf16[2048,512]{1,0:T(8,128)(2,1)}, bf16[2048,512]{1,0:T(8,128)(2,1)}, ...) | async-done | bytes 8388624 | tf_op jit(solution)/shard_map/psum | solution.py:843
  797.4 4.3 convert_element_type.162
  801.8 2.6 convert_element_type.164
  804.4 2.6 convert_element_type.166
  807.0 2.5 convert_element_type.168
  809.5 39.5 %all-reduce = (f32[2048]{0:T(1024)}, f32[2048]{0:T(1024)}) all-reduce(f32[2048]{0:T(1024)S(1)} %get-tuple-element.20, f32[2048]{0:T(1024)S(1)} %get-tuple-element.18), channel_id=1, replica_groups=mesh['dp'=8,'tensor'=4] {'dp','tensor'}, use_global_device_ids=true, to_apply=%region_36.37 | all-reduce | flops 4096 | bytes 32768 | tf_op jit(solution)/shard_map/psum | solution.py:850
  849.1 78.9 %all-reduce.8.cloned.1.call-done = f32[2048,16]{0,1:T(8,128)} async-done(((f32[2048,16]{0,1:T(8,128)}), f32[2048,16]{0,1:T(8,128)}) %all-reduce.8.cloned.1.call-update) | async-done | bytes 131088 | tf_op jit(solution)/shard_map/psum | solution.py:850
  928.0 1.6 copy.74
  (197 shorter events, 33.1 us)
Async XLA Ops:
  8.0 300.1 %copy-start = (bf16[2,256,2048]{2,1,0:T(8,128)(2,1)S(1)}, bf16[2,256,2048]{2,1,0:T(8,128)(2,1)}, u32[]{:S(2)}) copy-start(bf16[2,256,2048]{2,1,0:T(8,128)(2,1)} %param.30) | copy-start | bytes 6291460
  8.0 52.0 %all-gather.4.cloned.1.call-start = ((), (), s32[]{:S(2)}) async-start(), calls=%async_computation.3 | async-start | bytes 2621440 | tf_op jit(solution)/shard_map/all_gather | solution.py:706
  11.5 152.9 %reduce-scatter.4.cloned.1.call-start = ((), (), s32[]{:S(2)}) async-start(), calls=%async_computation.4 | async-start | bytes 2621440 | tf_op jit(solution)/shard_map/reduce_scatter | solution.py:737
  14.0 71.9 %copy-start.13 = (pred[512,512]{0,1:T(8,128)(4,1)}, pred[512,512]{0,1:T(8,128)(4,1)S(1)}, u32[]{:S(2)}) copy-start(pred[512,512]{0,1:T(8,128)(4,1)S(1)} %fusion.24) | copy-start | bytes 786436
  60.0 4.6 copy-start.29
  60.0 4.6 copy-start.59
  64.7 12.2 %copy-start.51 = (f32[512]{0:T(512)S(1)}, f32[512]{0:T(512)}, u32[]{:S(2)}) copy-start(f32[512]{0:T(512)} %param.23) | copy-start | bytes 6148
  67.0 11.4 %copy-start.53 = (f32[512]{0:T(512)S(1)}, f32[512]{0:T(512)}, u32[]{:S(2)}) copy-start(f32[512]{0:T(512)} %param.24) | copy-start | bytes 6148
  76.8 3.0 copy-start.47
  76.8 3.0 copy-start.49
  80.5 4.1 copy-start.60
  81.5 4.4 copy-start.4
  86.0 2.2 copy-start.58
  88.2 3.3 copy-start.57
  90.8 217.3 %all-gather.6.cloned.1.call-start = ((), (), s32[]{:S(2)}) async-start(), calls=%async_computation.5 | async-start | bytes 17301504 | tf_op jit(solution)/shard_map/all_gather | solution.py:586
  91.4 373.7 %reduce-scatter.6.cloned.1.call-start = ((), (), s32[]{:S(2)}) async-start(), calls=%async_computation.6 | async-start | bytes 270336 | tf_op jit(solution)/shard_map/reduce_scatter | solution.py:637
  160.0 4.4 copy-start.6
  160.1 5.7 copy-start.43
  167.0 111.4 %copy-start.2 = (bf16[128,2048]{1,0:T(8,128)(2,1)}, bf16[128,2048]{1,0:T(8,128)(2,1)S(1)}, u32[]{:S(2)}) copy-start(bf16[128,2048]{1,0:T(8,128)(2,1)S(1)} %multiply_convert_fusion.5.x_ref) | copy-start | bytes 1572868
  167.0 111.4 %copy-start.38 = (bf16[2048,16]{0,1:T(8,128)(2,1)S(1)}, bf16[2048,16]{0,1:T(8,128)(2,1)}, u32[]{:S(2)}) copy-start(bf16[2048,16]{0,1:T(8,128)(2,1)} %param.27) | copy-start | bytes 196612
  278.4 7.1 copy-start.1
  278.7 6.9 copy-start.34
  278.8 6.9 copy-start.35
  278.8 6.9 copy-start.36
  278.8 6.9 copy-start.37
  329.3 187.4 %all-gather.8.cloned.1.call-start = ((), (), s32[]{:S(2)}) async-start(), calls=%async_computation.7 | async-start | bytes 2621440 | tf_op jit(solution)/shard_map/all_gather | solution.py:758
  376.7 89.9 %copy-start.7 = (bf16[128,2048]{1,0:T(8,128)(2,1)S(1)}, bf16[128,2048]{1,0:T(8,128)(2,1)}, u32[]{:S(2)}) copy-start(bf16[128,2048]{1,0:T(8,128)(2,1)} %reduce-scatter.4.cloned.1.call-done) | copy-start | bytes 1572868
  471.6 236.0 %reduce-scatter.8.cloned.1.call-start = ((), (), s32[]{:S(2)}) async-start(), calls=%async_computation.8 | async-start | bytes 2621440 | tf_op jit(solution)/shard_map/reduce_scatter | solution.py:822
  496.1 24.2 %copy-start.14 = (pred[512,512]{0,1:T(8,128)(4,1)S(1)}, pred[512,512]{0,1:T(8,128)(4,1)}, u32[]{:S(2)}) copy-start(pred[512,512]{0,1:T(8,128)(4,1)} %copy-done.13) | copy-start | bytes 786436
  496.1 24.2 %copy-start.46 = (f32[4,512]{1,0:T(4,128)S(1)}, f32[4,512]{1,0:T(4,128)}, u32[]{:S(2)}) copy-start(f32[4,512]{1,0:T(4,128)} %copy-done.45) | copy-start | bytes 24580
  516.7 3.7 copy-start.5
  539.5 3.9 copy-start.30
  541.4 3.3 copy-start.20
  549.6 247.8 %all-reduce.10.cloned.1.call-start = ((), (), s32[]{:S(2)}) async-start(), calls=%async_computation.10 | async-start | bytes 16777216 | tf_op jit(solution)/shard_map/psum | solution.py:843
  659.1 2.4 copy-start.62
  659.1 2.9 copy-start.64
  662.0 2.6 copy-start.42
  662.0 2.6 copy-start.61
  664.6 2.7 copy-start.23
  667.2 2.7 copy-start.21
  672.6 255.4 %all-reduce.8.cloned.1.call-start = ((), (), s32[]{:S(2)}) async-start(), calls=%async_computation.9 | async-start | bytes 262144 | tf_op jit(solution)/shard_map/psum | solution.py:850
  672.6 4.8 copy-start.19
  677.5 13.9 %copy-start.3 = (bf16[128,2048]{1,0:T(8,128)(2,1)S(1)}, bf16[128,2048]{1,0:T(8,128)(2,1)}, u32[]{:S(2)}) copy-start(bf16[128,2048]{1,0:T(8,128)(2,1)} %copy-done.2) | copy-start | bytes 1572868
  677.5 30.1 %copy-start.44 = (f32[2048]{0:T(1024)S(1)}, f32[2048]{0:T(1024)}, u32[]{:S(2)}) copy-start(f32[2048]{0:T(1024)} %param.19) | copy-start | bytes 24580
  677.5 30.1 %copy-start.56 = (f32[128]{0:T(128)S(1)}, f32[128]{0:T(128)}, u32[]{:S(2)}) copy-start(f32[128]{0:T(128)} %copy-done.55) | copy-start | bytes 1540
  797.4 4.4 copy-start.28
  801.8 2.6 copy-start.27
  804.4 2.6 copy-start.26
  (25 other events, 40.4 us)
Sparse Core Ops, SparseCore 0:
  11.6 48.3 all-gather.3
  90.9 51.0 reduce-scatter.3
  471.7 44.8 all-gather.7
  549.7 41.8 reduce-scatter.7
  672.7 124.6 all-reduce.9
  803.4 124.5 all-reduce.7
Sparse Core Ops, SparseCore 1:
  94.3 179.5 all-gather.5
  329.3 134.5 reduce-scatter.5

commit v2 on v1

--- a/solution.py
+++ b/solution.py
@@ -83,46 +83,71 @@
     pl.semaphore_wait(barrier, 3 + ends)
 
 
-def gather_kernel(nz, x_ref, out_ref, local_sem, sz, sx, sy, sda, sdb, sc, rz, rx, ry, rda, rdb, rc):
+def remote(src, dst, send, recv, device):
+    return pltpu.make_async_remote_copy(
+        src_ref=src, dst_ref=dst, send_sem=send, recv_sem=recv, device_id=device, device_id_type=MESH
+    )
+
+
+def gather_kernel(nz, x_ref, t_ref, out_ref, tags_ref, local_sem, sz, sx, sy, sda, sdb, sc, rz, rx, ry, rda, rdb, rc):
     dp, z = lax.axis_index("dp"), lax.axis_index("tensor")
     half = x_ref.shape[0] // 2
     greet(dp, z, nz)
 
-    def at(flip, zz):
+    def rows_at(flip, zz):
         return out_ref.at[(dp ^ flip) * nz + zz]
 
-    def remote(src, dst, send, recv, device):
-        return pltpu.make_async_remote_copy(
-            src_ref=src, dst_ref=dst, send_sem=send, recv_sem=recv, device_id=device, device_id_type=MESH
+    def tags_at(flip, zz):
+        return tags_ref.at[(dp ^ flip) * nz + zz]
+
+    def whole(flip, zz, own, send, recv, device):
+        return (
+            remote(x_ref if own else rows_at(flip, zz), rows_at(flip, zz), send(0), recv(0), device),
+            remote(t_ref if own else tags_at(flip, zz), tags_at(flip, zz), send(1), recv(1), device),
         )
 
     def z_copy(zz, step, own):
-        src = x_ref if own else at(0, zz)
-        return remote(src, at(0, zz), sz.at[(step + 1) // 2, zz], rz.at[zz], (dp, z + step))
+        return whole(
+            0, zz, own, lambda k: sz.at[k, (step + 1) // 2, zz], lambda k: rz.at[k, zz], (dp, z + step)
+        )
 
     def x_copy(zz, own):
-        return remote(x_ref if own else at(0, zz), at(0, zz), sx.at[zz], rx.at[zz], (dp ^ 2, z))
+        return whole(0, zz, own, lambda k: sx.at[k, zz], lambda k: rx.at[k, zz], (dp ^ 2, z))
 
     def y_copy(zz, own):
-        return remote(x_ref if own else at(0, zz), at(0, zz), sy.at[zz], ry.at[zz], (dp ^ 4, z))
+        return whole(0, zz, own, lambda k: sy.at[k, zz], lambda k: ry.at[k, zz], (dp ^ 4, z))
 
     def a_copy(zz):
-        ref = at(4, zz).at[pl.ds(0, half)]
-        return remote(ref, ref, sda.at[zz], rda.at[zz], (dp ^ 2, z))
+        ref = rows_at(4, zz).at[pl.ds(0, half)]
+        return (
+            remote(ref, ref, sda.at[0, zz], rda.at[0, zz], (dp ^ 2, z)),
+            remote(tags_at(4, zz), tags_at(4, zz), sda.at[1, zz], rda.at[1, zz], (dp ^ 2, z)),
+        )
 
     def b_copy(zz):
-        ref = at(2, zz).at[pl.ds(half, half)]
-        return remote(ref, ref, sdb.at[zz], rdb.at[zz], (dp ^ 4, z))
+        ref = rows_at(2, zz).at[pl.ds(half, half)]
+        return (remote(ref, ref, sdb.at[zz], rdb.at[zz], (dp ^ 4, z)),)
 
     def c_copy(kind, zz, own=False):
+        send, recv = (lambda k: sc.at[k, kind, zz]), (lambda k: rc.at[k, kind, zz])
         if kind < 3:
-            dst = at((0, 2, 4)[kind], zz)
-        else:
-            dst = at(6, zz).at[pl.ds((kind - 3) * half, half)]
-        return remote(x_ref if own else dst, dst, sc.at[kind, zz], rc.at[kind, zz], (dp ^ 1, z))
+            return whole((0, 2, 4)[kind], zz, own, send, recv, (dp ^ 1, z))
+        ref = rows_at(6, zz).at[pl.ds((kind - 3) * half, half)]
+        copies = (remote(ref, ref, send(0), recv(0), (dp ^ 1, z)),)
+        if kind == 3:
+            copies += (remote(tags_at(6, zz), tags_at(6, zz), send(1), recv(1), (dp ^ 1, z)),)
+        return copies
+
+    def start(copies):
+        for copy in copies:
+            copy.start()
 
     def arrived(ref, sem):
         remote(ref, ref, sem, sem, (dp ^ 1, z)).wait_recv()
+
+    def both_arrived(flip, zz, recv):
+        arrived(rows_at(flip, zz), recv(0))
+        arrived(tags_at(flip, zz), recv(1))
 
     def places(distance):
         for sign in (0,) if distance == 0 else (-1, 1):
@@ -135,47 +160,50 @@
             @pl.when((zz >= 0) & (zz < nz))
             def _():
                 if not own:
-                    arrived(at(0, zz), rz.at[zz])
+                    both_arrived(0, zz, lambda k: rz.at[k, zz])
                 if sign <= 0:
 
                     @pl.when(z < nz - 1)
                     def _():
-                        z_copy(zz, 1, own).start()
+                        start(z_copy(zz, 1, own))
 
                 if sign >= 0:
 
                     @pl.when(z > 0)
                     def _():
-                        z_copy(zz, -1, own).start()
-
-                x_copy(zz, own).start()
-                y_copy(zz, own).start()
-                c_copy(0, zz, own).start()
+                        start(z_copy(zz, -1, own))
+
+                start(x_copy(zz, own))
+                start(y_copy(zz, own))
+                start(c_copy(0, zz, own))
 
     def relay(distance):
         for _, zz in places(distance):
 
             @pl.when((zz >= 0) & (zz < nz))
             def _():
-                arrived(at(4, zz), ry.at[zz])
-                a_copy(zz).start()
-                c_copy(2, zz).start()
-                arrived(at(2, zz), rx.at[zz])
-                b_copy(zz).start()
-                c_copy(1, zz).start()
+                both_arrived(4, zz, lambda k: ry.at[k, zz])
+                start(a_copy(zz))
+                start(c_copy(2, zz))
+                both_arrived(2, zz, lambda k: rx.at[k, zz])
+                start(b_copy(zz))
+                start(c_copy(1, zz))
 
     def corner(distance):
         for _, zz in places(distance):
 
             @pl.when((zz >= 0) & (zz < nz))
             def _():
-                arrived(at(6, zz).at[pl.ds(0, half)], rda.at[zz])
-                c_copy(3, zz).start()
-                arrived(at(6, zz).at[pl.ds(half, half)], rdb.at[zz])
-                c_copy(4, zz).start()
-
-    keep = pltpu.make_async_copy(x_ref, at(0, z), local_sem)
+                arrived(rows_at(6, zz).at[pl.ds(0, half)], rda.at[0, zz])
+                arrived(tags_at(6, zz), rda.at[1, zz])
+                start(c_copy(3, zz))
+                arrived(rows_at(6, zz).at[pl.ds(half, half)], rdb.at[zz])
+                start(c_copy(4, zz))
+
+    keep = pltpu.make_async_copy(x_ref, rows_at(0, z), local_sem.at[0])
+    keep_tags = pltpu.make_async_copy(t_ref, tags_at(0, z), local_sem.at[1])
     keep.start()
+    keep_tags.start()
     for step in range(nz + 2):
         if step < nz:
             spread(step)
@@ -184,51 +212,340 @@
         if 0 <= step - 2 < nz:
             corner(step - 2)
     keep.wait()
+    keep_tags.wait()
+
+    def sent(copies):
+        for copy in copies:
+            copy.wait_send()
+
     for zz in range(nz):
 
         @pl.when((zz <= z) & (z < nz - 1))
         def _():
-            z_copy(zz, 1, False).wait_send()
+            sent(z_copy(zz, 1, False))
 
         @pl.when((zz >= z) & (z > 0))
         def _():
-            z_copy(zz, -1, False).wait_send()
-
-        x_copy(zz, False).wait_send()
-        y_copy(zz, False).wait_send()
-        a_copy(zz).wait_send()
-        b_copy(zz).wait_send()
+            sent(z_copy(zz, -1, False))
+
+        sent(x_copy(zz, False))
+        sent(y_copy(zz, False))
+        sent(a_copy(zz))
+        sent(b_copy(zz))
         for kind in range(5):
-            c_copy(kind, zz).wait_send()
+            sent(c_copy(kind, zz))
         for kind, flip in ((0, 1), (1, 3), (2, 5)):
-            arrived(at(flip, zz), rc.at[kind, zz])
+            both_arrived(flip, zz, lambda k: rc.at[k, kind, zz])
         for kind in (3, 4):
-            arrived(at(7, zz).at[pl.ds((kind - 3) * half, half)], rc.at[kind, zz])
-
-
-def gather_all(x, nz, collective_id):
+            arrived(rows_at(7, zz).at[pl.ds((kind - 3) * half, half)], rc.at[0, kind, zz])
+        arrived(tags_at(7, zz), rc.at[1, 3, zz])
+
+
+def gather_all(x, tags, nz, collective_id):
     rows, width = x.shape
     dma = pltpu.SemaphoreType.DMA
+    any_place, vmem = pl.BlockSpec(memory_space=pl.ANY), pl.BlockSpec(memory_space=pltpu.VMEM)
     return pl.pallas_call(
         functools.partial(gather_kernel, nz),
         name="gather_all",
-        out_shape=jax.ShapeDtypeStruct((8 * nz, rows, width), x.dtype),
-        in_specs=[pl.BlockSpec(memory_space=pltpu.VMEM)],
-        out_specs=pl.BlockSpec(memory_space=pl.ANY),
-        scratch_shapes=[dma(())]
-        + [dma((2, nz)), dma((nz,)), dma((nz,)), dma((nz,)), dma((nz,)), dma((5, nz))]
-        + [dma((nz,)), dma((nz,)), dma((nz,)), dma((nz,)), dma((nz,)), dma((5, nz))],
+        out_shape=(
+            jax.ShapeDtypeStruct((8 * nz, rows, width), x.dtype),
+            jax.ShapeDtypeStruct((8 * nz,) + tags.shape, tags.dtype),
+        ),
+        in_specs=[vmem, vmem],
+        out_specs=(any_place, any_place),
+        scratch_shapes=[dma((2,))]
+        + [dma((2, 2, nz)), dma((2, nz)), dma((2, nz)), dma((2, nz)), dma((nz,)), dma((2, 5, nz))]
+        + [dma((2, nz)), dma((2, nz)), dma((2, nz)), dma((2, nz)), dma((nz,)), dma((2, 5, nz))],
         compiler_params=pltpu.CompilerParams(
             collective_id=collective_id, has_side_effects=True, vmem_limit_bytes=8 * 2**20
         ),
-    )(x)
+    )(x, tags)
+
+
+def greet_line(dp, z, nz):
+    barrier = pltpu.get_barrier_semaphore()
+
+    @pl.when(z > 0)
+    def _():
+        pl.semaphore_signal(barrier, 1, device_id=(dp, z - 1), device_id_type=MESH)
+
+    @pl.when(z < nz - 1)
+    def _():
+        pl.semaphore_signal(barrier, 1, device_id=(dp, z + 1), device_id_type=MESH)
+
+    pl.semaphore_wait(barrier, jnp.where(z > 0, 1, 0) + jnp.where(z < nz - 1, 1, 0))
+
+
+PARTS = 2
+PIECES = 2
+
+
+def greet_total(dp, z, nz):
+    barrier = pltpu.get_barrier_semaphore()
+    for flip in (1, 2, 4):
+        pl.semaphore_signal(barrier, 1, device_id=(dp ^ flip, z), device_id_type=MESH)
+    for turn in range(1, nz):
+        pl.semaphore_signal(barrier, 1, device_id=(dp, lax.rem(z + turn, nz)), device_id_type=MESH)
+    pl.semaphore_wait(barrier, 2 + nz)
+
+
+class Total:
+    steps = 5
+
+    def __init__(self, nz, dp, z, got, s_plane, r_plane, s_line, r_line):
+        self.nz, self.z, self.got = nz, z, got
+        self.plane = [
+            remote(got.at[2 * k], got.at[2 * k + 1], s_plane.at[k], r_plane.at[k], (dp ^ flip, z))
+            for k, flip in enumerate((1, 2, 4))
+        ]
+        self.line = [
+            remote(got.at[6], got.at[6 + turn], s_line.at[turn - 1], r_line.at[turn - 1], (dp, lax.rem(z + turn, nz)))
+            for turn in range(1, nz)
+        ]
+
+    def step(self, k, out_ref):
+        got, nz = self.got, self.nz
+        if 1 <= k <= 3:
+            self.plane[k - 1].wait()
+            got[2 * k] = got[2 * k - 2] + got[2 * k - 1]
+        if k < 3:
+            self.plane[k].start()
+        elif k == 3:
+            for copy in self.line:
+                copy.start()
+        else:
+            for copy in self.line:
+                copy.wait()
+            total = got[6 + lax.rem(self.z, nz)]
+            for zz in range(1, nz):
+                total = total + got[6 + lax.rem(self.z - zz + nz, nz)]
+            out_ref[...] = total
+
+
+def total_scratch(nz, shape, dtype):
+    dma = pltpu.SemaphoreType.DMA
+    return [pltpu.VMEM((6 + nz,) + shape, dtype), dma((3,)), dma((3,)), dma((nz - 1,)), dma((nz - 1,))]
+
+
+def line_gather_kernel(nz, *refs):
+    dp, z = lax.axis_index("dp"), lax.axis_index("tensor")
+    summed = len(refs) > 6
+    if summed:
+        x_ref, small_ref, out_ref, total_ref, local_sem, s_up, s_down, r_line = refs[:8]
+        greet_total(dp, z, nz)
+        total = Total(nz, dp, z, *refs[8:])
+        total.got[0] = small_ref[...]
+    else:
+        x_ref, out_ref, local_sem, s_up, s_down, r_line = refs
+        greet_line(dp, z, nz)
+    part = x_ref.shape[0] // PARTS
+
+    def copy(zz, k, step, own):
+        at = pl.ds(k * part, part)
+        dst = out_ref.at[zz, at]
+        sems = s_up if step > 0 else s_down
+        return remote(x_ref.at[at] if own else dst, dst, sems.at[zz, k], r_line.at[zz, k], (dp, z + step))
+
+    keep = pltpu.make_async_copy(x_ref, out_ref.at[z], local_sem)
+    for distance in range(nz):
+        for k in range(PARTS):
+            for sign in (0,) if distance == 0 else (-1, 1):
+                zz, own = z + sign * distance, distance == 0
+
+                @pl.when((zz >= 0) & (zz < nz))
+                def _():
+                    if not own:
+                        copy(zz, k, 1, False).wait_recv()
+                    if sign <= 0:
+
+                        @pl.when(z < nz - 1)
+                        def _():
+                            copy(zz, k, 1, own).start()
+
+                    if sign >= 0:
+
+                        @pl.when(z > 0)
+                        def _():
+                            copy(zz, k, -1, own).start()
+
+        if distance == 0:
+            keep.start()
+        if summed:
+            total.step(distance, total_ref)
+    if summed:
+        for k in range(nz, Total.steps):
+            total.step(k, total_ref)
+    keep.wait()
+    for zz in range(nz):
+        for k in range(PARTS):
+
+            @pl.when((zz <= z) & (z < nz - 1))
+            def _():
+                copy(zz, k, 1, False).wait_send()
+
+            @pl.when((zz >= z) & (z > 0))
+            def _():
+                copy(zz, k, -1, False).wait_send()
+
+
+def line_gather(x, nz, collective_id, small=None):
+    dma, vmem = pltpu.SemaphoreType.DMA, pl.BlockSpec(memory_space=pltpu.VMEM)
+    blocks = jax.ShapeDtypeStruct((nz,) + x.shape, x.dtype)
+    scratch = [dma(())] + [dma((nz, PARTS)) for _ in range(3)]
+    params = pltpu.CompilerParams(
+        collective_id=collective_id, has_side_effects=True, vmem_limit_bytes=8 * 2**20
+    )
+    kernel = functools.partial(line_gather_kernel, nz)
+    if small is None:
+        return pl.pallas_call(
+            kernel,
+            name="line_gather",
+            out_shape=blocks,
+            in_specs=[vmem],
+            out_specs=pl.BlockSpec(memory_space=pl.ANY),
+            scratch_shapes=scratch,
+            compiler_params=params,
+        )(x)
+    return pl.pallas_call(
+        kernel,
+        name="line_gather_total",
+        out_shape=(blocks, jax.ShapeDtypeStruct(small.shape, small.dtype)),
+        in_specs=[vmem, vmem],
+        out_specs=(pl.BlockSpec(memory_space=pl.ANY), vmem),
+        scratch_shapes=scratch + total_scratch(nz, small.shape, small.dtype),
+        compiler_params=params,
+    )(x, small)
+
+
+CHUNK = 16
+
+
+def add_rows(dst, *others, start=0, count):
+    def body(k, carry):
+        at = pl.ds(start + k * CHUNK, CHUNK)
+        total = dst[at, :].astype(jnp.float32)
+        for ref, base in others:
+            total = total + ref[pl.ds(base + k * CHUNK, CHUNK), :].astype(jnp.float32)
+        dst[at, :] = total.astype(dst.dtype)
+        return carry
+
+    lax.fori_loop(0, count // CHUNK, body, 0)
+
+
+class Line:
+    def __init__(self, nz, dp, z, acc, up, down, s_up, r_up, s_down, r_down):
+        self.nz, self.dp, self.z, self.acc, self.up, self.down = nz, dp, z, acc, up, down
+        self.sems = s_up, r_up, s_down, r_down
+        self.part = acc.shape[1] // PARTS
+
+    def copy(self, zz, k, step):
+        at = pl.ds(k * self.part, self.part)
+        s_up, r_up, s_down, r_down = self.sems
+        if step > 0:
+            return remote(self.acc.at[zz, at], self.up.at[zz, at], s_up.at[zz, k], r_up.at[zz, k], (self.dp, self.z + 1))
+        return remote(self.acc.at[zz, at], self.down.at[zz, at], s_down.at[zz, k], r_down.at[zz, k], (self.dp, self.z - 1))
+
+    def first(self):
+        nz, z = self.nz, self.z
+
+        @pl.when(z == 0)
+        def _():
+            for zz in range(nz - 1, 0, -1):
+                for k in range(PARTS):
+                    self.copy(zz, k, 1).start()
+
+        @pl.when(z == nz - 1)
+        def _():
+            for zz in range(nz - 1):
+                for k in range(PARTS):
+                    self.copy(zz, k, -1).start()
+
+    def step(self, distance):
+        nz, z = self.nz, self.z
+        for k in range(PARTS):
+            for sign in (1, -1):
+                far = nz - distance if sign > 0 else distance - 1
+                through = (far > z) & (z > 0) if sign > 0 else (far < z) & (z < nz - 1)
+
+                @pl.when(through)
+                def _():
+                    self.copy(far, k, sign).wait_recv()
+                    source = self.up if sign > 0 else self.down
+                    add_rows(self.acc.at[far], (source.at[far], k * self.part), start=k * self.part, count=self.part)
+                    self.copy(far, k, sign).start()
+
+    def finish(self, out_ref):
+        nz, z = self.nz, self.z
+        for k in range(PARTS):
+
+            @pl.when(z > 0)
+            def _():
+                self.copy(z, k, 1).wait_recv()
+
+            @pl.when(z < nz - 1)
+            def _():
+                self.copy(z, k, -1).wait_recv()
+
+        def body(k, carry):
+            at = pl.ds(k * CHUNK, CHUNK)
+            total = self.acc[z, at, :].astype(jnp.float32)
+            zero = jnp.zeros_like(total)
+            total = total + jnp.where(z > 0, self.up[z, at, :].astype(jnp.float32), zero)
+            total = total + jnp.where(z < nz - 1, self.down[z, at, :].astype(jnp.float32), zero)
+            out_ref[at, :] = total
+            return carry
+
+        lax.fori_loop(0, out_ref.shape[0] // CHUNK, body, 0)
+
+    def drain(self):
+        nz, z = self.nz, self.z
+        for zz in range(nz):
+            for k in range(PARTS):
+
+                @pl.when(zz > z)
+                def _():
+                    self.copy(zz, k, 1).wait_send()
+
+                @pl.when(zz < z)
+                def _():
+                    self.copy(zz, k, -1).wait_send()
+
+
+def line_scatter_kernel(nz, p_ref, out_ref, acc, up, down, local_sem, s_up, r_up, s_down, r_down):
+    dp, z = lax.axis_index("dp"), lax.axis_index("tensor")
+    loaded = pltpu.make_async_copy(p_ref, acc, local_sem)
+    loaded.start()
+    greet_line(dp, z, nz)
+    loaded.wait()
+    line = Line(nz, dp, z, acc, up, down, s_up, r_up, s_down, r_down)
+    line.first()
+    for distance in range(1, nz - 1):
+        line.step(distance)
+    line.finish(out_ref)
+    line.drain()
+
+
+def line_scatter(p, nz, collective_id):
+    _, rows, width = p.shape
+    dma, vmem = pltpu.SemaphoreType.DMA, functools.partial(pltpu.VMEM, dtype=p.dtype)
+    return pl.pallas_call(
+        functools.partial(line_scatter_kernel, nz),
+        name="line_scatter",
+        out_shape=jax.ShapeDtypeStruct((rows, width), jnp.float32),
+        in_specs=[pl.BlockSpec(memory_space=pl.ANY)],
+        out_specs=pl.BlockSpec(memory_space=pltpu.VMEM),
+        scratch_shapes=[vmem((nz, rows, width)) for _ in range(3)]
+        + [dma(())]
+        + [dma((nz, PARTS)) for _ in range(4)],
+        compiler_params=pltpu.CompilerParams(
+            collective_id=collective_id, has_side_effects=True, vmem_limit_bytes=16 * 2**20
+        ),
+    )(p)
 
 
 def z_order(nz):
     return [sorted(range(nz), key=lambda zz: (-abs(zz - z), zz if z >= nz // 2 else -zz)) for z in range(nz)]
-
-
-CHUNK = 16
 
 
 def scatter_kernel(nz, p_ref, out_ref, acc, rc, ra, rb, rx, ry, ru, rd, s_local, s_core, r_core, s_a, r_a, s_b, r_b, s_x, r_x, s_y, r_y, s_u, r_u, s_d, r_d):
@@ -243,11 +560,6 @@
             zz = jnp.where(z == zv, order[zv][i], zz)
         return zz
 
-    def remote(src, dst, send, recv, device):
-        return pltpu.make_async_remote_copy(
-            src_ref=src, dst_ref=dst, send_sem=send, recv_sem=recv, device_id=device, device_id_type=MESH
-        )
-
     flips = (0, 2, 4, 6)
 
     def load(kind, zz):
@@ -279,15 +591,7 @@
         return remote(acc.at[0, zz], rd.at[zz], s_d.at[zz], r_d.at[zz], (dp, z - 1))
 
     def add(dst, *others, start=0, count=rows):
-        def body(k, carry):
-            at = pl.ds(start + k * CHUNK, CHUNK)
-            total = dst[at, :].astype(jnp.float32)
-            for ref, base in others:
-                total = total + ref[pl.ds(base + k * CHUNK, CHUNK), :].astype(jnp.float32)
-            dst[at, :] = total.astype(dst.dtype)
-            return carry
-
-        lax.fori_loop(0, count // CHUNK, body, 0)
+        add_rows(dst, *others, start=start, count=count)
 
     def wave(i):
         zz = place(i)
@@ -417,6 +721,205 @@
             collective_id=collective_id, has_side_effects=True, vmem_limit_bytes=VMEM_LIMIT
         ),
     )(p)
+
+
+def finish_kernel(nz, nc, g_ref, p_ref, unit_ref, small_ref, sum_q, sum_k, sum_v, out_ref, total_ref, buf, acc, rc, ra, rb, rx, ry, line_acc, up, down, *sems):
+    (s_load, s_core, r_core, s_a, r_a, s_b, r_b, s_x, r_x, s_y, r_y) = sems[:11]
+    (t_x, q_x, t_y, q_y, t_a, q_a, t_b, q_b, t_c, q_c) = sems[11:21]
+    s_line, s_store, s_up, r_up, s_down, r_down = sems[21:27]
+    total = Total(nz, lax.axis_index("dp"), lax.axis_index("tensor"), *sems[27:])
+    dp, z = lax.axis_index("dp"), lax.axis_index("tensor")
+    rows = acc.shape[2]
+    half = rows // 2
+    flips = (0, 2, 4, 6)
+
+    def load(kind, c):
+        return pltpu.make_async_copy(g_ref.at[(dp ^ flips[kind]) * nc + c], acc.at[kind, c], s_load.at[kind, c])
+
+    def core_copy(kind, c):
+        return remote(
+            g_ref.at[(dp ^ flips[kind] ^ 1) * nc + c], rc.at[kind, c], s_core.at[kind, c], r_core.at[kind, c], (dp ^ 1, z)
+        )
+
+    def a_copy(c):
+        return remote(acc.at[3, c, pl.ds(0, half)], ra.at[c], s_a.at[c], r_a.at[c], (dp ^ 2, z))
+
+    def b_copy(c):
+        return remote(acc.at[3, c, pl.ds(half, half)], rb.at[c], s_b.at[c], r_b.at[c], (dp ^ 4, z))
+
+    def x_copy(c):
+        return remote(acc.at[1, c], rx.at[c], s_x.at[c], r_x.at[c], (dp ^ 2, z))
+
+    def y_copy(c):
+        return remote(acc.at[2, c], ry.at[c], s_y.at[c], r_y.at[c], (dp ^ 4, z))
+
+    def full(flip, c):
+        return buf.at[(dp ^ flip) * nc + c]
+
+    def back_x(c):
+        return remote(full(0, c), full(0, c), t_x.at[c], q_x.at[c], (dp ^ 2, z))
+
+    def back_y(c):
+        return remote(full(0, c), full(0, c), t_y.at[c], q_y.at[c], (dp ^ 4, z))
+
+    def back_a(c):
+        ref = full(4, c).at[pl.ds(0, half)]
+        return remote(ref, ref, t_a.at[c], q_a.at[c], (dp ^ 2, z))
+
+    def back_b(c):
+        ref = full(2, c).at[pl.ds(half, half)]
+        return remote(ref, ref, t_b.at[c], q_b.at[c], (dp ^ 4, z))
+
+    def back_core(kind, c):
+        ref = full((0, 2, 4, 6, 6)[kind], c)
+        if kind >= 3:
+            ref = ref.at[pl.ds((kind - 3) * half, half)]
+        return remote(ref, ref, t_c.at[kind, c], q_c.at[kind, c], (dp ^ 1, z))
+
+    def arrived(ref, sem):
+        remote(ref, ref, sem, sem, (dp ^ 1, z)).wait_recv()
+
+    def paired(kind, c):
+        load(kind, c).wait()
+        core_copy(kind, c).wait_recv()
+
+    def stage_diagonal(c):
+        paired(3, c)
+        add_rows(acc.at[3, c], (rc.at[3, c], 0), count=rows)
+        a_copy(c).start()
+        b_copy(c).start()
+
+    def stage_side(c):
+        paired(1, c)
+        paired(2, c)
+        a_copy(c).wait_recv()
+        add_rows(acc.at[2, c], (rc.at[2, c], 0), (ra.at[c], 0), start=0, count=half)
+        add_rows(acc.at[2, c], (rc.at[2, c], half), start=half, count=half)
+        y_copy(c).start()
+        b_copy(c).wait_recv()
+        add_rows(acc.at[1, c], (rc.at[1, c], half), (rb.at[c], 0), start=half, count=half)
+        add_rows(acc.at[1, c], (rc.at[1, c], 0), start=0, count=half)
+        x_copy(c).start()
+
+    def stage_own(c):
+        paired(0, c)
+        x_copy(c).wait_recv()
+        y_copy(c).wait_recv()
+        dst = full(0, c)
+
+        def body(k, carry):
+            at = pl.ds(k * CHUNK, CHUNK)
+            total = acc[0, c, at, :].astype(jnp.float32) + rc[0, c, at, :].astype(jnp.float32)
+            total = total + rx[c, at, :].astype(jnp.float32) + ry[c, at, :].astype(jnp.float32)
+            dst[at, :] = total.astype(dst.dtype)
+            return carry
+
+        lax.fori_loop(0, rows // CHUNK, body, 0)
+        back_x(c).start()
+        back_y(c).start()
+        back_core(0, c).start()
+
+    def stage_relay(c):
+        arrived(full(4, c), q_y.at[c])
+        back_a(c).start()
+        back_core(2, c).start()
+        arrived(full(2, c), q_x.at[c])
+        back_b(c).start()
+        back_core(1, c).start()
+
+    def stage_corner(c):
+        arrived(full(6, c).at[pl.ds(0, half)], q_a.at[c])
+        back_core(3, c).start()
+        arrived(full(6, c).at[pl.ds(half, half)], q_b.at[c])
+        back_core(4, c).start()
+
+    line_load = pltpu.make_async_copy(p_ref, line_acc, s_line)
+    line_load.start()
+    for c in range(nc):
+        for kind in (3, 1, 2, 0):
+            load(kind, c).start()
+    greet_total(dp, z, nz)
+    for c in range(nc):
+        for kind in (3, 1, 2, 0):
+            core_copy(kind, c).start()
+    line = Line(nz, dp, z, line_acc, up, down, s_up, r_up, s_down, r_down)
+    line_load.wait()
+    line.first()
+    def line_end():
+        line.finish(out_ref)
+        line.drain()
+        share = jnp.sum(out_ref[...] * unit_ref[...], axis=0, keepdims=True)
+        total.got[0] = small_ref[...]
+        wide = small_ref.shape[1]
+        for k in range(out_ref.shape[1] // wide):
+            total.got[0, k : k + 1, :] = share[:, k * wide : (k + 1) * wide]
+
+    side = [functools.partial(line.step, distance) for distance in range(1, nz - 1)] + [line_end]
+    side += [functools.partial(total.step, k, total_ref) for k in range(Total.steps)]
+    stages = (stage_diagonal, stage_side, stage_own, stage_relay, stage_corner)
+    for i in range(nc + len(stages) - 1):
+        for lag, stage in enumerate(stages):
+            if 0 <= i - lag < nc:
+                stage(i - lag)
+                if i >= 1 and side:
+                    side.pop(0)()
+    for one in side:
+        one()
+    for c in range(nc):
+        for kind, flip in ((0, 1), (1, 3), (2, 5)):
+            arrived(full(flip, c), q_c.at[kind, c])
+        for kind in (3, 4):
+            arrived(full(7, c).at[pl.ds((kind - 3) * half, half)], q_c.at[kind, c])
+    wide = buf.shape[2] // 3
+    stores = [
+        pltpu.make_async_copy(buf.at[:, :, pl.ds(k * wide, wide)], ref, s_store.at[k])
+        for k, ref in enumerate((sum_q, sum_k, sum_v))
+    ]
+    for store in stores:
+        store.start()
+    for c in range(nc):
+        for kind in range(4):
+            core_copy(kind, c).wait_send()
+        for copy in (a_copy, b_copy, x_copy, y_copy, back_x, back_y, back_a, back_b):
+            copy(c).wait_send()
+        for kind in range(5):
+            back_core(kind, c).wait_send()
+    for store in stores:
+        store.wait()
+
+
+def finish_sums(g, p, unit, small, nz, nc, collective_id):
+    _, rows, width = g.shape
+    _, line_rows, line_width = p.shape
+    half = rows // 2
+    dma, vmem = pltpu.SemaphoreType.DMA, functools.partial(pltpu.VMEM, dtype=g.dtype)
+    return pl.pallas_call(
+        functools.partial(finish_kernel, nz, nc),
+        name="finish_sums",
+        out_shape=(
+            *[jax.ShapeDtypeStruct(g.shape[:2] + (width // 3,), g.dtype)] * 3,
+            jax.ShapeDtypeStruct((line_rows, line_width), jnp.float32),
+            jax.ShapeDtypeStruct(small.shape, small.dtype),
+        ),
+        in_specs=[pl.BlockSpec(memory_space=pl.ANY)] * 2 + [pl.BlockSpec(memory_space=pltpu.VMEM)] * 2,
+        out_specs=(
+            *[pl.BlockSpec(memory_space=pl.ANY)] * 3,
+            *[pl.BlockSpec(memory_space=pltpu.VMEM)] * 2,
+        ),
+        scratch_shapes=[vmem(g.shape), vmem((4, nc, rows, width)), vmem((4, nc, rows, width))]
+        + [vmem((nc, half, width)) for _ in range(2)]
+        + [vmem((nc, rows, width)) for _ in range(2)]
+        + [vmem((nz, line_rows, line_width)) for _ in range(3)]
+        + [dma((4, nc)) for _ in range(3)]
+        + [dma((nc,)) for _ in range(16)]
+        + [dma((5, nc)), dma((5, nc))]
+        + [dma(()), dma((3,))]
+        + [dma((nz, PARTS)) for _ in range(4)]
+        + total_scratch(nz, small.shape, small.dtype),
+        compiler_params=pltpu.CompilerParams(
+            collective_id=collective_id, has_side_effects=True, vmem_limit_bytes=VMEM_LIMIT
+        ),
+    )(g, p, unit, small)
 
 
 def experts_routed(
@@ -567,6 +1070,7 @@
     w_up,
     w_down,
     grad_output,
+    all_cotangents,
 ):
     tok_count, d_model = hidden_after_attention.shape
     n_tensor = lax.axis_size("tensor")
@@ -582,23 +1086,18 @@
     expert_at = jnp.arange(experts, dtype=jnp.int32)
     local_at = lax.axis_index("dp") * exp_dev + jnp.arange(exp_dev, dtype=jnp.int32)
 
-    all_rows = gather_all(second_normalized, n_tensor, 0).reshape(all_count, d_model)
-    all_cotangents = lax.all_gather(grad_output, everyone, axis=0, tiled=True)
-    all_ids = lax.all_gather(expert_ids, everyone, axis=0, tiled=True)
-
-    def route(rows):
-        return jax.nn.softmax(
-            jnp.dot(rows, w_router, preferred_element_type=jnp.float32), axis=-1
-        )
+    chosen = jnp.any(expert_ids[:, :, None] == expert_at[None, None, :], axis=1)
+    route_probs = jax.nn.softmax(
+        jnp.dot(second_normalized, w_router, preferred_element_type=jnp.float32), axis=-1
+    )
+    gates = jnp.where(chosen, route_probs, 0.0).T
+    all_rows, all_gates = gather_all(second_normalized, gates, n_tensor, 0)
+    all_rows = all_rows.reshape(all_count, d_model)
 
     down_rows = w_down.reshape(exp_dev * width, d_model)
     wide = jnp.concatenate([w_gate[e] for e in range(exp_dev)] + [w_up[e] for e in range(exp_dev)], axis=1)
-    all_route = route(all_rows)
-    named = jnp.any(all_ids[:, :, None] == local_at[None, None, :], axis=1)
-    local_route = jnp.sum(
-        jnp.where(local_at[None, :, None] == expert_at[None, None, :], all_route[:, None, :], 0.0), axis=-1
-    )
-    local_gate = jnp.where(named, local_route, 0.0)
+    local_gate = lax.dynamic_slice_in_dim(all_gates, lax.axis_index("dp") * exp_dev, exp_dev, axis=1)
+    local_gate = local_gate.transpose(0, 2, 1).reshape(all_count, exp_dev)
     spread = jnp.repeat(local_gate, width, axis=1)
     both = exp_dev * width
     pre = jnp.dot(all_rows, wide, preferred_element_type=jnp.float32)
@@ -628,16 +1127,17 @@
 
     route_grads = jnp.sum(
         jnp.where(
-            (named[:, :, None]) & (local_at[None, :, None] == expert_at[None, None, :]),
+            local_at[None, :, None] == expert_at[None, None, :],
             gate_grads[:, :, None],
             0.0,
         ),
         axis=1,
     )
-    grad_route = lax.psum_scatter(route_grads, everyone, scatter_dimension=0, tiled=True)
+    grad_route = jnp.where(
+        chosen, lax.psum_scatter(route_grads, everyone, scatter_dimension=0, tiled=True), 0.0
+    )
     cotangent = grad_output.astype(jnp.float32)
     result = (hidden_after_attention + moe_out).astype(jnp.bfloat16)
-    route_probs = route(second_normalized)
     grad_logits = (
         route_probs * (grad_route - jnp.sum(route_probs * grad_route, axis=-1, keepdims=True))
     ).astype(jnp.bfloat16)
@@ -669,7 +1169,211 @@
     )
 
 
-def local(
+def local_gathered(
+    tokens,
+    file_ids,
+    expert_ids,
+    attention_norm_gain,
+    w_query,
+    w_key,
+    w_value,
+    query_gain,
+    key_gain,
+    w_output,
+    expert_norm_gain,
+    w_router,
+    w_gate,
+    w_up,
+    w_down,
+    grad_output,
+):
+    tok_count, d_model = tokens.shape
+    n_tensor = lax.axis_size("tensor")
+    n_dp = lax.axis_size("dp")
+    devices = n_dp * n_tensor
+    local_dim = w_query.shape[1]
+    head_dim = HEAD_DIM
+    local_heads = local_dim // head_dim
+    seq_len = tok_count * n_tensor
+    block_rows = min(512, seq_len)
+    score_scale = 1.0 / math.sqrt(head_dim)
+    file_row = file_ids[0]
+    cosine, sine_table = rope_tables(seq_len, head_dim)
+    input_tensors = tokens.astype(jnp.float32)
+    first_norm_scale = root_mean_square_scale(input_tensors)
+    first_unit_rows = input_tensors * first_norm_scale
+    first_normalized = (first_unit_rows * attention_norm_gain).astype(jnp.bfloat16)
+    normed_all = line_gather(first_normalized, n_tensor, 2).reshape(seq_len, d_model)
+    normed_all, later_cotangent = lax.optimization_barrier((normed_all, grad_output))
+    all_cotangents = lax.all_gather(later_cotangent, ("dp", "tensor"), axis=0, tiled=True)
+    query_raw = jnp.dot(normed_all, w_query, preferred_element_type=jnp.float32)
+    key_raw = jnp.dot(normed_all, w_key, preferred_element_type=jnp.float32)
+    value_rows = (
+        jnp.dot(normed_all, w_value, preferred_element_type=jnp.float32)
+        .astype(jnp.bfloat16)
+        .reshape(seq_len, local_heads, head_dim)
+    )
+    query_total, key_total = lax.psum(
+        (jnp.sum(query_raw * query_raw, axis=1), jnp.sum(key_raw * key_raw, axis=1)), "tensor"
+    )
+    query_scale = lax.rsqrt(query_total / d_model + EPSILON)[:, None]
+    key_scale = lax.rsqrt(key_total / d_model + EPSILON)[:, None]
+    query_hat = query_raw * query_scale
+    key_hat = key_raw * key_scale
+    queries = rotate(
+        (query_hat * query_gain).reshape(seq_len, local_heads, head_dim), cosine, sine_table
+    ).astype(jnp.bfloat16)
+    key_rows = rotate(
+        (key_hat * key_gain).reshape(seq_len, local_heads, head_dim), cosine, sine_table
+    ).astype(jnp.bfloat16)
+    block_start = 0
+    scores = block_scores(queries, key_rows, file_row, block_start, score_scale)
+    row_peak = jnp.max(scores, axis=-1, keepdims=True)
+    log_total = row_peak + jnp.log(jnp.sum(jnp.exp(scores - row_peak), axis=-1, keepdims=True))
+    attn_probs = jnp.exp(scores - log_total).astype(jnp.bfloat16)
+    context_blocks = jnp.einsum(
+        "hqk,khd->qhd", attn_probs, value_rows, preferred_element_type=jnp.float32
+    )
+    log_totals = [log_total]
+    context = context_blocks.reshape(seq_len, local_dim).astype(jnp.bfloat16)
+    attn_out = line_scatter(
+        jnp.dot(context, w_output, preferred_element_type=jnp.float32)
+        .astype(jnp.bfloat16)
+        .reshape(n_tensor, tok_count, d_model),
+        n_tensor,
+        3,
+    )
+    hidden_after_attention = input_tensors + attn_out
+    result, grad_hidden_one, grad_expert_share, grad_router_part, grad_gate, grad_up, grad_down = (
+        experts_dense(
+            hidden_after_attention,
+            expert_ids,
+            expert_norm_gain,
+            w_router,
+            w_gate,
+            w_up,
+            w_down,
+            grad_output,
+            all_cotangents,
+        )
+    )
+    grad_attn = grad_hidden_one.astype(jnp.bfloat16)
+    side_parts = jnp.concatenate([grad_router_part.T, grad_expert_share[None, :]])
+    grad_attn_all, side_total = line_gather(grad_attn, n_tensor, 5, side_parts)
+    grad_attn_all = grad_attn_all.reshape(seq_len, d_model)
+    total_router, total_ffn_gain = side_total[:-1].T, side_total[-1]
+    grad_output_part = jnp.einsum(
+        "sd,se->de", context, grad_attn_all, preferred_element_type=jnp.float32
+    )
+    grad_context = (
+        jnp.einsum("se,de->sd", grad_attn_all, w_output, preferred_element_type=jnp.float32)
+        .astype(jnp.bfloat16)
+        .reshape(seq_len, local_heads, head_dim)
+    )
+    grad_query_blocks = []
+    grad_key_total = jnp.zeros((seq_len, local_heads, head_dim), jnp.float32)
+    grad_value_total = jnp.zeros((seq_len, local_heads, head_dim), jnp.float32)
+    for block_index, block_start in enumerate(range(0, seq_len, block_rows)):
+        scores = block_scores(queries, key_rows, file_row, block_start, score_scale)
+        probs_full = jnp.exp(scores - log_totals[block_index])
+        probs_low = probs_full.astype(jnp.bfloat16)
+        grad_value_total = jnp.einsum(
+            "hqk,qhd->khd", probs_low, grad_context, preferred_element_type=jnp.float32
+        )
+        grad_probs = jnp.einsum(
+            "qhd,khd->hqk", grad_context, value_rows, preferred_element_type=jnp.float32
+        )
+        row_shift = jnp.sum(probs_full * grad_probs, axis=-1, keepdims=True)
+        grad_scores = (probs_full * (grad_probs - row_shift)).astype(jnp.bfloat16)
+        grad_query_blocks.append(
+            jnp.einsum("hqk,khd->qhd", grad_scores, key_rows, preferred_element_type=jnp.float32)
+            * score_scale
+        )
+        grad_key_total = (
+            jnp.einsum("hqk,qhd->khd", grad_scores, queries, preferred_element_type=jnp.float32)
+            * score_scale
+        )
+    grad_query_normed = unrotate(grad_query_blocks[0], cosine, sine_table).reshape(
+        seq_len, local_dim
+    )
+    grad_key_normed = unrotate(grad_key_total, cosine, sine_table).reshape(seq_len, local_dim)
+    grad_qgain_part = jnp.sum(grad_query_normed * query_hat, axis=0)
+    grad_kgain_part = jnp.sum(grad_key_normed * key_hat, axis=0)
+    grad_query_hat = grad_query_normed * query_gain
+    grad_key_hat = grad_key_normed * key_gain
+    query_inner, key_inner = lax.psum(
+        (jnp.sum(grad_query_hat * query_hat, axis=1), jnp.sum(grad_key_hat * key_hat, axis=1)),
+        "tensor",
+    )
+    grad_query_raw = (
+        query_scale * (grad_query_hat - query_hat * (query_inner / d_model)[:, None])
+    ).astype(jnp.bfloat16)
+    grad_key_raw = (key_scale * (grad_key_hat - key_hat * (key_inner / d_model)[:, None])).astype(
+        jnp.bfloat16
+    )
+    grad_value_raw = grad_value_total.reshape(seq_len, local_dim).astype(jnp.bfloat16)
+    grad_raw = jnp.concatenate([grad_query_raw, grad_key_raw, grad_value_raw], axis=1)
+    w_raw = jnp.concatenate([w_query, w_key, w_value], axis=1)
+    raw_part = jnp.einsum("sd,sf->df", normed_all, grad_raw, preferred_element_type=jnp.float32)
+    row_part = jnp.einsum("sf,df->sd", grad_raw, w_raw, preferred_element_type=jnp.float32)
+    mine = (jnp.arange(n_tensor) == lax.axis_index("tensor"))[:, None]
+    gain_parts = jnp.stack(
+        [
+            jnp.zeros((d_model,), jnp.float32),
+            jnp.where(mine, grad_qgain_part[None, :], 0.0).reshape(-1),
+            jnp.where(mine, grad_kgain_part[None, :], 0.0).reshape(-1),
+            jnp.zeros((d_model,), jnp.float32),
+        ]
+    )
+    total_query, total_key, total_value, grad_first_normalized, gain_totals = finish_sums(
+        raw_part.astype(jnp.bfloat16).reshape(n_dp * PIECES, -1, 3 * local_dim),
+        row_part.astype(jnp.bfloat16).reshape(n_tensor, tok_count, d_model),
+        first_unit_rows,
+        gain_parts.reshape(8, -1),
+        n_tensor,
+        PIECES,
+        4,
+    )
+    total_query, total_key, total_value = (
+        total.reshape(d_model, local_dim).astype(jnp.float32)
+        for total in (total_query, total_key, total_value)
+    )
+    grad_first_unit_rows = grad_first_normalized * attention_norm_gain
+    grad_tokens = (
+        first_norm_scale
+        * (
+            grad_first_unit_rows
+            - first_unit_rows
+            * jnp.mean(grad_first_unit_rows * first_unit_rows, axis=-1, keepdims=True)
+        )
+        + grad_hidden_one
+    ).astype(jnp.bfloat16)
+    total_output = lax.psum(grad_output_part.astype(jnp.bfloat16), "dp").astype(jnp.float32)
+    gain_totals = gain_totals.reshape(4, d_model)
+    total_attn_gain = gain_totals[0]
+    own_gains = lax.dynamic_slice_in_dim(
+        gain_totals, lax.axis_index("tensor") * local_dim, local_dim, axis=1
+    )
+    total_qgain, total_kgain = own_gains[1], own_gains[2]
+    return (
+        result,
+        grad_tokens,
+        total_query,
+        total_key,
+        total_value,
+        total_output,
+        total_qgain,
+        total_kgain,
+        total_attn_gain,
+        total_ffn_gain,
+        total_router,
+        grad_gate,
+        grad_up,
+        grad_down,
+    )
+
+
+def local_routed(
     tokens,
     file_ids,
     expert_ids,
@@ -741,18 +1445,17 @@
         tiled=True,
     ).astype(jnp.float32)
     hidden_after_attention = input_tensors + attn_out
-    dense = n_dp == 8 and n_dp <= expert_ids.shape[1]
     result, grad_hidden_one, grad_expert_share, grad_router_part, grad_gate, grad_up, grad_down = (
-        experts_dense if dense else experts_routed
-    )(
-        hidden_after_attention,
-        expert_ids,
-        expert_norm_gain,
-        w_router,
-        w_gate,
-        w_up,
-        w_down,
-        grad_output,
+        experts_routed(
+            hidden_after_attention,
+            expert_ids,
+            expert_norm_gain,
+            w_router,
+            w_gate,
+            w_up,
+            w_down,
+            grad_output,
+        )
     )
     grad_attn = grad_hidden_one.astype(jnp.bfloat16)
     grad_attn_all = lax.all_gather(grad_attn, "tensor", axis=0, tiled=True)
@@ -870,7 +1573,7 @@
 
 def solution(mesh):
     return jax.shard_map(
-        local,
+        local_gathered if mesh.shape["dp"] == 8 else local_routed,
         mesh=mesh,
         in_specs=(
             P(("dp", "tensor"), None),

time: 944 us -> 854 us (0.905)
  Pallas kernels: 288 us -> 517 us
  waiting for transfers between devices: 231 us -> 47.6 us
  blocking collectives: 142 us -> 24.1 us
  other arithmetic: 73.4 us -> 49.2 us
    pallas_call x0 -> x4, Pallas kernels: none -> 228 us  [the longest x1 78.2 us: finish_sums(): pl.pallas_call(functools.partial(finish_kernel, nz, nc), name='finish_sum...]
    psum x2 -> x1, waiting for transfers between devices: 164 us -> 47.6 us  [local_gathered(): lax.psum(grad_output_part.astype(jnp.bfloat16), 'dp').astype(jnp.float32)]
    all_gather x1 -> x0, blocking collectives: 68.3 us -> none  [experts_dense(): all_ids = lax.all_gather(expert_ids, everyone, axis=0, tiled=True)]
    all_gather x3 -> x1, waiting for transfers between devices: 66.5 us -> 0.01 us  [local_gathered(): lax.all_gather(later_cotangent, ('dp', 'tensor'), axis=0, tiled=True)]
    psum x4 -> x2, blocking collectives: 73.7 us -> 24.1 us  [the longest x1 12.9 us: local_gathered(): lax.psum((jnp.sum(grad_query_hat * query_hat, axis=1), jnp.sum(grad_key_h...]
    convert_element_type x14 -> x10, other arithmetic: 50.3 us -> 21.2 us  [the longest x3 9.82 us: local_gathered(): total.reshape(d_model, local_dim).astype(jnp.float32)]
    reduce_sum x7, other arithmetic: 4.1 us -> 13.8 us  [the longest x1 9.74 us: experts_dense(): jnp.sum((hidden * back).reshape(all_count, exp_dev, width), axis=-1)]
    dot_general x19 -> x14, matrix products: 41.3 us -> 35.3 us  [the longest x1 6.54 us: local_gathered(): jnp.einsum('sf,df->sd', grad_raw, w_raw, preferred_element_type=jnp.float32)]
  transfers between devices with their start and end apart: 8 -> 3, of which waited for: 4 -> 1; matrix products, arithmetic and copies ran while one was open for 19% -> 11% of each run, Pallas kernels for 31% -> 41%
where the time goes in v2:
time: 854 us; the launch traced here: 845 us
  Pallas kernels  517 us (61%)
  matrix products  164 us (19%)
  other arithmetic  49.2 us (6%)
  waiting for transfers between devices  47.6 us (6%)
  local copies, waits for them, and re-layouts  27.4 us (3%)
  blocking collectives  24.1 us (3%)
  between operations  15.3 us (2%)
    pallas_call x2, Pallas kernels, scatter_all(): pl.pallas_call(functools.partial(scatter_kernel, nz), name='scatter_all',...  180 us
    pallas_call x1, Pallas kernels, gather_all(): pl.pallas_call(functools.partial(gather_kernel, nz), name='gather_all', o...  109 us
    pallas_call x1, Pallas kernels, finish_sums(): pl.pallas_call(functools.partial(finish_kernel, nz, nc), name='finish_sum...  78.2 us
    pallas_call x1, Pallas kernels, line_gather(): pl.pallas_call(kernel, name='line_gather_total', out_shape=(blocks, jax.S...  56.6 us
    pallas_call x1, Pallas kernels, line_scatter(): pl.pallas_call(functools.partial(line_scatter_kernel, nz), name='line_sca...  54.2 us
    psum x1, waiting for transfers between devices, local_gathered(): lax.psum(grad_output_part.astype(jnp.bfloat16), 'dp').astype(jnp.float32)  47.6 us
    pallas_call x1, Pallas kernels, line_gather(): pl.pallas_call(kernel, name='line_gather', out_shape=blocks, in_specs=[vm...  39 us
    dot_general x1, matrix products, experts_dense(): jnp.einsum('td,tf->df', all_rows, grad_pre, preferred_element_type=jnp.fl...  24.7 us
  transfers between devices with their start and end apart: 3, of which 1 were waited for; matrix products, arithmetic and copies ran while one was open for 11% of the time, Pallas kernels for 41%

profile of v2, /device:TPU:0, one launch (start us, length us, event | category | flops | bytes accessed | tf_op | source)
XLA Modules:
  0.0 844.9 jit_solution(12123289604263356009)
XLA Ops:
  7.2 1.4 fusion.15
  8.6 2.2 convert_multiply_fusion
  10.9 39.0 %line_gather.1 = bf16[4,128,2048]{2,1,0:T(8,128)(2,1)S(1)} custom-call(bf16[128,2048]{1,0:T(8,128)(2,1)S(1)} %get-tuple-element.70.refs_0_), custom_call_target="tpu_custom_call" | custom-call | tf_op jit(solution)/shard_map/line_gather/pallas_call | solution.py:401
  49.8 1.3 copy-done.3
  51.3 4.6 multiply_reduce_fusion.7
  55.9 1.3 multiply_reduce_fusion.8
  57.3 11.2 %all-reduce.1 = (f32[512]{0:T(512)S(1)}, f32[512]{0:T(512)S(1)}) all-reduce(f32[512]{0:T(512)S(1)} %get-tuple-element.87, f32[512]{0:T(512)S(1)} %get-tuple-element.89), channel_id=1, replica_groups=mesh['dp'=8,'tensor'=4] {'tensor'}, use_global_device_ids=true, to_apply=%region_2.0 | all-reduce | flops 1024 | bytes 8192 | tf_op jit(solution)/shard_map/psum | solution.py:1216
  73.4 2.1 copy-done.79
  75.6 1.3 convolution_convert_fusion.6
  76.9 1.4 convolution_convert_fusion.8
  79.1 1.3 convolution_convert_fusion.4
  80.4 54.2 %line_scatter.1 = f32[128,2048]{1,0:T(8,128)S(1)} custom-call(bf16[4,128,2048]{2,1,0:T(8,128)(2,1)S(1)} %bitcast.147), custom_call_target="tpu_custom_call" | custom-call | tf_op jit(solution)/shard_map/line_scatter/pallas_call | solution.py:532
  137.2 109.0 %gather_all.1 = (bf16[32,128,2048]{2,1,0:T(8,128)(2,1)S(1)}, f32[32,16,128]{2,1,0:T(8,128)S(1)}) custom-call(bf16[128,2048]{1,0:T(8,128)(2,1)S(1)} %multiply_convert_fusion.5.x_ref, f32[16,128]{1,0:T(8,128)S(1)} %select_bitcast_fusion.2.t_ref), custom_call_target="tpu_custom_call" | custom-call | tf_op jit(solution)/shard_map/gather_all/pallas_call | solution.py:248
  246.2 5.8 copy-done.7
  252.6 2.4 slice_bitcast_fusion.5
  256.8 22.4 %fusion.23 = f32[4096,1024]{0,1:T(8,128)} fusion(bf16[4096,2048]{1,0:T(8,128)(2,1)} %bitcast.148, bf16[2048,256]{1,0:T(8,128)(2,1)S(1)} %get-tuple-element.58, bf16[2048,256]{1,0:T(8,128)(2,1)S(1)} %get-tuple-element.57, bf16[2048,256]{1,0:T(8,128)(2,1)S(1)} %get-tuple-element.104, bf16[2048,256]{1,0:T(8,128)(2,1)S(1)} %get-tuple-element.105), kind=kOutput, calls=%fused_computation.90 | convolution fusion | flops 17196646400 | bytes 37748736 | tf_op jit(solution)/shard_map/dot_general | solution.py:1103
  279.2 24.6 %multiply_convert_fusion.1 = (bf16[4096,512]{0,1:T(8,128)(2,1)}, bf16[4096,512]{0,1:T(8,128)(2,1)}, bf16[4096,512]{0,1:T(8,128)(2,1)}, f32[4096,512]{0,1:T(8,128)}) fusion(f32[4096,1024]{0,1:T(8,128)} %fusion.23, f32[4096,2]{0,1:T(2,128)S(1)} %dynamic-slice_bitcast_fusion, bf16[4096,2048]{1,0:T(8,128)(2,1)} %all-gather.2.cloned.1.call-done, ...), kind=kOutput, calls=%fused_computation.8 | convolution fusion | flops 8625586176 | bytes 56655872 | tf_op jit(solution)/shard_map/td,fd->tf/dot_general | solution.py:1110
  303.9 24.7 %fusion.8 = f32[2048,1024]{1,0:T(8,128)} fusion(bf16[4096,2048]{1,0:T(8,128)(2,1)} %bitcast.149, bf16[4096,512]{0,1:T(8,128)(2,1)} %get-tuple-element.49, bf16[4096,512]{0,1:T(8,128)(2,1)} %get-tuple-element.48), kind=kOutput, calls=%fused_computation.19 | convolution fusion | flops 17196646400 | bytes 33554432 | tf_op jit(solution)/shard_map/td,tf->df/dot_general | solution.py:1124
  328.5 23.7 %convolution_convert_fusion = bf16[4096,2048]{1,0:T(8,128)(2,1)} fusion(bf16[4096,512]{0,1:T(8,128)(2,1)} %get-tuple-element.49, bf16[4096,512]{0,1:T(8,128)(2,1)} %get-tuple-element.48, bf16[2048,256]{1,0:T(8,128)(2,1)} %copy-done.41, bf16[2048,256]{1,0:T(8,128)(2,1)S(1)} %get-tuple-element.57, bf16[2048,256]{1,0:T(8,128)(2,1)} %copy-done.42, ...), kind=kOutput, calls=%fused_computation | convolution fusion | flops 17221812224 | bytes 29360128 | tf_op jit(solution)/shard_map/tf,df->td/dot_general | solution.py:1118
  352.2 9.7 %bitcast_reduce_fusion = f32[4096,2]{0,1:T(2,128)S(1)} fusion(f32[4096,512]{0,1:T(8,128)} %get-tuple-element.95, f32[4096,1024]{0,1:T(8,128)} %fusion.23), kind=kLoop, calls=%fused_computation.6 | loop fusion | flops 14671872 | bytes 25198592 | tf_op jit(solution)/shard_map/reduce_sum | solution.py:1111
  362.9 3.6 slice_bitcast_fusion.1
  367.3 93.6 %scatter_all.3 = f32[128,2048]{1,0:T(8,128)} custom-call(bf16[32,128,2048]{2,1,0:T(8,128)(2,1)} %bitcast.152), custom_call_target="tpu_custom_call" | custom-call | tf_op jit(solution)/shard_map/scatter_all/pallas_call | solution.py:709
  460.9 14.6 %convolution_convert_fusion.1 = bf16[4096,2048]{1,0:T(8,128)(2,1)} fusion(bf16[4096,512]{0,1:T(8,128)(2,1)} %get-tuple-element.50, bf16[512,2048]{1,0:T(8,128)(2,1)S(1)} %bitcast.141), kind=kOutput, calls=%fused_computation.1 | convolution fusion | flops 8598323200 | bytes 23068672 | tf_op jit(solution)/shard_map/dot_general | solution.py:1109
  475.6 86.7 %scatter_all.2 = f32[128,2048]{1,0:T(8,128)} custom-call(bf16[32,128,2048]{2,1,0:T(8,128)(2,1)} %bitcast.153), custom_call_target="tpu_custom_call" | custom-call | tf_op jit(solution)/shard_map/scatter_all/pallas_call | solution.py:709
  562.3 15.0 %fusion.42 = f32[512,2048]{1,0:T(8,128)} fusion(bf16[4096,512]{0,1:T(8,128)(2,1)} %get-tuple-element.50, bf16[4096,2048]{1,0:T(8,128)(2,1)} %all-gather.2.cloned.1.call-done), kind=kOutput, calls=%fused_computation.146 | convolution fusion | flops 8589934592 | bytes 25165824 | tf_op jit(solution)/shard_map/tf,td->fd/dot_general | solution.py:1121
  577.4 2.4 pad_maximum_fusion.5
  579.8 1.3 copy-done.24
  581.1 2.3 pad_maximum_fusion.4
  585.5 2.1 multiply_reduce_fusion.4
  588.0 56.6 %line_gather_total.1 = (bf16[4,128,2048]{2,1,0:T(8,128)(2,1)S(1)}, f32[17,2048]{1,0:T(8,128)S(1)}) custom-call(bf16[128,2048]{1,0:T(8,128)(2,1)S(1)} %fusion.36.refs_0_, f32[17,2048]{1,0:T(8,128)S(1)} %pad_maximum_fusion.13.refs_1_), custom_call_target="tpu_custom_call" | custom-call | tf_op jit(solution)/shard_map/line_gather_total/pallas_call | solution.py:410
  644.6 2.1 convolution_convert_fusion.5
  646.7 2.6 convolution_convert_fusion.3
  649.4 4.6 convolution_convert_fusion.7
  653.9 1.6 multiply_reduce_fusion
  655.6 1.3 multiply_convert_fusion.2
  660.6 12.9 %all-reduce = (f32[512]{0:T(512)S(1)}, f32[512]{0:T(512)S(1)}) all-reduce(f32[512]{0:T(512)S(1)} %get-tuple-element.39, f32[512]{0:T(512)S(1)} %get-tuple-element.37), channel_id=1, replica_groups=mesh['dp'=8,'tensor'=4] {'tensor'}, use_global_device_ids=true, to_apply=%region_21.22 | all-reduce | flops 1024 | bytes 8192 | tf_op jit(solution)/shard_map/psum | solution.py:1304
  673.5 1.9 multiply_convert_fusion.3
  675.4 1.6 multiply_convert_fusion.4
  677.0 6.5 fusion.11
  683.6 6.4 convolution_convert_fusion.2
  690.7 78.2 %finish_sums.1 = (bf16[16,128,512]{2,1,0:T(8,128)(2,1)}, bf16[16,128,512]{2,1,0:T(8,128)(2,1)}, bf16[16,128,512]{2,1,0:T(8,128)(2,1)}, f32[128,2048]{1,0:T(8,128)}, f32[8,1024]{1,0:T(8,128)}) custom-call(bf16[16,128,1536]{2,1,0:T(8,128)(2,1)} %bitcast.158, bf16[4,128,2048]{2,1,0:T(8,128)(2,1)} %bitcast.159, f32[128,2048]{1,0:T(8,128)} %get-tuple-element.69.unit_ref, ...), custom_call_target="tpu_custom_call" | custom-call | tf_op jit(solution)/shard_map/finish_sums/pallas_call | solution.py:896
  771.2 1.7 multiply_reduce_fusion.1
  773.5 4.2 bitcast_convert_fusion.2
  777.7 2.7 bitcast_convert_fusion.1
  780.5 2.9 bitcast_convert_fusion
  784.7 1.5 add_convert_fusion
  786.2 47.6 %all-reduce.4.cloned.1.call-done = bf16[512,2048]{1,0:T(8,128)(2,1)} async-done(((bf16[512,2048]{1,0:T(8,128)(2,1)}), bf16[512,2048]{1,0:T(8,128)(2,1)}) %all-reduce.4.cloned.1.call-update) | async-done | bytes 2097168 | tf_op jit(solution)/shard_map/psum | solution.py:1351
  833.8 4.1 convert_element_type.154
  (230 shorter events, 23.1 us)
Async XLA Ops:
  7.2 272.0 %copy-start = (bf16[2,256,2048]{2,1,0:T(8,128)(2,1)S(1)}, bf16[2,256,2048]{2,1,0:T(8,128)(2,1)}, u32[]{:S(2)}) copy-start(bf16[2,256,2048]{2,1,0:T(8,128)(2,1)} %param.30) | copy-start | bytes 6291460
  7.2 272.0 %all-gather.2.cloned.1.call-start = ((), (), s32[]{:S(2)}) async-start(), calls=%async_computation.1 | async-start | bytes 17301504 | tf_op jit(solution)/shard_map/all_gather | solution.py:1208
  8.6 41.2 %copy-start.73 = (f32[128]{0:T(128)}, f32[128]{0:T(128)S(1)}, u32[]{:S(2)}) copy-start(f32[128]{0:T(128)S(1)} %add_rsqrt_fusion.3) | copy-start | bytes 1540
  51.2 532.3 %reduce-scatter.2.cloned.1.call-start = ((), (), s32[]{:S(2)}) async-start(), calls=%async_computation.2 | async-start | bytes 270336 | tf_op jit(solution)/shard_map/reduce_scatter | solution.py:1137
  51.2 4.7 copy-start.4
  51.2 4.7 copy-start.82
  55.9 14.0 %copy-start.68 = (s32[1,512]{1,0:T(1,128)S(1)}, s32[1,512]{1,0:T(1,128)}, u32[]{:S(2)}) copy-start(s32[1,512]{1,0:T(1,128)} %param.17) | copy-start | bytes 6148
  55.9 14.3 %copy-start.64 = (f32[512]{0:T(512)S(1)}, f32[512]{0:T(512)}, u32[]{:S(2)}) copy-start(f32[512]{0:T(512)} %param.23) | copy-start | bytes 6148
  57.2 13.5 %copy-start.16 = (f32[512,512]{0,1:T(8,128)}, f32[512,512]{0,1:T(8,128)S(1)}, u32[]{:S(2)}) copy-start(f32[512,512]{0,1:T(8,128)S(1)} %get-tuple-element.88) | copy-start | bytes 3145732
  57.2 13.2 %copy-start.62 = (f32[512]{0:T(512)S(1)}, f32[512]{0:T(512)}, u32[]{:S(2)}) copy-start(f32[512]{0:T(512)} %param.24) | copy-start | bytes 6148
  70.2 6.7 copy-start.27
  71.5 4.1 copy-start.79
  72.5 4.5 copy-start.8
  79.1 55.5 %copy-start.13 = (bf16[128,2048]{1,0:T(8,128)(2,1)S(1)}, bf16[128,2048]{1,0:T(8,128)(2,1)}, u32[]{:S(2)}) copy-start(bf16[128,2048]{1,0:T(8,128)(2,1)} %param.16) | copy-start | bytes 1572868
  80.4 55.1 %copy-start.51 = (f32[2048]{0:T(1024)S(1)}, f32[2048]{0:T(1024)}, u32[]{:S(2)}) copy-start(f32[2048]{0:T(1024)} %param.26) | copy-start | bytes 24580
  80.4 55.2 %copy-start.47 = (bf16[2048,16]{0,1:T(8,128)(2,1)S(1)}, bf16[2048,16]{0,1:T(8,128)(2,1)}, u32[]{:S(2)}) copy-start(bf16[2048,16]{0,1:T(8,128)(2,1)} %param.27) | copy-start | bytes 196612
  80.4 55.5 %copy-start.75 = (s32[128,8]{0,1:T(8,128)S(1)}, s32[128,8]{0,1:T(8,128)}, u32[]{:S(2)}) copy-start(s32[128,8]{0,1:T(8,128)} %param.18) | copy-start | bytes 12292
  246.2 5.8 copy-start.7
  352.2 10.6 %copy-start.22 = (f32[2048,1024]{1,0:T(8,128)S(1)}, f32[2048,1024]{1,0:T(8,128)}, u32[]{:S(2)}) copy-start(f32[2048,1024]{1,0:T(8,128)} %fusion.8) | copy-start | bytes 25165828
  367.3 466.5 %all-reduce.4.cloned.1.call-start = ((), (), s32[]{:S(2)}) async-start(), calls=%async_computation.3 | async-start | bytes 4194304 | tf_op jit(solution)/shard_map/psum | solution.py:1351
  562.3 15.1 %copy-start.25 = (f32[1,2048,256]{2,1,0:T(8,128)S(1)}, f32[1,2048,256]{2,1,0:T(8,128)}, u32[]{:S(2)}) copy-start(f32[1,2048,256]{2,1,0:T(8,128)} %get-tuple-element.51) | copy-start | bytes 6291460
  562.3 15.1 %copy-start.26 = (f32[1,2048,256]{2,1,0:T(8,128)S(1)}, f32[1,2048,256]{2,1,0:T(8,128)}, u32[]{:S(2)}) copy-start(f32[1,2048,256]{2,1,0:T(8,128)} %get-tuple-element.52) | copy-start | bytes 6291460
  577.4 3.7 copy-start.24
  581.1 4.2 copy-start.2
  581.1 4.3 copy-start.48
  581.1 4.3 copy-start.52
  581.1 4.3 copy-start.70
  583.4 4.1 copy-start.29
  583.5 4.1 copy-start.11
  583.5 61.1 %copy-start.78 = (bf16[512,2048]{1,0:T(8,128)(2,1)S(1)}, bf16[512,2048]{1,0:T(8,128)(2,1)}, u32[]{:S(2)}) copy-start(bf16[512,2048]{1,0:T(8,128)(2,1)} %param.25) | copy-start | bytes 6291460
  587.5 57.1 %copy-start.20 = (f32[128,2048]{1,0:T(8,128)}, f32[128,2048]{1,0:T(8,128)S(1)}, u32[]{:S(2)}) copy-start(f32[128,2048]{1,0:T(8,128)S(1)} %get-tuple-element.96) | copy-start | bytes 3145732
  587.9 58.7 %copy-start.84 = (bf16[4,128,512]{2,1,0:T(8,128)(2,1)S(1)}, bf16[4,128,512]{2,1,0:T(8,128)(2,1)}, u32[]{:S(2)}) copy-start(bf16[4,128,512]{2,1,0:T(8,128)(2,1)} %copy-done.83) | copy-start | bytes 1572868
  649.3 4.6 copy-start.45
  649.3 4.6 copy-start.9
  649.3 4.6 copy-start.46
  673.5 3.5 copy-start.81
  673.5 3.5 copy-start.85
  677.0 6.6 copy-start.6
  683.6 6.4 copy-start.76
  690.7 80.4 %copy-start.14 = (bf16[128,2048]{1,0:T(8,128)(2,1)S(1)}, bf16[128,2048]{1,0:T(8,128)(2,1)}, u32[]{:S(2)}) copy-start(bf16[128,2048]{1,0:T(8,128)(2,1)} %param.16) | copy-start | bytes 1572868
  690.7 80.4 %copy-start.53 = (f32[2048]{0:T(1024)S(1)}, f32[2048]{0:T(1024)}, u32[]{:S(2)}) copy-start(f32[2048]{0:T(1024)} %param.19) | copy-start | bytes 24580
  690.7 80.5 %copy-start.74 = (f32[128]{0:T(128)S(1)}, f32[128]{0:T(128)}, u32[]{:S(2)}) copy-start(f32[128]{0:T(128)} %copy-done.73) | copy-start | bytes 1540
  771.2 6.5 copy-start.38
  780.4 4.2 copy-start.12
  780.4 4.2 copy-start.21
  780.4 4.2 copy-start.30
  780.4 4.2 copy-start.35
  780.4 4.2 copy-start.36
  (41 other events, 67.5 us)
Sparse Core Ops, SparseCore 0:
  51.3 156.9 all-gather.1
  367.4 138.3 reduce-scatter.1
  771.3 62.4 all-reduce.3

commit v3 on v2

--- a/solution.py
+++ b/solution.py
@@ -418,6 +418,41 @@
     )(x, small)
 
 
+def line_total_kernel(nz, x_ref, out_ref, got, send, recv):
+    dp, z = lax.axis_index("dp"), lax.axis_index("tensor")
+    others = [lax.rem(z + turn, nz) for turn in range(1, nz)]
+    barrier = pltpu.get_barrier_semaphore()
+    for other in others:
+        pl.semaphore_signal(barrier, 1, device_id=(dp, other), device_id_type=MESH)
+    pl.semaphore_wait(barrier, nz - 1)
+    copies = [
+        remote(x_ref, got.at[turn], send.at[turn], recv.at[turn], (dp, other)) for turn, other in enumerate(others)
+    ]
+    for copy in copies:
+        copy.start()
+    for copy in copies:
+        copy.wait()
+    total = x_ref[...]
+    for turn in range(nz - 1):
+        total = total + got[turn]
+    out_ref[...] = total
+
+
+def line_total(x, nz, collective_id):
+    dma, vmem = pltpu.SemaphoreType.DMA, pl.BlockSpec(memory_space=pltpu.VMEM)
+    return pl.pallas_call(
+        functools.partial(line_total_kernel, nz),
+        name="line_total",
+        out_shape=jax.ShapeDtypeStruct(x.shape, x.dtype),
+        in_specs=[vmem],
+        out_specs=vmem,
+        scratch_shapes=[pltpu.VMEM((nz - 1,) + x.shape, x.dtype), dma((nz - 1,)), dma((nz - 1,))],
+        compiler_params=pltpu.CompilerParams(
+            collective_id=collective_id, has_side_effects=True, vmem_limit_bytes=4 * 2**20
+        ),
+    )(x)
+
+
 CHUNK = 16
 
 
@@ -548,7 +583,7 @@
     return [sorted(range(nz), key=lambda zz: (-abs(zz - z), zz if z >= nz // 2 else -zz)) for z in range(nz)]
 
 
-def scatter_kernel(nz, p_ref, out_ref, acc, rc, ra, rb, rx, ry, ru, rd, s_local, s_core, r_core, s_a, r_a, s_b, r_b, s_x, r_x, s_y, r_y, s_u, r_u, s_d, r_d):
+def scatter_kernel(nz, p_ref, t_ref, out_ref, tiles_ref, acc, rc, ra, rb, rx, ry, ru, rd, s_tile, r_tile, s_keep, s_local, s_core, r_core, s_a, r_a, s_b, r_b, s_x, r_x, s_y, r_y, s_u, r_u, s_d, r_d):
     dp, z = lax.axis_index("dp"), lax.axis_index("tensor")
     rows = acc.shape[2]
     half = rows // 2
@@ -653,8 +688,27 @@
             add(acc.at[0, zz], (rd.at[zz], 0))
             down_copy(zz).start()
 
-    greet(dp, z, nz)
+    def peers():
+        for flip in range(8):
+            for turn in range(nz):
+                if flip or turn:
+                    yield flip, turn, dp ^ flip, lax.rem(z + turn, nz)
+
+    def tile_copy(flip, turn, peer, line):
+        here = dp * nz + z
+        return remote(
+            t_ref.at[peer * nz + line], tiles_ref.at[here], s_tile.at[flip, turn], r_tile.at[flip, turn], (peer, line)
+        )
+
+    barrier = pltpu.get_barrier_semaphore()
+    for _, _, peer, line in peers():
+        pl.semaphore_signal(barrier, 1, device_id=(peer, line), device_id_type=MESH)
+    pl.semaphore_wait(barrier, 8 * nz - 1)
     wave(0)
+    keep = pltpu.make_async_copy(t_ref.at[dp * nz + z], tiles_ref.at[dp * nz + z], s_keep)
+    keep.start()
+    for peer in peers():
+        tile_copy(*peer).start()
     for i in range(nz + 3):
         if i + 1 < nz:
             wave(i + 1)
@@ -667,6 +721,12 @@
         if 0 <= i - 3 < nz:
             stage_line(i - 3)
 
+    keep.wait()
+    for flip, turn, peer, line in peers():
+        tile_copy(flip, turn, peer, line).wait_send()
+        source = tiles_ref.at[peer * nz + lax.rem(z - turn + nz, nz)]
+        remote(source, source, s_tile.at[flip, turn], r_tile.at[flip, turn], (dp ^ 1, z)).wait_recv()
+
     @pl.when(z > 0)
     def _():
         up_copy(z).wait_recv()
@@ -702,28 +762,32 @@
             down_copy(zz).wait_send()
 
 
-def scatter_all(p, nz, collective_id):
+def scatter_all(p, tiles, nz, collective_id):
     _, rows, width = p.shape
     dma, vmem = pltpu.SemaphoreType.DMA, functools.partial(pltpu.VMEM, dtype=p.dtype)
     half = rows // 2
     return pl.pallas_call(
         functools.partial(scatter_kernel, nz),
         name="scatter_all",
-        out_shape=jax.ShapeDtypeStruct((rows, width), jnp.float32),
-        in_specs=[pl.BlockSpec(memory_space=pl.ANY)],
-        out_specs=pl.BlockSpec(memory_space=pltpu.VMEM),
+        out_shape=(
+            jax.ShapeDtypeStruct((rows, width), jnp.float32),
+            jax.ShapeDtypeStruct(tiles.shape, tiles.dtype),
+        ),
+        in_specs=[pl.BlockSpec(memory_space=pl.ANY), pl.BlockSpec(memory_space=pltpu.VMEM)],
+        out_specs=(pl.BlockSpec(memory_space=pltpu.VMEM), pl.BlockSpec(memory_space=pltpu.VMEM)),
         scratch_shapes=[vmem((4, nz, rows, width)), vmem((4, nz, rows, width))]
         + [vmem((nz, half, width)) for _ in range(2)]
         + [vmem((nz, rows, width)) for _ in range(4)]
+        + [dma((8, nz)), dma((8, nz)), dma(())]
         + [dma((4, nz)), dma((4, nz)), dma((4, nz))]
         + [dma((nz,)) for _ in range(12)],
         compiler_params=pltpu.CompilerParams(
             collective_id=collective_id, has_side_effects=True, vmem_limit_bytes=VMEM_LIMIT
         ),
-    )(p)
-
-
-def finish_kernel(nz, nc, g_ref, p_ref, unit_ref, small_ref, sum_q, sum_k, sum_v, out_ref, total_ref, buf, acc, rc, ra, rb, rx, ry, line_acc, up, down, *sems):
+    )(p, tiles)
+
+
+def finish_kernel(nz, nc, g_ref, h_ref, p_ref, unit_ref, small_ref, sum_q, sum_k, sum_v, sum_o, out_ref, total_ref, buf, acc, rc, ra, rb, rx, ry, line_acc, up, down, *sems):
     (s_load, s_core, r_core, s_a, r_a, s_b, r_b, s_x, r_x, s_y, r_y) = sems[:11]
     (t_x, q_x, t_y, q_y, t_a, q_a, t_b, q_b, t_c, q_c) = sems[11:21]
     s_line, s_store, s_up, r_up, s_down, r_down = sems[21:27]
@@ -733,13 +797,27 @@
     half = rows // 2
     flips = (0, 2, 4, 6)
 
-    def load(kind, c):
-        return pltpu.make_async_copy(g_ref.at[(dp ^ flips[kind]) * nc + c], acc.at[kind, c], s_load.at[kind, c])
-
-    def core_copy(kind, c):
-        return remote(
-            g_ref.at[(dp ^ flips[kind] ^ 1) * nc + c], rc.at[kind, c], s_core.at[kind, c], r_core.at[kind, c], (dp ^ 1, z)
-        )
+    parts = ((g_ref, 0, g_ref.shape[2]), (h_ref, g_ref.shape[2], h_ref.shape[2]))
+
+    def loads(kind, c):
+        return [
+            pltpu.make_async_copy(
+                ref.at[(dp ^ flips[kind]) * nc + c], acc.at[kind, c, :, pl.ds(at, size)], s_load.at[k, kind, c]
+            )
+            for k, (ref, at, size) in enumerate(parts)
+        ]
+
+    def core_copies(kind, c):
+        return [
+            remote(
+                ref.at[(dp ^ flips[kind] ^ 1) * nc + c],
+                rc.at[kind, c, :, pl.ds(at, size)],
+                s_core.at[k, kind, c],
+                r_core.at[k, kind, c],
+                (dp ^ 1, z),
+            )
+            for k, (ref, at, size) in enumerate(parts)
+        ]
 
     def a_copy(c):
         return remote(acc.at[3, c, pl.ds(0, half)], ra.at[c], s_a.at[c], r_a.at[c], (dp ^ 2, z))
@@ -780,8 +858,10 @@
         remote(ref, ref, sem, sem, (dp ^ 1, z)).wait_recv()
 
     def paired(kind, c):
-        load(kind, c).wait()
-        core_copy(kind, c).wait_recv()
+        for copy in loads(kind, c):
+            copy.wait()
+        for copy in core_copies(kind, c):
+            copy.wait_recv()
 
     def stage_diagonal(c):
         paired(3, c)
@@ -837,11 +917,13 @@
     line_load.start()
     for c in range(nc):
         for kind in (3, 1, 2, 0):
-            load(kind, c).start()
+            for copy in loads(kind, c):
+                copy.start()
     greet_total(dp, z, nz)
     for c in range(nc):
         for kind in (3, 1, 2, 0):
-            core_copy(kind, c).start()
+            for copy in core_copies(kind, c):
+                copy.start()
     line = Line(nz, dp, z, line_acc, up, down, s_up, r_up, s_down, r_down)
     line_load.wait()
     line.first()
@@ -870,16 +952,17 @@
             arrived(full(flip, c), q_c.at[kind, c])
         for kind in (3, 4):
             arrived(full(7, c).at[pl.ds((kind - 3) * half, half)], q_c.at[kind, c])
-    wide = buf.shape[2] // 3
+    wide = buf.shape[2] // 4
     stores = [
         pltpu.make_async_copy(buf.at[:, :, pl.ds(k * wide, wide)], ref, s_store.at[k])
-        for k, ref in enumerate((sum_q, sum_k, sum_v))
+        for k, ref in enumerate((sum_q, sum_k, sum_v, sum_o))
     ]
     for store in stores:
         store.start()
     for c in range(nc):
         for kind in range(4):
-            core_copy(kind, c).wait_send()
+            for copy in core_copies(kind, c):
+                copy.wait_send()
         for copy in (a_copy, b_copy, x_copy, y_copy, back_x, back_y, back_a, back_b):
             copy(c).wait_send()
         for kind in range(5):
@@ -888,8 +971,9 @@
         store.wait()
 
 
-def finish_sums(g, p, unit, small, nz, nc, collective_id):
+def finish_sums(g, h, p, unit, small, nz, nc, collective_id):
     _, rows, width = g.shape
+    width += h.shape[2]
     _, line_rows, line_width = p.shape
     half = rows // 2
     dma, vmem = pltpu.SemaphoreType.DMA, functools.partial(pltpu.VMEM, dtype=g.dtype)
@@ -897,29 +981,93 @@
         functools.partial(finish_kernel, nz, nc),
         name="finish_sums",
         out_shape=(
-            *[jax.ShapeDtypeStruct(g.shape[:2] + (width // 3,), g.dtype)] * 3,
+            *[jax.ShapeDtypeStruct(g.shape[:2] + (width // 4,), g.dtype)] * 4,
             jax.ShapeDtypeStruct((line_rows, line_width), jnp.float32),
             jax.ShapeDtypeStruct(small.shape, small.dtype),
         ),
-        in_specs=[pl.BlockSpec(memory_space=pl.ANY)] * 2 + [pl.BlockSpec(memory_space=pltpu.VMEM)] * 2,
+        in_specs=[pl.BlockSpec(memory_space=pl.ANY)] * 3 + [pl.BlockSpec(memory_space=pltpu.VMEM)] * 2,
         out_specs=(
-            *[pl.BlockSpec(memory_space=pl.ANY)] * 3,
+            *[pl.BlockSpec(memory_space=pl.ANY)] * 4,
             *[pl.BlockSpec(memory_space=pltpu.VMEM)] * 2,
         ),
-        scratch_shapes=[vmem(g.shape), vmem((4, nc, rows, width)), vmem((4, nc, rows, width))]
+        scratch_shapes=[vmem(g.shape[:2] + (width,)), vmem((4, nc, rows, width)), vmem((4, nc, rows, width))]
         + [vmem((nc, half, width)) for _ in range(2)]
         + [vmem((nc, rows, width)) for _ in range(2)]
         + [vmem((nz, line_rows, line_width)) for _ in range(3)]
-        + [dma((4, nc)) for _ in range(3)]
+        + [dma((2, 4, nc)) for _ in range(3)]
         + [dma((nc,)) for _ in range(16)]
         + [dma((5, nc)), dma((5, nc))]
-        + [dma(()), dma((3,))]
+        + [dma(()), dma((4,))]
         + [dma((nz, PARTS)) for _ in range(4)]
         + total_scratch(nz, small.shape, small.dtype),
         compiler_params=pltpu.CompilerParams(
             collective_id=collective_id, has_side_effects=True, vmem_limit_bytes=VMEM_LIMIT
         ),
-    )(g, p, unit, small)
+    )(g, h, p, unit, small)
+
+
+class Spread:
+    def __init__(self, nz, row_shape):
+        self.nz, self.row_shape = nz, row_shape
+
+    @staticmethod
+    def swap(value, flip):
+        return lax.ppermute(value, "dp", [(i, i ^ flip) for i in range(8)])
+
+    @staticmethod
+    def plus(a, b):
+        return (a.astype(jnp.float32) + b.astype(jnp.float32)).astype(a.dtype)
+
+    def pair(self, mine, partners):
+        self.mine = mine
+        return self.swap(partners, 1)
+
+    def sides(self, theirs):
+        nz, plus = self.nz, self.plus
+        self.low, self.high = slice(0, nz // 2), slice(nz // 2, nz)
+        mine = self.mine.reshape((4, nz) + self.row_shape)
+        self.whole = whole = plus(mine, theirs.reshape(mine.shape))
+        to_x = jnp.stack([whole[1, self.low], whole[3, self.low]])
+        to_y = jnp.stack([whole[2, self.high], whole[3, self.high]])
+        return to_x, to_y
+
+    def side(self, sides):
+        return self.swap(sides[0], 2), self.swap(sides[1], 4)
+
+    def last_side(self, sides):
+        by_x, by_y = sides
+        whole, low, high, plus = self.whole, self.low, self.high, self.plus
+        self.low_own, low_y = plus(whole[0, low], by_x[0]), plus(whole[2, low], by_x[1])
+        self.high_own, high_x = plus(whole[0, high], by_y[0]), plus(whole[1, high], by_y[1])
+        return self.swap(low_y, 4), self.swap(high_x, 2)
+
+    def column(self, sides):
+        return jnp.concatenate([self.plus(self.low_own, sides[0]), self.plus(self.high_own, sides[1])])
+
+    def blocks(self, column):
+        z = lax.axis_index("tensor")
+        return tuple(
+            lax.dynamic_index_in_dim(column, (z + turn) % self.nz, axis=0, keepdims=False)
+            for turn in range(self.nz)
+        )
+
+    def line(self, blocks):
+        nz = self.nz
+        self.own = blocks[0]
+        return tuple(
+            lax.ppermute(blocks[turn], "tensor", [(i, (i + turn) % nz) for i in range(nz)])
+            for turn in range(1, nz)
+        )
+
+    def total(self, terms):
+        total = self.own.astype(jnp.float32)
+        for term in terms:
+            total = total + term.astype(jnp.float32)
+        return total
+
+
+def hold(first, second):
+    return lax.optimization_barrier((first, second))
 
 
 def experts_routed(
@@ -1084,7 +1232,6 @@
     exp_dev, _, width = w_gate.shape
     all_count = devices * tok_count
     expert_at = jnp.arange(experts, dtype=jnp.int32)
-    local_at = lax.axis_index("dp") * exp_dev + jnp.arange(exp_dev, dtype=jnp.int32)
 
     chosen = jnp.any(expert_ids[:, :, None] == expert_at[None, None, :], axis=1)
     route_probs = jax.nn.softmax(
@@ -1106,7 +1253,17 @@
     silu_gate = gate_pre * gate_sigmoid
     hidden = silu_gate * up_pre
     gated_hidden = (spread * hidden).astype(jnp.bfloat16)
-    out_part = jnp.dot(gated_hidden, down_rows, preferred_element_type=jnp.float32).astype(jnp.bfloat16)
+    lines = gated_hidden.reshape(n_dp, n_tensor * tok_count, both)
+
+    def out_rows(places):
+        picked = [
+            lax.dynamic_index_in_dim(lines, lax.axis_index("dp") ^ k, axis=0, keepdims=False)
+            for k in places
+        ]
+        return jnp.dot(
+            jnp.concatenate(picked), down_rows, preferred_element_type=jnp.float32
+        ).astype(jnp.bfloat16)
+
     back = jnp.einsum("td,fd->tf", all_cotangents, down_rows, preferred_element_type=jnp.float32)
     gate_grads = jnp.sum((hidden * back).reshape(all_count, exp_dev, width), axis=-1)
     grad_hidden = spread * back
@@ -1116,8 +1273,17 @@
     grad_up_pre = (grad_hidden * silu_gate).astype(jnp.bfloat16)
     grad_pre = jnp.concatenate([grad_gate_pre, grad_up_pre], axis=1)
     in_part = jnp.einsum("tf,df->td", grad_pre, wide, preferred_element_type=jnp.float32).astype(jnp.bfloat16)
-    grad_in = scatter_all(in_part.reshape(devices, tok_count, d_model), n_tensor, 1)
-    moe_out = scatter_all(out_part.reshape(devices, tok_count, d_model), n_tensor, 1)
+    spread = Spread(n_tensor, (tok_count, d_model))
+    partner_rows = out_rows((1, 3, 5, 7))
+    in_part, partner_rows = hold(in_part, partner_rows)
+    theirs = spread.pair(out_rows((0, 2, 4, 6)), partner_rows)
+    tiles = gate_grads.reshape(devices, tok_count, exp_dev).transpose(0, 2, 1)
+    tiles = jnp.pad(tiles, ((0, 0), (0, 8 - exp_dev), (0, 0)))
+    grad_in, gate_tiles = scatter_all(
+        in_part.reshape(devices, tok_count, d_model), tiles, n_tensor, 1
+    )
+    grad_in, theirs = hold(grad_in, theirs)
+    sides = spread.side(spread.sides(theirs))
     grad_down = jnp.einsum(
         "tf,td->fd", gated_hidden, all_cotangents, preferred_element_type=jnp.float32
     ).reshape(exp_dev, width, d_model)
@@ -1125,19 +1291,9 @@
     grad_gate = jnp.stack([grad_wide[:, e * width : (e + 1) * width] for e in range(exp_dev)])
     grad_up = jnp.stack([grad_wide[:, both + e * width : both + (e + 1) * width] for e in range(exp_dev)])
 
-    route_grads = jnp.sum(
-        jnp.where(
-            local_at[None, :, None] == expert_at[None, None, :],
-            gate_grads[:, :, None],
-            0.0,
-        ),
-        axis=1,
-    )
-    grad_route = jnp.where(
-        chosen, lax.psum_scatter(route_grads, everyone, scatter_dimension=0, tiled=True), 0.0
-    )
+    grad_route = jnp.sum(gate_tiles[:, :exp_dev].reshape(n_dp, n_tensor, exp_dev, tok_count), axis=1)
+    grad_route = jnp.where(chosen, grad_route.reshape(experts, tok_count).T, 0.0)
     cotangent = grad_output.astype(jnp.float32)
-    result = (hidden_after_attention + moe_out).astype(jnp.bfloat16)
     grad_logits = (
         route_probs * (grad_route - jnp.sum(route_probs * grad_route, axis=-1, keepdims=True))
     ).astype(jnp.bfloat16)
@@ -1159,7 +1315,8 @@
         + cotangent
     )
     return (
-        result,
+        spread,
+        sides,
         grad_hidden_one,
         grad_expert_share,
         grad_router_part,
@@ -1213,8 +1370,8 @@
         .astype(jnp.bfloat16)
         .reshape(seq_len, local_heads, head_dim)
     )
-    query_total, key_total = lax.psum(
-        (jnp.sum(query_raw * query_raw, axis=1), jnp.sum(key_raw * key_raw, axis=1)), "tensor"
+    query_total, key_total = line_total(
+        jnp.stack([jnp.sum(query_raw * query_raw, axis=1), jnp.sum(key_raw * key_raw, axis=1)]), n_tensor, 6
     )
     query_scale = lax.rsqrt(query_total / d_model + EPSILON)[:, None]
     key_scale = lax.rsqrt(key_total / d_model + EPSILON)[:, None]
@@ -1244,7 +1401,7 @@
         3,
     )
     hidden_after_attention = input_tensors + attn_out
-    result, grad_hidden_one, grad_expert_share, grad_router_part, grad_gate, grad_up, grad_down = (
+    spread, sides, grad_hidden_one, grad_expert_share, grad_router_part, grad_gate, grad_up, grad_down = (
         experts_dense(
             hidden_after_attention,
             expert_ids,
@@ -1259,11 +1416,13 @@
     )
     grad_attn = grad_hidden_one.astype(jnp.bfloat16)
     side_parts = jnp.concatenate([grad_router_part.T, grad_expert_share[None, :]])
-    grad_attn_all, side_total = line_gather(grad_attn, n_tensor, 5, side_parts)
+    side_total = lax.psum(side_parts, ("dp", "tensor"))
+    grad_attn_all = line_gather(grad_attn, n_tensor, 2)
+    grad_attn_all, sides = hold(grad_attn_all, sides)
+    sides = spread.last_side(sides)
     grad_attn_all = grad_attn_all.reshape(seq_len, d_model)
-    total_router, total_ffn_gain = side_total[:-1].T, side_total[-1]
     grad_output_part = jnp.einsum(
-        "sd,se->de", context, grad_attn_all, preferred_element_type=jnp.float32
+        "sd,se->ed", context, grad_attn_all, preferred_element_type=jnp.float32
     )
     grad_context = (
         jnp.einsum("se,de->sd", grad_attn_all, w_output, preferred_element_type=jnp.float32)
@@ -1301,9 +1460,12 @@
     grad_kgain_part = jnp.sum(grad_key_normed * key_hat, axis=0)
     grad_query_hat = grad_query_normed * query_gain
     grad_key_hat = grad_key_normed * key_gain
-    query_inner, key_inner = lax.psum(
-        (jnp.sum(grad_query_hat * query_hat, axis=1), jnp.sum(grad_key_hat * key_hat, axis=1)),
-        "tensor",
+    query_inner, key_inner = line_total(
+        jnp.stack(
+            [jnp.sum(grad_query_hat * query_hat, axis=1), jnp.sum(grad_key_hat * key_hat, axis=1)]
+        ),
+        n_tensor,
+        6,
     )
     grad_query_raw = (
         query_scale * (grad_query_hat - query_hat * (query_inner / d_model)[:, None])
@@ -1313,6 +1475,8 @@
     )
     grad_value_raw = grad_value_total.reshape(seq_len, local_dim).astype(jnp.bfloat16)
     grad_raw = jnp.concatenate([grad_query_raw, grad_key_raw, grad_value_raw], axis=1)
+    grad_raw, sides = hold(grad_raw, sides)
+    column = spread.column(sides)
     w_raw = jnp.concatenate([w_query, w_key, w_value], axis=1)
     raw_part = jnp.einsum("sd,sf->df", normed_all, grad_raw, preferred_element_type=jnp.float32)
     row_part = jnp.einsum("sf,df->sd", grad_raw, w_raw, preferred_element_type=jnp.float32)
@@ -1325,8 +1489,11 @@
             jnp.zeros((d_model,), jnp.float32),
         ]
     )
-    total_query, total_key, total_value, grad_first_normalized, gain_totals = finish_sums(
+    gain_parts, column = hold(gain_parts, column)
+    terms = spread.line(spread.blocks(column))
+    finished = finish_sums(
         raw_part.astype(jnp.bfloat16).reshape(n_dp * PIECES, -1, 3 * local_dim),
+        grad_output_part.astype(jnp.bfloat16).reshape(n_dp * PIECES, -1, local_dim),
         row_part.astype(jnp.bfloat16).reshape(n_tensor, tok_count, d_model),
         first_unit_rows,
         gain_parts.reshape(8, -1),
@@ -1334,10 +1501,14 @@
         PIECES,
         4,
     )
-    total_query, total_key, total_value = (
+    finished, (terms, side_total) = hold(finished, (terms, side_total))
+    total_query, total_key, total_value, total_output, grad_first_normalized, gain_totals = finished
+    total_router, total_ffn_gain = side_total[:-1].T, side_total[-1]
+    total_query, total_key, total_value, total_output = (
         total.reshape(d_model, local_dim).astype(jnp.float32)
-        for total in (total_query, total_key, total_value)
-    )
+        for total in (total_query, total_key, total_value, total_output)
+    )
+    total_output = total_output.T
     grad_first_unit_rows = grad_first_normalized * attention_norm_gain
     grad_tokens = (
         first_norm_scale
@@ -1348,7 +1519,7 @@
         )
         + grad_hidden_one
     ).astype(jnp.bfloat16)
-    total_output = lax.psum(grad_output_part.astype(jnp.bfloat16), "dp").astype(jnp.float32)
+    result = (hidden_after_attention + spread.total(terms)).astype(jnp.bfloat16)
     gain_totals = gain_totals.reshape(4, d_model)
     total_attn_gain = gain_totals[0]
     own_gains = lax.dynamic_slice_in_dim(

time: 854 us -> 787 us (0.922)
  waiting for transfers between devices: 47.6 us -> 5.92 us
  Pallas kernels: 517 us -> 477 us
  local copies, waits for them, and re-layouts: 27.4 us -> 55.1 us
  blocking collectives: 24.1 us -> 0 us
  other arithmetic: 49.2 us -> 65.2 us
  matrix products: 164 us -> 154 us
    pallas_call x2 -> x1, Pallas kernels: 180 us -> 92.6 us  [scatter_all(): pl.pallas_call(functools.partial(scatter_kernel, nz), name='scatter_all',...]
    psum x1, waiting for transfers between devices: 47.6 us -> 0.02 us  [local_gathered(): side_total = lax.psum(side_parts, ('dp', 'tensor'))]
    pallas_call x1 -> x2, Pallas kernels: 56.6 us -> 11 us  [line_total(): pl.pallas_call(functools.partial(line_total_kernel, nz), name='line_total...]
    pallas_call x1, Pallas kernels: 78.2 us -> 121 us  [finish_sums(): pl.pallas_call(functools.partial(finish_kernel, nz, nc), name='finish_sum...]
    pallas_call x1 -> x2, Pallas kernels: 39 us -> 76.8 us  [line_gather(): pl.pallas_call(kernel, name='line_gather', out_shape=blocks, in_specs=[vm...]
    psum x2 -> x0, blocking collectives: 24.1 us -> none  [the longest x1 12.9 us: local_gathered(): lax.psum((jnp.sum(grad_query_hat * query_hat, axis=1), jnp.sum(grad_key_h...]
    reshape x0 -> x1, local copies, waits for them, and re-layouts: none -> 15 us  [experts_dense(): lines = gated_hidden.reshape(n_dp, n_tensor * tok_count, both)]
    convert_element_type x1 -> x4, other arithmetic: 4.13 us -> 15.8 us  [the longest x3 13.2 us: plus(): return (a.astype(jnp.float32) + b.astype(jnp.float32)).astype(a.dtype)]
  transfers between devices with their start and end apart: 3 -> 10, of which waited for: 1 -> 2; matrix products, arithmetic and copies ran while one was open for 11% -> 16% of each run, Pallas kernels for 41% -> 44%
where the time goes in v3:
time: 787 us; the launch traced here: 781 us
  Pallas kernels  477 us (61%)
  matrix products  154 us (20%)
  other arithmetic  65.2 us (8%)
  local copies, waits for them, and re-layouts  55.1 us (7%)
  between operations  15.6 us (2%)
    pallas_call x1, Pallas kernels, finish_sums(): pl.pallas_call(functools.partial(finish_kernel, nz, nc), name='finish_sum...  121 us
    pallas_call x1, Pallas kernels, gather_all(): pl.pallas_call(functools.partial(gather_kernel, nz), name='gather_all', o...  118 us
    pallas_call x1, Pallas kernels, scatter_all(): pl.pallas_call(functools.partial(scatter_kernel, nz), name='scatter_all',...  92.6 us
    pallas_call x2, Pallas kernels, line_gather(): pl.pallas_call(kernel, name='line_gather', out_shape=blocks, in_specs=[vm...  76.8 us
    pallas_call x1, Pallas kernels, line_scatter(): pl.pallas_call(functools.partial(line_scatter_kernel, nz), name='line_sca...  57.6 us
    dot_general x1, matrix products, experts_dense(): jnp.einsum('td,fd->tf', all_cotangents, down_rows, preferred_element_type...  24.7 us
    dot_general x1, matrix products, experts_dense(): jnp.einsum('tf,df->td', grad_pre, wide, preferred_element_type=jnp.float32)  23.7 us
    dot_general x1, matrix products, experts_dense(): pre = jnp.dot(all_rows, wide, preferred_element_type=jnp.float32)  22.4 us
  transfers between devices with their start and end apart: 10, of which 2 were waited for; matrix products, arithmetic and copies ran while one was open for 16% of the time, Pallas kernels for 44%

profile of v3, /device:TPU:0, one launch (start us, length us, event | category | flops | bytes accessed | tf_op | source)
XLA Modules:
  0.0 780.8 jit_solution(12149420075496656659)
XLA Ops:
  8.6 2.3 convert_multiply_fusion
  10.9 39.0 %line_gather.2 = bf16[4,128,2048]{2,1,0:T(8,128)(2,1)S(1)} custom-call(bf16[128,2048]{1,0:T(8,128)(2,1)S(1)} %get-tuple-element.129.refs_0_), custom_call_target="tpu_custom_call" | custom-call | tf_op jit(solution)/shard_map/line_gather/pallas_call | solution.py:401
  51.4 3.7 multiply_reduce_fusion.8
  56.5 5.5 line_total.2
  71.9 57.6 %line_scatter.1 = f32[128,2048]{1,0:T(8,128)S(1)} custom-call(bf16[4,128,2048]{2,1,0:T(8,128)(2,1)S(1)} %bitcast.213), custom_call_target="tpu_custom_call" | custom-call | tf_op jit(solution)/shard_map/line_scatter/pallas_call | solution.py:567
  130.9 117.8 %gather_all.1 = (bf16[32,128,2048]{2,1,0:T(8,128)(2,1)S(1)}, f32[32,16,128]{2,1,0:T(8,128)S(1)}) custom-call(bf16[128,2048]{1,0:T(8,128)(2,1)S(1)} %multiply_convert_fusion.5.x_ref, f32[16,128]{1,0:T(8,128)S(1)} %select_bitcast_fusion.2.t_ref), custom_call_target="tpu_custom_call" | custom-call | tf_op jit(solution)/shard_map/gather_all/pallas_call | solution.py:248
  248.8 5.8 copy-done.6
  255.0 2.4 slice_bitcast_fusion.5
  259.2 22.4 %fusion.48 = f32[4096,1024]{0,1:T(8,128)} fusion(bf16[4096,2048]{1,0:T(8,128)(2,1)} %bitcast.214, bf16[2048,256]{1,0:T(8,128)(2,1)S(1)} %get-tuple-element.119, bf16[2048,256]{1,0:T(8,128)(2,1)S(1)} %get-tuple-element.118, bf16[2048,256]{1,0:T(8,128)(2,1)S(1)} %get-tuple-element.167, bf16[2048,256]{1,0:T(8,128)(2,1)S(1)} %get-tuple-element.168), kind=kOutput, calls=%fused_computation.124 | convolution fusion | flops 17196646400 | bytes 37748736 | tf_op jit(solution)/shard_map/dot_general | solution.py:1250
  281.6 24.7 %multiply_convert_fusion.1 = (bf16[4096,512]{0,1:T(8,128)(2,1)}, bf16[4096,512]{0,1:T(8,128)(2,1)}, bf16[4096,512]{0,1:T(8,128)(2,1)}, f32[4096,512]{0,1:T(8,128)}) fusion(f32[4096,1024]{0,1:T(8,128)} %fusion.48, f32[4096,2]{0,1:T(2,128)S(1)} %dynamic-slice_bitcast_fusion.11, bf16[4096,2048]{1,0:T(8,128)(2,1)} %all-gather.2.cloned.1.call-done, ...), kind=kOutput, calls=%fused_computation.8 | convolution fusion | flops 8625586176 | bytes 56655872 | tf_op jit(solution)/shard_map/td,fd->tf/dot_general | solution.py:1267
  306.3 9.4 %bitcast_reduce_fusion = f32[4096,2]{0,1:T(2,128)S(1)} fusion(f32[4096,512]{0,1:T(8,128)} %get-tuple-element.158, f32[4096,1024]{0,1:T(8,128)} %fusion.48), kind=kLoop, calls=%fused_computation.6 | loop fusion | flops 14671872 | bytes 25198592 | tf_op jit(solution)/shard_map/reduce_sum | solution.py:1268
  315.8 15.0 %copy.85 = bf16[4096,512]{1,0:T(8,128)(2,1)} copy(bf16[4096,512]{0,1:T(8,128)(2,1)} %get-tuple-element.94) | data formatting | bytes 8388608 | tf_op jit(solution)/shard_map/reshape | solution.py:1256
  330.7 23.7 %convolution_convert_fusion = bf16[4096,2048]{1,0:T(8,128)(2,1)} fusion(bf16[4096,512]{0,1:T(8,128)(2,1)} %get-tuple-element.93, bf16[4096,512]{0,1:T(8,128)(2,1)} %get-tuple-element.92, bf16[2048,256]{1,0:T(8,128)(2,1)} %copy-done.33, bf16[2048,256]{1,0:T(8,128)(2,1)S(1)} %get-tuple-element.118, bf16[2048,256]{1,0:T(8,128)(2,1)} %copy-done.34, ...), kind=kOutput, calls=%fused_computation.1 | convolution fusion | flops 17221812224 | bytes 29360128 | tf_op jit(solution)/shard_map/tf,df->td/dot_general | solution.py:1275
  354.4 3.7 dynamic-slice_bitcast_fusion.6
  358.1 9.6 %convolution_convert_fusion.2 = bf16[2048,2048]{1,0:T(8,128)(2,1)} fusion(bf16[512,2048]{1,0:T(8,128)(2,1)S(1)} %bitcast.205, bf16[512,512]{1,0:T(8,128)(2,1)S(1)} %get-tuple-element.109, bf16[512,512]{1,0:T(8,128)(2,1)S(1)} %get-tuple-element.110, bf16[512,512]{1,0:T(8,128)(2,1)S(1)} %get-tuple-element.111, bf16[512,512]{1,0:T(8,128)(2,1)S(1)} %get-tuple-element.112), kind=kOutput, calls=%fused_computation.13 | convolution fusion | flops 4307550208 | bytes 12582912 | tf_op jit(solution)/shard_map/dot_general | solution.py:1263
  368.4 92.6 %scatter_all.1 = (f32[128,2048]{1,0:T(8,128)}, f32[32,8,128]{2,1,0:T(8,128)}) custom-call(bf16[32,128,2048]{2,1,0:T(8,128)(2,1)} %bitcast.224, f32[32,8,128]{2,1,0:T(8,128)} %pad.4.t_ref), custom_call_target="tpu_custom_call" | custom-call | tf_op jit(solution)/shard_map/scatter_all/pallas_call | solution.py:769
  462.0 22.3 %fusion.8 = f32[2048,1024]{1,0:T(8,128)S(1)} fusion(bf16[4096,2048]{1,0:T(8,128)(2,1)} %bitcast.215, bf16[4096,512]{0,1:T(8,128)(2,1)} %get-tuple-element.93, bf16[4096,512]{0,1:T(8,128)(2,1)} %get-tuple-element.92), kind=kOutput, calls=%fused_computation.20 | convolution fusion | flops 17196646400 | bytes 33554432 | tf_op jit(solution)/shard_map/td,tf->df/dot_general | solution.py:1290
  484.4 3.4 slice_bitcast_fusion.1
  487.8 9.1 %fusion.22 = bf16[2048,2048]{1,0:T(8,128)(2,1)} fusion(bf16[512,2048]{1,0:T(8,128)(2,1)S(1)} %bitcast.206, bf16[512,512]{1,0:T(8,128)(2,1)} %get-tuple-element.106, bf16[512,512]{1,0:T(8,128)(2,1)} %get-tuple-element.107, bf16[512,512]{1,0:T(8,128)(2,1)} %get-tuple-element.108, bf16[512,512]{1,0:T(8,128)(2,1)} %get-tuple-element.105), kind=kOutput, calls=%fused_computation.46 | convolution fusion | flops 4303355904 | bytes 12582912 | tf_op jit(solution)/shard_map/dot_general | solution.py:1263
  496.9 12.2 %fusion.69 = f32[512,2048]{1,0:T(8,128)} fusion(bf16[4096,512]{0,1:T(8,128)(2,1)} %get-tuple-element.94, bf16[4096,2048]{1,0:T(8,128)(2,1)S(1)} %bitcast.223), kind=kOutput, calls=%fused_computation.193 | convolution fusion | flops 8589934592 | bytes 25165824 | tf_op jit(solution)/shard_map/tf,td->fd/dot_general | solution.py:1287
  509.1 7.5 add_convert_fusion
  516.6 1.6 stack.60
  518.3 2.7 copy-done.9
  521.0 1.5 pad_maximum_fusion.6
  524.7 2.4 pad_maximum_fusion.5
  528.4 2.3 pad_maximum_fusion.4
  532.9 3.2 fusion.62
  536.1 37.9 %line_gather.3 = bf16[4,128,2048]{2,1,0:T(8,128)(2,1)S(1)} custom-call(bf16[128,2048]{1,0:T(8,128)(2,1)S(1)} %get-tuple-element.88.refs_0_), custom_call_target="tpu_custom_call" | custom-call | tf_op jit(solution)/shard_map/line_gather/pallas_call | solution.py:401
  575.4 2.5 fusion.35
  580.0 1.6 multiply_reduce_fusion
  586.5 5.5 line_total.3
  594.3 2.6 convolution_convert_fusion.3
  596.9 5.4 collective-permute-done.4
  602.8 3.1 fusion.31
  607.3 2.7 collective-permute-start.7
  610.7 4.7 fusion.11
  615.4 5.4 convolution_convert_fusion.1
  621.4 121.4 %finish_sums.1 = (bf16[16,128,512]{2,1,0:T(8,128)(2,1)}, bf16[16,128,512]{2,1,0:T(8,128)(2,1)}, bf16[16,128,512]{2,1,0:T(8,128)(2,1)}, bf16[16,128,512]{2,1,0:T(...) custom-call(bf16[16,128,1536]{2,1,0:T(8,128)(2,1)} %bitcast.230, bf16[16,128,512]{2,1,0:T(8,128)(2,1)} %bitcast.232, ...), custom_call_target="tpu_custom_call" | custom-call | tf_op jit(solution)/shard_map/finish_sums/pallas_call | solution.py:980
  744.4 1.6 slice.134
  746.0 1.6 slice_bitcast_fusion.8
  747.6 1.7 multiply_reduce_fusion.1
  749.8 4.2 bitcast_convert_fusion.3
  754.0 2.7 bitcast_convert_fusion.2
  756.8 2.7 bitcast_convert_fusion.1
  759.5 2.7 bitcast_convert_fusion
  762.2 5.3 copy.76
  767.6 2.8 add_convert_fusion.5
  770.4 2.7 fusion.44
  (239 shorter events, 41.0 us)
Async XLA Ops:
  7.2 274.4 %copy-start = (bf16[2,256,2048]{2,1,0:T(8,128)(2,1)S(1)}, bf16[2,256,2048]{2,1,0:T(8,128)(2,1)}, u32[]{:S(2)}) copy-start(bf16[2,256,2048]{2,1,0:T(8,128)(2,1)} %param.30) | copy-start | bytes 6291460
  7.2 274.4 %all-gather.2.cloned.1.call-start = ((), (), s32[]{:S(2)}) async-start(), calls=%async_computation | async-start | bytes 17301504 | tf_op jit(solution)/shard_map/all_gather | solution.py:1365
  8.6 41.2 %copy-start.56 = (f32[128]{0:T(128)}, f32[128]{0:T(128)S(1)}, u32[]{:S(2)}) copy-start(f32[128]{0:T(128)S(1)} %add_rsqrt_fusion.3) | copy-start | bytes 1540
  51.2 691.6 %all-reduce.3.cloned.1.call-start = ((), (), s32[]{:S(2)}) async-start(), calls=%async_computation.1 | async-start | bytes 393216 | tf_op jit(solution)/shard_map/psum | solution.py:1419
  55.1 8.6 %copy-start.15 = (f32[512,512]{0,1:T(8,128)}, f32[512,512]{0,1:T(8,128)S(1)}, u32[]{:S(2)}) copy-start(f32[512,512]{0,1:T(8,128)S(1)} %get-tuple-element.153) | copy-start | bytes 3145732
  55.1 8.4 %copy-start.55 = (s32[1,512]{1,0:T(1,128)S(1)}, s32[1,512]{1,0:T(1,128)}, u32[]{:S(2)}) copy-start(s32[1,512]{1,0:T(1,128)} %param.17) | copy-start | bytes 6148
  55.1 8.6 %copy-start.51 = (f32[512]{0:T(512)S(1)}, f32[512]{0:T(512)}, u32[]{:S(2)}) copy-start(f32[512]{0:T(512)} %param.23) | copy-start | bytes 6148
  55.1 8.8 %copy-start.53 = (f32[512]{0:T(512)S(1)}, f32[512]{0:T(512)}, u32[]{:S(2)}) copy-start(f32[512]{0:T(512)} %param.24) | copy-start | bytes 6148
  56.4 7.9 %copy-start.13 = (f32[512,512]{0,1:T(8,128)}, f32[512,512]{0,1:T(8,128)S(1)}, u32[]{:S(2)}) copy-start(f32[512,512]{0,1:T(8,128)S(1)} %get-tuple-element.151) | copy-start | bytes 3145732
  63.7 4.6 copy-start.21
  70.5 59.0 %copy-start.12 = (bf16[128,2048]{1,0:T(8,128)(2,1)S(1)}, bf16[128,2048]{1,0:T(8,128)(2,1)}, u32[]{:S(2)}) copy-start(bf16[128,2048]{1,0:T(8,128)(2,1)} %param.16) | copy-start | bytes 1572868
  71.9 58.0 %copy-start.42 = (f32[2048]{0:T(1024)S(1)}, f32[2048]{0:T(1024)}, u32[]{:S(2)}) copy-start(f32[2048]{0:T(1024)} %param.26) | copy-start | bytes 24580
  71.9 58.1 %copy-start.40 = (bf16[2048,16]{0,1:T(8,128)(2,1)S(1)}, bf16[2048,16]{0,1:T(8,128)(2,1)}, u32[]{:S(2)}) copy-start(bf16[2048,16]{0,1:T(8,128)(2,1)} %param.27) | copy-start | bytes 196612
  71.9 58.4 %copy-start.60 = (s32[128,8]{0,1:T(8,128)S(1)}, s32[128,8]{0,1:T(8,128)}, u32[]{:S(2)}) copy-start(s32[128,8]{0,1:T(8,128)} %param.18) | copy-start | bytes 12292
  248.8 5.8 copy-start.6
  461.9 47.2 %collective-permute-start = (bf16[2048,2048]{1,0:T(8,128)(2,1)}, bf16[2048,2048]{1,0:T(8,128)(2,1)}, u32[]{:S(2)}, u32[]{:S(2)}) collective-permute-start(bf16[2048,2048]{1,0:T(8,128)(2,1)} %convolution_convert_fusion.2), channel_id=1, source_target_pairs={{0,4},{4,0},{8,12},{12,8},{16,20},{20,16},{24,28},{28,24},{1,5},{5... | collective-permute-start | bytes 25165832 | tf_op jit(solution)/shard_map/ppermute | solution.py:1015
  484.3 12.5 %slice-start.2 = ((s8[16777216]{0:T(1024)(128)(4,1)}), s8[4194304]{0:T(1024)(128)(4,1)S(1)}, s32[]{:S(2)}) async-start(s8[16777216]{0:T(1024)(128)(4,1)} %bitcast.222), calls=%async_computation.4 | async-start | bytes 8388608
  484.4 12.5 %slice-start.3 = ((s8[16777216]{0:T(1024)(128)(4,1)}), s8[4194304]{0:T(1024)(128)(4,1)S(1)}, s32[]{:S(2)}) async-start(s8[16777216]{0:T(1024)(128)(4,1)} %bitcast.222), calls=%async_computation.5 | async-start | bytes 8388608
  487.8 9.1 %slice-start.4 = ((s8[16777216]{0:T(1024)(128)(4,1)}), s8[4194304]{0:T(1024)(128)(4,1)S(1)}, s32[]{:S(2)}) async-start(s8[16777216]{0:T(1024)(128)(4,1)} %bitcast.222), calls=%async_computation.6 | async-start | bytes 8388608
  487.8 9.1 %slice-start.5 = ((s8[16777216]{0:T(1024)(128)(4,1)}), s8[4194304]{0:T(1024)(128)(4,1)S(1)}, s32[]{:S(2)}) async-start(s8[16777216]{0:T(1024)(128)(4,1)} %bitcast.222), calls=%async_computation.7 | async-start | bytes 8388608
  516.6 4.4 copy-start.9
  518.2 6.3 copy-start.2
  518.2 6.5 copy-start.20
  522.5 51.4 %collective-permute-start.1 = (bf16[2,2,128,2048]{3,2,1,0:T(8,128)(2,1)}, bf16[2,2,128,2048]{3,2,1,0:T(8,128)(2,1)}, u32[]{:S(2)}, u32[]{:S(2)}) collective-permute-start(bf16[2,2,128,2048]{3,2,1,0:T(8,128)(2,1)} %pad_maximum_fusion.6), channel_id=1, source_target_pairs={{0,8},{4,12},{8,0},{12,4},{16,24},{20,28},{24,16},{28,20},{1,9},{5... | collective-permute-start | bytes 6291464 | tf_op jit(solution)/shard_map/ppermute | solution.py:1015
  523.1 50.9 %collective-permute-start.2 = (bf16[2,2,128,2048]{3,2,1,0:T(8,128)(2,1)}, bf16[2,2,128,2048]{3,2,1,0:T(8,128)(2,1)}, u32[]{:S(2)}, u32[]{:S(2)}) collective-permute-start(bf16[2,2,128,2048]{3,2,1,0:T(8,128)(2,1)} %stack.60), channel_id=1, source_target_pairs={{0,16},{4,20},{8,24},{12,28},{16,0},{20,4},{24,8},{28,12},{1,17},{... | collective-permute-start | bytes 6291464 | tf_op jit(solution)/shard_map/ppermute | solution.py:1015
  532.8 41.1 %copy-start.63 = (bf16[512,2048]{1,0:T(8,128)(2,1)S(1)}, bf16[512,2048]{1,0:T(8,128)(2,1)}, u32[]{:S(2)}) copy-start(bf16[512,2048]{1,0:T(8,128)(2,1)} %param.25) | copy-start | bytes 6291460
  532.9 42.4 %slice-start = ((s8[8388608]{0:T(1024)(128)(4,1)}), s8[4194304]{0:T(1024)(128)(4,1)S(1)}, s32[]{:S(2)}) async-start(s8[8388608]{0:T(1024)(128)(4,1)} %bitcast.218), calls=%async_computation.2 | async-start | bytes 8388608
  536.1 39.2 %slice-start.1 = ((s8[8388608]{0:T(1024)(128)(4,1)}), s8[4194304]{0:T(1024)(128)(4,1)S(1)}, s32[]{:S(2)}) async-start(s8[8388608]{0:T(1024)(128)(4,1)} %bitcast.218), calls=%async_computation.3 | async-start | bytes 8388608
  575.3 6.4 copy-start.38
  575.3 4.7 copy-start.8
  575.3 4.7 copy-start.22
  575.3 4.7 copy-start.37
  575.3 4.7 copy-start.46
  577.9 24.4 %collective-permute-start.4 = (bf16[2,128,2048]{2,1,0:T(8,128)(2,1)S(1)}, bf16[2,128,2048]{2,1,0:T(8,128)(2,1)S(1)}, u32[]{:S(2)}, u32[]{:S(2)}) collective-permute-start(bf16[2,128,2048]{2,1,0:T(8,128)(2,1)S(1)} %get-tuple-element.101), channel_id=1, source_target_pairs={{0,8},{4,12},{8,0},{12,4},{16,24},{20,28},{24,16},{28,20},{1,9},{5... | collective-permute-start | bytes 3145736 | tf_op jit(solution)/shard_map/ppermute | solution.py:1015
  578.7 24.1 %collective-permute-start.3 = (bf16[2,128,2048]{2,1,0:T(8,128)(2,1)S(1)}, bf16[2,128,2048]{2,1,0:T(8,128)(2,1)}, u32[]{:S(2)}, u32[]{:S(2)}) collective-permute-start(bf16[2,128,2048]{2,1,0:T(8,128)(2,1)S(1)} %get-tuple-element.102), channel_id=1, source_target_pairs={{0,16},{4,20},{8,24},{12,28},{16,0},{20,4},{24,8},{28,12},{1,17},{... | collective-permute-start | bytes 3145736 | tf_op jit(solution)/shard_map/ppermute | solution.py:1015
  586.1 6.5 copy-start.61
  586.1 6.6 copy-start.39
  605.9 4.8 copy-start.65
  605.9 4.8 copy-start.67
  605.9 4.8 copy-start.68
  606.1 3.9 copy-start.17
  607.3 135.5 %collective-permute-start.7 = (bf16[128,2048]{1,0:T(8,128)(2,1)}, bf16[128,2048]{1,0:T(8,128)(2,1)}, u32[]{:S(2)}, u32[]{:S(2)}) collective-permute-start(bf16[128,2048]{1,0:T(8,128)(2,1)} %get-tuple-element.113), channel_id=1, source_target_pairs={{0,3},{1,0},{2,1},{3,2},{4,7},{5,4},{6,5},{7,6},{8,11},{9,8},{10,9... | collective-permute-start | bytes 1572872 | tf_op jit(solution)/shard_map/ppermute | solution.py:1058
  610.0 132.8 %collective-permute-start.6 = (bf16[128,2048]{1,0:T(8,128)(2,1)}, bf16[128,2048]{1,0:T(8,128)(2,1)}, u32[]{:S(2)}, u32[]{:S(2)}) collective-permute-start(bf16[128,2048]{1,0:T(8,128)(2,1)} %get-tuple-element.114), channel_id=1, source_target_pairs={{0,2},{1,3},{2,0},{3,1},{4,6},{5,7},{6,4},{7,5},{8,10},{9,11},{10,... | collective-permute-start | bytes 1572872 | tf_op jit(solution)/shard_map/ppermute | solution.py:1058
  610.0 5.3 copy-start.5
  610.0 132.8 %collective-permute-start.5 = (bf16[128,2048]{1,0:T(8,128)(2,1)}, bf16[128,2048]{1,0:T(8,128)(2,1)}, u32[]{:S(2)}, u32[]{:S(2)}) collective-permute-start(bf16[128,2048]{1,0:T(8,128)(2,1)} %get-tuple-element.115), channel_id=1, source_target_pairs={{0,1},{1,2},{2,3},{3,0},{4,5},{5,6},{6,7},{7,4},{8,9},{9,10},{10,1... | collective-permute-start | bytes 1572872 | tf_op jit(solution)/shard_map/ppermute | solution.py:1058
  621.4 126.2 %copy-start.44 = (f32[2048]{0:T(1024)S(1)}, f32[2048]{0:T(1024)}, u32[]{:S(2)}) copy-start(f32[2048]{0:T(1024)} %param.19) | copy-start | bytes 24580
  621.4 126.2 %copy-start.57 = (f32[128]{0:T(128)S(1)}, f32[128]{0:T(128)}, u32[]{:S(2)}) copy-start(f32[128]{0:T(128)} %copy-done.56) | copy-start | bytes 1540
  744.4 9.6 %copy-start.30 = (bf16[16,128,512]{2,1,0:T(8,128)(2,1)S(1)}, bf16[16,128,512]{2,1,0:T(8,128)(2,1)}, u32[]{:S(2)}) copy-start(bf16[16,128,512]{2,1,0:T(8,128)(2,1)} %get-tuple-element.77) | copy-start | bytes 6291460
  (39 other events, 72.7 us)
Sparse Core Ops, SparseCore 0:
  51.3 169.3 all-gather.1
  533.0 141.1 all-reduce.2

commit v4 on v3

--- a/solution.py
+++ b/solution.py
@@ -89,53 +89,57 @@
     )
 
 
-def gather_kernel(nz, x_ref, t_ref, out_ref, tags_ref, local_sem, sz, sx, sy, sda, sdb, sc, rz, rx, ry, rda, rdb, rc):
+def experts_kernel(nz, x_ref, t_ref, g_ref, wide_ref, down_ref, rows_ref, slopes_ref, gated_ref, tiles_ref, land, tags, g_buf, pre, back, gate_at, grad_at, local_sem, s_rows, s_g, sz, sx, sy, sda, sdb, sc, rz, rx, ry, rda, rdb, rc):
     dp, z = lax.axis_index("dp"), lax.axis_index("tensor")
-    half = x_ref.shape[0] // 2
-    greet(dp, z, nz)
+    count, width = x_ref.shape
+    half = count // 2
+    both = back.shape[1]
+    each = both // gate_at.shape[0]
+    other = (dp ^ 1, z)
 
     def rows_at(flip, zz):
-        return out_ref.at[(dp ^ flip) * nz + zz]
+        place = dp ^ flip
+        return land.at[place // 2, zz, pl.ds(pl.multiple_of((place % 2) * count, count), count)]
+
+    def half_at(flip, zz, k):
+        place = dp ^ flip
+        return land.at[place // 2, zz, pl.ds(pl.multiple_of((place % 2) * count + k * half, half), half)]
 
     def tags_at(flip, zz):
-        return tags_ref.at[(dp ^ flip) * nz + zz]
-
-    def whole(flip, zz, own, send, recv, device):
+        return tags.at[(dp ^ flip) * nz + zz]
+
+    def whole(flip, zz, send, recv, device):
         return (
-            remote(x_ref if own else rows_at(flip, zz), rows_at(flip, zz), send(0), recv(0), device),
-            remote(t_ref if own else tags_at(flip, zz), tags_at(flip, zz), send(1), recv(1), device),
+            remote(rows_at(flip, zz), rows_at(flip, zz), send(0), recv(0), device),
+            remote(tags_at(flip, zz), tags_at(flip, zz), send(1), recv(1), device),
         )
 
-    def z_copy(zz, step, own):
-        return whole(
-            0, zz, own, lambda k: sz.at[k, (step + 1) // 2, zz], lambda k: rz.at[k, zz], (dp, z + step)
-        )
-
-    def x_copy(zz, own):
-        return whole(0, zz, own, lambda k: sx.at[k, zz], lambda k: rx.at[k, zz], (dp ^ 2, z))
-
-    def y_copy(zz, own):
-        return whole(0, zz, own, lambda k: sy.at[k, zz], lambda k: ry.at[k, zz], (dp ^ 4, z))
+    def z_copy(zz, step):
+        return whole(0, zz, lambda k: sz.at[k, (step + 1) // 2, zz], lambda k: rz.at[k, zz], (dp, z + step))
+
+    def x_copy(zz):
+        return whole(0, zz, lambda k: sx.at[k, zz], lambda k: rx.at[k, zz], (dp ^ 2, z))
+
+    def y_copy(zz):
+        return whole(0, zz, lambda k: sy.at[k, zz], lambda k: ry.at[k, zz], (dp ^ 4, z))
 
     def a_copy(zz):
-        ref = rows_at(4, zz).at[pl.ds(0, half)]
         return (
-            remote(ref, ref, sda.at[0, zz], rda.at[0, zz], (dp ^ 2, z)),
+            remote(half_at(4, zz, 0), half_at(4, zz, 0), sda.at[0, zz], rda.at[0, zz], (dp ^ 2, z)),
             remote(tags_at(4, zz), tags_at(4, zz), sda.at[1, zz], rda.at[1, zz], (dp ^ 2, z)),
         )
 
     def b_copy(zz):
-        ref = rows_at(2, zz).at[pl.ds(half, half)]
-        return (remote(ref, ref, sdb.at[zz], rdb.at[zz], (dp ^ 4, z)),)
-
-    def c_copy(kind, zz, own=False):
+        return (remote(half_at(2, zz, 1), half_at(2, zz, 1), sdb.at[zz], rdb.at[zz], (dp ^ 4, z)),)
+
+    def c_copy(kind, zz):
         send, recv = (lambda k: sc.at[k, kind, zz]), (lambda k: rc.at[k, kind, zz])
         if kind < 3:
-            return whole((0, 2, 4)[kind], zz, own, send, recv, (dp ^ 1, z))
-        ref = rows_at(6, zz).at[pl.ds((kind - 3) * half, half)]
-        copies = (remote(ref, ref, send(0), recv(0), (dp ^ 1, z)),)
+            return whole((0, 2, 4)[kind], zz, send, recv, other)
+        ref = half_at(6, zz, kind - 3)
+        copies = (remote(ref, ref, send(0), recv(0), other),)
         if kind == 3:
-            copies += (remote(tags_at(6, zz), tags_at(6, zz), send(1), recv(1), (dp ^ 1, z)),)
+            copies += (remote(tags_at(6, zz), tags_at(6, zz), send(1), recv(1), other),)
         return copies
 
     def start(copies):
@@ -143,44 +147,43 @@
             copy.start()
 
     def arrived(ref, sem):
-        remote(ref, ref, sem, sem, (dp ^ 1, z)).wait_recv()
+        remote(ref, ref, sem, sem, other).wait_recv()
 
     def both_arrived(flip, zz, recv):
         arrived(rows_at(flip, zz), recv(0))
         arrived(tags_at(flip, zz), recv(1))
 
-    def places(distance):
-        for sign in (0,) if distance == 0 else (-1, 1):
-            yield sign, z + sign * distance
+    def held(distance, zz, sign):
+        inside = (distance >= 0) & (distance < nz) & (zz >= 0) & (zz < nz)
+        return inside & ((distance > 0) | (sign > 0))
 
     def spread(distance):
-        for sign, zz in places(distance):
-            own = distance == 0
-
-            @pl.when((zz >= 0) & (zz < nz))
+        for sign in (1, -1):
+            zz = z + sign * distance
+
+            @pl.when(held(distance, zz, sign))
             def _():
-                if not own:
+                @pl.when(distance > 0)
+                def _():
                     both_arrived(0, zz, lambda k: rz.at[k, zz])
-                if sign <= 0:
-
-                    @pl.when(z < nz - 1)
-                    def _():
-                        start(z_copy(zz, 1, own))
-
-                if sign >= 0:
-
-                    @pl.when(z > 0)
-                    def _():
-                        start(z_copy(zz, -1, own))
-
-                start(x_copy(zz, own))
-                start(y_copy(zz, own))
-                start(c_copy(0, zz, own))
+
+                @pl.when((zz <= z) & (z < nz - 1))
+                def _():
+                    start(z_copy(zz, 1))
+
+                @pl.when((zz >= z) & (z > 0))
+                def _():
+                    start(z_copy(zz, -1))
+
+                start(x_copy(zz))
+                start(y_copy(zz))
+                start(c_copy(0, zz))
 
     def relay(distance):
-        for _, zz in places(distance):
-
-            @pl.when((zz >= 0) & (zz < nz))
+        for sign in (1, -1):
+            zz = z + sign * distance
+
+            @pl.when(held(distance, zz, sign))
             def _():
                 both_arrived(4, zz, lambda k: ry.at[k, zz])
                 start(a_copy(zz))
@@ -190,29 +193,125 @@
                 start(c_copy(1, zz))
 
     def corner(distance):
-        for _, zz in places(distance):
-
-            @pl.when((zz >= 0) & (zz < nz))
+        for sign in (1, -1):
+            zz = z + sign * distance
+
+            @pl.when(held(distance, zz, sign))
             def _():
-                arrived(rows_at(6, zz).at[pl.ds(0, half)], rda.at[0, zz])
+                arrived(half_at(6, zz, 0), rda.at[0, zz])
                 arrived(tags_at(6, zz), rda.at[1, zz])
                 start(c_copy(3, zz))
-                arrived(rows_at(6, zz).at[pl.ds(half, half)], rdb.at[zz])
+                arrived(half_at(6, zz, 1), rdb.at[zz])
                 start(c_copy(4, zz))
+
+    def store_rows(chip, zz):
+        return pltpu.make_async_copy(land.at[chip, zz], rows_ref.at[chip, zz], s_rows.at[chip, zz])
+
+    def load_g(chip, zz, c):
+        return pltpu.make_async_copy(
+            g_ref.at[(2 * chip + c) * nz + zz], g_buf.at[pl.ds(c * count, count)], s_g.at[c]
+        )
+
+    diagonal = (
+        lax.broadcasted_iota(jnp.int32, (count, count), 0) == lax.broadcasted_iota(jnp.int32, (count, count), 1)
+    ).astype(jnp.float32)
+
+    def experts(chip, zz):
+        store_rows(chip, zz).start()
+        for c in range(2):
+            load_g(chip, zz, c).start()
+        x = land.at[chip, zz]
+
+        def product(k, carry):
+            at = pl.ds(pl.multiple_of(k * 256, 256), 256)
+            pre[:, at] = jnp.dot(x[...], wide_ref[:, at], preferred_element_type=jnp.float32)
+            return carry
+
+        lax.fori_loop(0, 2 * both // 256, product, 0, unroll=True)
+        for j in range(gate_at.shape[0]):
+            for c in range(2):
+                row = tags[(2 * chip + c) * nz + zz, pl.ds(dp * gate_at.shape[0] + j, 1), :]
+                column = jnp.sum(diagonal * row, axis=1, keepdims=True)
+                gate_at[j, pl.ds(c * count, count), :] = jnp.broadcast_to(column, (count, 128))
+        for c in range(2):
+            load_g(chip, zz, c).wait()
+
+        def back_product(k, carry):
+            at = pl.ds(pl.multiple_of(k * 256, 256), 256)
+            back[:, at] = jnp.dot(g_buf[...], down_ref[:, at], preferred_element_type=jnp.float32)
+            return carry
+
+        lax.fori_loop(0, both // 256, back_product, 0, unroll=True)
+
+        def elementwise(k, carry):
+            at = pl.ds(pl.multiple_of(k * 64, 64), 64)
+            for j in range(gate_at.shape[0]):
+                cols, up_cols = pl.ds(j * each, each), pl.ds(both + j * each, each)
+                gate = jnp.concatenate([gate_at[j, at, :]] * (each // 128), axis=1)
+                gate_pre, up_pre, grad = pre[at, cols], pre[at, up_cols], back[at, cols]
+                sigmoid = 1.0 / (1.0 + jnp.exp(-gate_pre))
+                silu = gate_pre * sigmoid
+                hidden = silu * up_pre
+                gated_ref[chip, zz, at, cols] = (gate * hidden).astype(gated_ref.dtype)
+                share = jnp.sum(hidden * grad, axis=1, keepdims=True)
+                grad_at[j, at, :] = jnp.broadcast_to(share, (64, 128))
+                slope = gate * grad
+                slopes_ref[chip, zz, at, cols] = (
+                    slope * up_pre * sigmoid * (1.0 + gate_pre * (1.0 - sigmoid))
+                ).astype(slopes_ref.dtype)
+                slopes_ref[chip, zz, at, up_cols] = (slope * silu).astype(slopes_ref.dtype)
+            return carry
+
+        lax.fori_loop(0, 2 * count // 64, elementwise, 0)
+        for c in range(2):
+            shares = [
+                jnp.sum(diagonal * grad_at[j, pl.ds(c * count, count), :], axis=0, keepdims=True)
+                for j in range(gate_at.shape[0])
+            ]
+            shares.append(jnp.zeros((8 - len(shares), count), jnp.float32))
+            tiles_ref[(2 * chip + c) * nz + zz] = jnp.concatenate(shares, axis=0)
+
+    def job(step, k):
+        kind, sign = k // 2, 1 - 2 * (k % 2)
+        distance = step - 1 - (kind + 1) // 2
+        zz = z + sign * distance
+        flip = 2 * kind
+
+        @pl.when(held(distance, zz, sign))
+        def _():
+            @pl.when(kind < 3)
+            def _():
+                both_arrived(flip + 1, zz, lambda m: rc.at[m, kind, zz])
+
+            @pl.when(kind == 3)
+            def _():
+                arrived(half_at(7, zz, 0), rc.at[0, 3, zz])
+                arrived(tags_at(7, zz), rc.at[1, 3, zz])
+                arrived(half_at(7, zz, 1), rc.at[0, 4, zz])
+
+            experts((dp ^ flip) // 2, zz)
 
     keep = pltpu.make_async_copy(x_ref, rows_at(0, z), local_sem.at[0])
     keep_tags = pltpu.make_async_copy(t_ref, tags_at(0, z), local_sem.at[1])
     keep.start()
     keep_tags.start()
-    for step in range(nz + 2):
-        if step < nz:
-            spread(step)
-        if 0 <= step - 1 < nz:
-            relay(step - 1)
-        if 0 <= step - 2 < nz:
-            corner(step - 2)
+    greet(dp, z, nz)
     keep.wait()
     keep_tags.wait()
+
+    def step_body(step, carry):
+        spread(step)
+        relay(step - 1)
+        corner(step - 2)
+
+        def inner(k, inner_carry):
+            job(step, k)
+            return inner_carry
+
+        lax.fori_loop(0, 8, inner, 0)
+        return carry
+
+    lax.fori_loop(0, nz + 3, step_body, 0)
 
     def sent(copies):
         for copy in copies:
@@ -222,45 +321,59 @@
 
         @pl.when((zz <= z) & (z < nz - 1))
         def _():
-            sent(z_copy(zz, 1, False))
+            sent(z_copy(zz, 1))
 
         @pl.when((zz >= z) & (z > 0))
         def _():
-            sent(z_copy(zz, -1, False))
-
-        sent(x_copy(zz, False))
-        sent(y_copy(zz, False))
+            sent(z_copy(zz, -1))
+
+        sent(x_copy(zz))
+        sent(y_copy(zz))
         sent(a_copy(zz))
         sent(b_copy(zz))
         for kind in range(5):
             sent(c_copy(kind, zz))
-        for kind, flip in ((0, 1), (1, 3), (2, 5)):
-            both_arrived(flip, zz, lambda k: rc.at[k, kind, zz])
-        for kind in (3, 4):
-            arrived(rows_at(7, zz).at[pl.ds((kind - 3) * half, half)], rc.at[0, kind, zz])
-        arrived(tags_at(7, zz), rc.at[1, 3, zz])
-
-
-def gather_all(x, tags, nz, collective_id):
+        for chip in range(4):
+            store_rows(chip, zz).wait()
+
+
+def gather_experts(x, gates, cotangents, wide, down, experts_here, nz, collective_id):
     rows, width = x.shape
-    dma = pltpu.SemaphoreType.DMA
-    any_place, vmem = pl.BlockSpec(memory_space=pl.ANY), pl.BlockSpec(memory_space=pltpu.VMEM)
+    both = down.shape[1]
+    dma, vmem = pltpu.SemaphoreType.DMA, pl.BlockSpec(memory_space=pltpu.VMEM)
+    any_place = pl.BlockSpec(memory_space=pl.ANY)
+    group = (4, nz, 2 * rows)
+    flops = 2 * 8 * nz * rows * width * 3 * both
     return pl.pallas_call(
-        functools.partial(gather_kernel, nz),
-        name="gather_all",
+        functools.partial(experts_kernel, nz),
+        name="gather_experts",
         out_shape=(
-            jax.ShapeDtypeStruct((8 * nz, rows, width), x.dtype),
-            jax.ShapeDtypeStruct((8 * nz,) + tags.shape, tags.dtype),
+            jax.ShapeDtypeStruct(group + (width,), x.dtype),
+            jax.ShapeDtypeStruct(group + (2 * both,), x.dtype),
+            jax.ShapeDtypeStruct(group + (both,), x.dtype),
+            jax.ShapeDtypeStruct((8 * nz, 8, rows), jnp.float32),
         ),
-        in_specs=[vmem, vmem],
-        out_specs=(any_place, any_place),
-        scratch_shapes=[dma((2,))]
+        in_specs=[vmem, vmem, any_place, vmem, vmem],
+        out_specs=(any_place, vmem, vmem, vmem),
+        scratch_shapes=[
+            pltpu.VMEM(group + (width,), x.dtype),
+            pltpu.VMEM((8 * nz,) + gates.shape, gates.dtype),
+            pltpu.VMEM((2 * rows, width), x.dtype),
+            pltpu.VMEM((2 * rows, 2 * both), jnp.float32),
+            pltpu.VMEM((2 * rows, both), jnp.float32),
+            pltpu.VMEM((experts_here, 2 * rows, 128), jnp.float32),
+            pltpu.VMEM((experts_here, 2 * rows, 128), jnp.float32),
+            dma((2,)),
+            dma((4, nz)),
+            dma((2,)),
+        ]
         + [dma((2, 2, nz)), dma((2, nz)), dma((2, nz)), dma((2, nz)), dma((nz,)), dma((2, 5, nz))]
         + [dma((2, nz)), dma((2, nz)), dma((2, nz)), dma((2, nz)), dma((nz,)), dma((2, 5, nz))],
         compiler_params=pltpu.CompilerParams(
-            collective_id=collective_id, has_side_effects=True, vmem_limit_bytes=8 * 2**20
+            collective_id=collective_id, has_side_effects=True, vmem_limit_bytes=VMEM_LIMIT
         ),
-    )(x, tags)
+        cost_estimate=pl.CostEstimate(flops=flops, bytes_accessed=64 * 2**20, transcendentals=0),
+    )(x, gates, cotangents, wide, down)
 
 
 def greet_line(dp, z, nz):
@@ -595,16 +708,19 @@
             zz = jnp.where(z == zv, order[zv][i], zz)
         return zz
 
+    def block_of(place, zz):
+        return p_ref.at[(place // 2 * nz + zz) * 2 + place % 2]
+
     flips = (0, 2, 4, 6)
 
     def load(kind, zz):
         return pltpu.make_async_copy(
-            p_ref.at[(dp ^ flips[kind]) * nz + zz], acc.at[kind, zz], s_local.at[kind, zz]
+            block_of(dp ^ flips[kind], zz), acc.at[kind, zz], s_local.at[kind, zz]
         )
 
     def core_copy(kind, zz):
         return remote(
-            p_ref.at[(dp ^ flips[kind] ^ 1) * nz + zz], rc.at[kind, zz], s_core.at[kind, zz], r_core.at[kind, zz], (dp ^ 1, z)
+            block_of(dp ^ flips[kind] ^ 1, zz), rc.at[kind, zz], s_core.at[kind, zz], r_core.at[kind, zz], (dp ^ 1, z)
         )
 
     def a_copy(zz):
@@ -787,10 +903,11 @@
     )(p, tiles)
 
 
-def finish_kernel(nz, nc, g_ref, h_ref, p_ref, unit_ref, small_ref, sum_q, sum_k, sum_v, sum_o, out_ref, total_ref, buf, acc, rc, ra, rb, rx, ry, line_acc, up, down, *sems):
+def finish_kernel(nz, nc, g_ref, h_ref, p_ref, e_ref, unit_ref, small_ref, sum_q, sum_k, sum_v, sum_o, out_ref, routed_ref, total_ref, buf, acc, rc, ra, rb, rx, ry, line_acc, up, down, more_acc, more_got, *sems):
     (s_load, s_core, r_core, s_a, r_a, s_b, r_b, s_x, r_x, s_y, r_y) = sems[:11]
     (t_x, q_x, t_y, q_y, t_a, q_a, t_b, q_b, t_c, q_c) = sems[11:21]
     s_line, s_store, s_up, r_up, s_down, r_down = sems[21:27]
+    (s_load_more, s_more, r_more), sems = sems[27:30], sems[:27] + sems[30:]
     total = Total(nz, lax.axis_index("dp"), lax.axis_index("tensor"), *sems[27:])
     dp, z = lax.axis_index("dp"), lax.axis_index("tensor")
     rows = acc.shape[2]
@@ -915,6 +1032,8 @@
 
     line_load = pltpu.make_async_copy(p_ref, line_acc, s_line)
     line_load.start()
+    more_load = pltpu.make_async_copy(e_ref, more_acc, s_load_more)
+    more_load.start()
     for c in range(nc):
         for kind in (3, 1, 2, 0):
             for copy in loads(kind, c):
@@ -927,6 +1046,7 @@
     line = Line(nz, dp, z, line_acc, up, down, s_up, r_up, s_down, r_down)
     line_load.wait()
     line.first()
+
     def line_end():
         line.finish(out_ref)
         line.drain()
@@ -936,8 +1056,34 @@
         for k in range(out_ref.shape[1] // wide):
             total.got[0, k : k + 1, :] = share[:, k * wide : (k + 1) * wide]
 
-    side = [functools.partial(line.step, distance) for distance in range(1, nz - 1)] + [line_end]
-    side += [functools.partial(total.step, k, total_ref) for k in range(Total.steps)]
+    others = [lax.rem(z + turn, nz) for turn in range(1, nz)]
+    more = [
+        remote(more_acc.at[place], more_got.at[turn], s_more.at[turn], r_more.at[turn], (dp, place))
+        for turn, place in enumerate(others)
+    ]
+
+    def more_start():
+        more_load.wait()
+        for copy in more:
+            copy.start()
+
+    def more_end():
+        for copy in more:
+            copy.wait()
+
+        def body(k, carry):
+            at = pl.ds(k * CHUNK, CHUNK)
+            part = more_acc[z, at, :].astype(jnp.float32)
+            for turn in range(nz - 1):
+                part = part + more_got[turn, at, :].astype(jnp.float32)
+            routed_ref[at, :] = part
+            return carry
+
+        lax.fori_loop(0, routed_ref.shape[0] // CHUNK, body, 0)
+
+    side = [functools.partial(line.step, distance) for distance in range(1, nz - 1)] + [line_end, more_start]
+    late = [functools.partial(total.step, k, total_ref) for k in range(3)] + [more_end]
+    late += [functools.partial(total.step, k, total_ref) for k in range(3, Total.steps)]
     stages = (stage_diagonal, stage_side, stage_own, stage_relay, stage_corner)
     for i in range(nc + len(stages) - 1):
         for lag, stage in enumerate(stages):
@@ -945,7 +1091,7 @@
                 stage(i - lag)
                 if i >= 1 and side:
                     side.pop(0)()
-    for one in side:
+    for one in side + late:
         one()
     for c in range(nc):
         for kind, flip in ((0, 1), (1, 3), (2, 5)):
@@ -971,7 +1117,7 @@
         store.wait()
 
 
-def finish_sums(g, h, p, unit, small, nz, nc, collective_id):
+def finish_sums(g, h, p, e, unit, small, nz, nc, collective_id):
     _, rows, width = g.shape
     width += h.shape[2]
     _, line_rows, line_width = p.shape
@@ -982,28 +1128,30 @@
         name="finish_sums",
         out_shape=(
             *[jax.ShapeDtypeStruct(g.shape[:2] + (width // 4,), g.dtype)] * 4,
-            jax.ShapeDtypeStruct((line_rows, line_width), jnp.float32),
+            *[jax.ShapeDtypeStruct((line_rows, line_width), jnp.float32)] * 2,
             jax.ShapeDtypeStruct(small.shape, small.dtype),
         ),
-        in_specs=[pl.BlockSpec(memory_space=pl.ANY)] * 3 + [pl.BlockSpec(memory_space=pltpu.VMEM)] * 2,
+        in_specs=[pl.BlockSpec(memory_space=pl.ANY)] * 4 + [pl.BlockSpec(memory_space=pltpu.VMEM)] * 2,
         out_specs=(
             *[pl.BlockSpec(memory_space=pl.ANY)] * 4,
-            *[pl.BlockSpec(memory_space=pltpu.VMEM)] * 2,
+            *[pl.BlockSpec(memory_space=pltpu.VMEM)] * 3,
         ),
         scratch_shapes=[vmem(g.shape[:2] + (width,)), vmem((4, nc, rows, width)), vmem((4, nc, rows, width))]
         + [vmem((nc, half, width)) for _ in range(2)]
         + [vmem((nc, rows, width)) for _ in range(2)]
-        + [vmem((nz, line_rows, line_width)) for _ in range(3)]
+        + [vmem((nz, line_rows, line_width)) for _ in range(4)]
+        + [vmem((nz - 1, line_rows, line_width))]
         + [dma((2, 4, nc)) for _ in range(3)]
         + [dma((nc,)) for _ in range(16)]
         + [dma((5, nc)), dma((5, nc))]
         + [dma(()), dma((4,))]
         + [dma((nz, PARTS)) for _ in range(4)]
+        + [dma(()), dma((nz - 1,)), dma((nz - 1,))]
         + total_scratch(nz, small.shape, small.dtype),
         compiler_params=pltpu.CompilerParams(
             collective_id=collective_id, has_side_effects=True, vmem_limit_bytes=VMEM_LIMIT
         ),
-    )(g, h, p, unit, small)
+    )(g, h, p, e, unit, small)
 
 
 class Spread:
@@ -1043,27 +1191,6 @@
 
     def column(self, sides):
         return jnp.concatenate([self.plus(self.low_own, sides[0]), self.plus(self.high_own, sides[1])])
-
-    def blocks(self, column):
-        z = lax.axis_index("tensor")
-        return tuple(
-            lax.dynamic_index_in_dim(column, (z + turn) % self.nz, axis=0, keepdims=False)
-            for turn in range(self.nz)
-        )
-
-    def line(self, blocks):
-        nz = self.nz
-        self.own = blocks[0]
-        return tuple(
-            lax.ppermute(blocks[turn], "tensor", [(i, (i + turn) % nz) for i in range(nz)])
-            for turn in range(1, nz)
-        )
-
-    def total(self, terms):
-        total = self.own.astype(jnp.float32)
-        for term in terms:
-            total = total + term.astype(jnp.float32)
-        return total
 
 
 def hold(first, second):
@@ -1238,22 +1365,24 @@
         jnp.dot(second_normalized, w_router, preferred_element_type=jnp.float32), axis=-1
     )
     gates = jnp.where(chosen, route_probs, 0.0).T
-    all_rows, all_gates = gather_all(second_normalized, gates, n_tensor, 0)
-    all_rows = all_rows.reshape(all_count, d_model)
 
     down_rows = w_down.reshape(exp_dev * width, d_model)
     wide = jnp.concatenate([w_gate[e] for e in range(exp_dev)] + [w_up[e] for e in range(exp_dev)], axis=1)
-    local_gate = lax.dynamic_slice_in_dim(all_gates, lax.axis_index("dp") * exp_dev, exp_dev, axis=1)
-    local_gate = local_gate.transpose(0, 2, 1).reshape(all_count, exp_dev)
-    spread = jnp.repeat(local_gate, width, axis=1)
     both = exp_dev * width
-    pre = jnp.dot(all_rows, wide, preferred_element_type=jnp.float32)
-    gate_pre, up_pre = pre[:, :both], pre[:, both:]
-    gate_sigmoid = jax.nn.sigmoid(gate_pre)
-    silu_gate = gate_pre * gate_sigmoid
-    hidden = silu_gate * up_pre
-    gated_hidden = (spread * hidden).astype(jnp.bfloat16)
-    lines = gated_hidden.reshape(n_dp, n_tensor * tok_count, both)
+    all_rows, grad_pre, gated, tiles = gather_experts(
+        second_normalized,
+        gates,
+        all_cotangents.reshape(devices, tok_count, d_model),
+        wide,
+        down_rows.T,
+        exp_dev,
+        n_tensor,
+        0,
+    )
+    all_rows, grad_pre = all_rows.reshape(all_count, d_model), grad_pre.reshape(all_count, 2 * both)
+    lines = gated.reshape(n_dp // 2, n_tensor, 2, tok_count, both).transpose(0, 2, 1, 3, 4)
+    gated_hidden = lines.reshape(all_count, both)
+    lines = lines.reshape(n_dp, n_tensor * tok_count, both)
 
     def out_rows(places):
         picked = [
@@ -1264,26 +1393,16 @@
             jnp.concatenate(picked), down_rows, preferred_element_type=jnp.float32
         ).astype(jnp.bfloat16)
 
-    back = jnp.einsum("td,fd->tf", all_cotangents, down_rows, preferred_element_type=jnp.float32)
-    gate_grads = jnp.sum((hidden * back).reshape(all_count, exp_dev, width), axis=-1)
-    grad_hidden = spread * back
-    grad_gate_pre = (
-        grad_hidden * up_pre * gate_sigmoid * (1.0 + gate_pre * (1.0 - gate_sigmoid))
-    ).astype(jnp.bfloat16)
-    grad_up_pre = (grad_hidden * silu_gate).astype(jnp.bfloat16)
-    grad_pre = jnp.concatenate([grad_gate_pre, grad_up_pre], axis=1)
     in_part = jnp.einsum("tf,df->td", grad_pre, wide, preferred_element_type=jnp.float32).astype(jnp.bfloat16)
     spread = Spread(n_tensor, (tok_count, d_model))
     partner_rows = out_rows((1, 3, 5, 7))
     in_part, partner_rows = hold(in_part, partner_rows)
-    theirs = spread.pair(out_rows((0, 2, 4, 6)), partner_rows)
-    tiles = gate_grads.reshape(devices, tok_count, exp_dev).transpose(0, 2, 1)
-    tiles = jnp.pad(tiles, ((0, 0), (0, 8 - exp_dev), (0, 0)))
     grad_in, gate_tiles = scatter_all(
         in_part.reshape(devices, tok_count, d_model), tiles, n_tensor, 1
     )
-    grad_in, theirs = hold(grad_in, theirs)
-    sides = spread.side(spread.sides(theirs))
+    grad_in, partner_rows = hold(grad_in, partner_rows)
+    theirs = spread.pair(out_rows((0, 2, 4, 6)), partner_rows)
+    sides = spread.sides(theirs)
     grad_down = jnp.einsum(
         "tf,td->fd", gated_hidden, all_cotangents, preferred_element_type=jnp.float32
     ).reshape(exp_dev, width, d_model)
@@ -1361,8 +1480,7 @@
     first_unit_rows = input_tensors * first_norm_scale
     first_normalized = (first_unit_rows * attention_norm_gain).astype(jnp.bfloat16)
     normed_all = line_gather(first_normalized, n_tensor, 2).reshape(seq_len, d_model)
-    normed_all, later_cotangent = lax.optimization_barrier((normed_all, grad_output))
-    all_cotangents = lax.all_gather(later_cotangent, ("dp", "tensor"), axis=0, tiled=True)
+    all_cotangents = lax.all_gather(grad_output, ("dp", "tensor"), axis=0, tiled=True)
     query_raw = jnp.dot(normed_all, w_query, preferred_element_type=jnp.float32)
     key_raw = jnp.dot(normed_all, w_key, preferred_element_type=jnp.float32)
     value_rows = (
@@ -1417,6 +1535,8 @@
     grad_attn = grad_hidden_one.astype(jnp.bfloat16)
     side_parts = jnp.concatenate([grad_router_part.T, grad_expert_share[None, :]])
     side_total = lax.psum(side_parts, ("dp", "tensor"))
+    grad_attn, sides = hold(grad_attn, sides)
+    sides = spread.side(sides)
     grad_attn_all = line_gather(grad_attn, n_tensor, 2)
     grad_attn_all, sides = hold(grad_attn_all, sides)
     sides = spread.last_side(sides)
@@ -1475,11 +1595,10 @@
     )
     grad_value_raw = grad_value_total.reshape(seq_len, local_dim).astype(jnp.bfloat16)
     grad_raw = jnp.concatenate([grad_query_raw, grad_key_raw, grad_value_raw], axis=1)
-    grad_raw, sides = hold(grad_raw, sides)
-    column = spread.column(sides)
     w_raw = jnp.concatenate([w_query, w_key, w_value], axis=1)
     raw_part = jnp.einsum("sd,sf->df", normed_all, grad_raw, preferred_element_type=jnp.float32)
     row_part = jnp.einsum("sf,df->sd", grad_raw, w_raw, preferred_element_type=jnp.float32)
+    column = spread.column(sides)
     mine = (jnp.arange(n_tensor) == lax.axis_index("tensor"))[:, None]
     gain_parts = jnp.stack(
         [
@@ -1489,20 +1608,19 @@
             jnp.zeros((d_model,), jnp.float32),
         ]
     )
-    gain_parts, column = hold(gain_parts, column)
-    terms = spread.line(spread.blocks(column))
     finished = finish_sums(
         raw_part.astype(jnp.bfloat16).reshape(n_dp * PIECES, -1, 3 * local_dim),
         grad_output_part.astype(jnp.bfloat16).reshape(n_dp * PIECES, -1, local_dim),
         row_part.astype(jnp.bfloat16).reshape(n_tensor, tok_count, d_model),
+        column,
         first_unit_rows,
         gain_parts.reshape(8, -1),
         n_tensor,
         PIECES,
         4,
     )
-    finished, (terms, side_total) = hold(finished, (terms, side_total))
-    total_query, total_key, total_value, total_output, grad_first_normalized, gain_totals = finished
+    finished, side_total = hold(finished, side_total)
+    total_query, total_key, total_value, total_output, grad_first_normalized, routed, gain_totals = finished
     total_router, total_ffn_gain = side_total[:-1].T, side_total[-1]
     total_query, total_key, total_value, total_output = (
         total.reshape(d_model, local_dim).astype(jnp.float32)
@@ -1519,7 +1637,7 @@
         )
         + grad_hidden_one
     ).astype(jnp.bfloat16)
-    result = (hidden_after_attention + spread.total(terms)).astype(jnp.bfloat16)
+    result = (hidden_after_attention + routed).astype(jnp.bfloat16)
     gain_totals = gain_totals.reshape(4, d_model)
     total_attn_gain = gain_totals[0]
     own_gains = lax.dynamic_slice_in_dim(

time: 787 us -> 733 us (0.931)
  matrix products: 154 us -> 114 us
  Pallas kernels: 477 us -> 493 us
  other arithmetic: 65.2 us -> 51.5 us
  local copies, waits for them, and re-layouts: 55.1 us -> 43.2 us
    dot_general x2 -> x0, matrix products: 47.1 us -> none  [the longest x1 24.7 us: experts_dense(): jnp.einsum('td,fd->tf', all_cotangents, down_rows, preferred_element_type...]
    pallas_call x2, Pallas kernels: 76.8 us -> 109 us  [line_gather(): pl.pallas_call(kernel, name='line_gather', out_shape=blocks, in_specs=[vm...]
    pallas_call x1, Pallas kernels: 121 us -> 106 us  [finish_sums(): pl.pallas_call(functools.partial(finish_kernel, nz, nc), name='finish_sum...]
    pallas_call x1, Pallas kernels: 118 us -> 105 us  [gather_experts(): pl.pallas_call(functools.partial(experts_kernel, nz), name='gather_expert...]
    pallas_call x1, Pallas kernels: 92.6 us -> 103 us  [scatter_all(): pl.pallas_call(functools.partial(scatter_kernel, nz), name='scatter_all',...]
    reduce_sum x1 -> x0, other arithmetic: 9.43 us -> none  [experts_dense(): jnp.sum((hidden * back).reshape(all_count, exp_dev, width), axis=-1)]
    reshape x2, local copies, waits for them, and re-layouts: 15 us -> 6.55 us  [the longest x1 3.93 us: experts_dense(): down_rows = w_down.reshape(exp_dev * width, d_model)]
    unnamed x158 -> x152, local copies, waits for them, and re-layouts: 16.5 us -> 17.1 us
  transfers between devices with their start and end apart: 10 -> 7, of which waited for: 2 -> 0; matrix products, arithmetic and copies ran while one was open for 16% -> 18% of each run, Pallas kernels for 44% -> 39%
where the time goes in v4:
time: 733 us; the launch traced here: 722 us
  Pallas kernels  493 us (67%)
  matrix products  114 us (16%)
  other arithmetic  51.5 us (7%)
  local copies, waits for them, and re-layouts  43.2 us (6%)
  between operations  15.7 us (2%)
    pallas_call x2, Pallas kernels, line_gather(): pl.pallas_call(kernel, name='line_gather', out_shape=blocks, in_specs=[vm...  109 us
    pallas_call x1, Pallas kernels, finish_sums(): pl.pallas_call(functools.partial(finish_kernel, nz, nc), name='finish_sum...  106 us
    pallas_call x1, Pallas kernels, gather_experts(): pl.pallas_call(functools.partial(experts_kernel, nz), name='gather_expert...  105 us
    pallas_call x1, Pallas kernels, scatter_all(): pl.pallas_call(functools.partial(scatter_kernel, nz), name='scatter_all',...  103 us
    pallas_call x1, Pallas kernels, line_scatter(): pl.pallas_call(functools.partial(line_scatter_kernel, nz), name='line_sca...  58.5 us
    dot_general x1, matrix products, experts_dense(): jnp.einsum('tf,df->td', grad_pre, wide, preferred_element_type=jnp.float32)  23.7 us
    dot_general x1, matrix products, experts_dense(): jnp.einsum('td,tf->df', all_rows, grad_pre, preferred_element_type=jnp.fl...  22.6 us
    dot_general x2, matrix products, out_rows(): jnp.dot(jnp.concatenate(picked), down_rows, preferred_element_type=jnp.fl...  18.7 us
  transfers between devices with their start and end apart: 7, of which 0 were waited for; matrix products, arithmetic and copies ran while one was open for 18% of the time, Pallas kernels for 39%

profile of v4, /device:TPU:0, one launch (start us, length us, event | category | flops | bytes accessed | tf_op | source)
XLA Modules:
  0.0 722.1 jit_solution(5163986872683084790)
XLA Ops:
  8.0 1.4 fusion.29
  9.4 2.2 convert_multiply_fusion
  11.6 72.7 %line_gather.2 = bf16[4,128,2048]{2,1,0:T(8,128)(2,1)S(1)} custom-call(bf16[128,2048]{1,0:T(8,128)(2,1)S(1)} %get-tuple-element.117.refs_0_), custom_call_target="tpu_custom_call" | custom-call | tf_op jit(solution)/shard_map/line_gather/pallas_call | solution.py:514
  84.4 2.3 multiply_reduce_fusion.8
  86.8 1.3 multiply_reduce_fusion.7
  88.2 5.6 line_total.2
  93.9 3.9 copy.79
  99.6 1.5 multiply_multiply_fusion.1
  104.2 2.1 copy-done.65
  107.7 1.4 convolution_convert_fusion.8
  110.4 58.5 %line_scatter.1 = f32[128,2048]{1,0:T(8,128)S(1)} custom-call(bf16[4,128,2048]{2,1,0:T(8,128)(2,1)S(1)} %bitcast.195), custom_call_target="tpu_custom_call" | custom-call | tf_op jit(solution)/shard_map/line_scatter/pallas_call | solution.py:680
  168.9 1.4 multiply_reduce_fusion.6
  174.8 2.3 pad_maximum_fusion.wide_ref
  177.1 105.0 %gather_experts.1 = (bf16[4,4,256,2048]{3,2,1,0:T(8,128)(2,1)}, bf16[4,4,256,1024]{3,2,1,0:T(8,128)(2,1)}, bf16[4,4,256,512]{3,2,1,0:T(8,128)(2,1)}, f32[32,8,128]{2,1,0:T(8,128)}) custom-call(bf16[128,2048]{1,0:T(8,128)(2,1)} %copy-done.17, f32[16,128]{1,0:T(8,128)} %select_bitcast_fusion.2.t_ref, bf16[32,128,2048]{2,1,0:T(8,128)(2,1)} %bitcast.243, ...), custom_call_target="tpu_custom_call" | custom-call | flops 25769803776 | bytes 67108864 | tf_op jit(solution)/shard_map/gather_experts/pallas_call | solution.py:347
  282.1 2.6 copy.60
  285.2 23.7 %convolution_convert_fusion = bf16[4096,2048]{1,0:T(8,128)(2,1)} fusion(bf16[4096,1024]{1,0:T(8,128)(2,1)} %bitcast.244, bf16[2048,256]{1,0:T(8,128)(2,1)S(1)} %copy-done.27, bf16[2048,256]{1,0:T(8,128)(2,1)S(1)} %copy-done.25, bf16[2048,256]{1,0:T(8,128)(2,1)S(1)} %copy-done.29, bf16[2048,256]{1,0:T(8,128)(2,1)} %copy-done.30), kind=kOutput, calls=%fused_computation.3 | convolution fusion | flops 17205035008 | bytes 29360128 | tf_op jit(solution)/shard_map/tf,df->td/dot_general | solution.py:1396
  308.9 1.4 dynamic-slice_bitcast_fusion.3
  311.3 9.6 %convolution_convert_fusion.2 = bf16[2048,2048]{1,0:T(8,128)(2,1)} fusion(bf16[512,2048]{1,0:T(8,128)(2,1)S(1)} %bitcast.213, bf16[512,512]{1,0:T(8,128)(2,1)S(1)} %get-tuple-element.98, bf16[512,512]{1,0:T(8,128)(2,1)S(1)} %get-tuple-element.99, bf16[512,512]{1,0:T(8,128)(2,1)S(1)} %get-tuple-element.100, bf16[512,512]{1,0:T(8,128)(2,1)S(1)} %get-tuple-element.101), kind=kOutput, calls=%fused_computation.5 | convolution fusion | flops 4307550208 | bytes 12582912 | tf_op jit(solution)/shard_map/dot_general | solution.py:1392
  320.9 102.8 %scatter_all.1 = (f32[128,2048]{1,0:T(8,128)}, f32[32,8,128]{2,1,0:T(8,128)}) custom-call(bf16[32,128,2048]{2,1,0:T(8,128)(2,1)} %bitcast.198, f32[32,8,128]{2,1,0:T(8,128)} %get-tuple-element.48.t_ref), custom_call_target="tpu_custom_call" | custom-call | tf_op jit(solution)/shard_map/scatter_all/pallas_call | solution.py:885
  423.8 6.4 copy.80
  432.4 2.7 multiply_reduce_fusion.2
  435.8 22.6 %convolution_bitcast_fusion = f32[2048,1024]{1,0:T(8,128)S(1)} fusion(bf16[4,4,256,2048]{3,2,1,0:T(8,128)(2,1)} %get-tuple-element.75, bf16[4,4,256,1024]{3,2,1,0:T(8,128)(2,1)} %get-tuple-element.45), kind=kOutput, calls=%fused_computation.12 | convolution fusion | flops 17179869184 | bytes 33554432 | tf_op jit(solution)/shard_map/td,tf->df/dot_general | solution.py:1409
  459.0 2.3 pad_maximum_fusion.2
  461.3 2.3 pad_maximum_fusion.1
  463.9 9.1 %add_convert_fusion = bf16[2048,2048]{1,0:T(8,128)(2,1)S(1)} fusion(bf16[2048,2048]{1,0:T(8,128)(2,1)} %collective-permute-done, bf16[512,2048]{1,0:T(8,128)(2,1)} %bitcast.212, bf16[512,512]{1,0:T(8,128)(2,1)} %get-tuple-element.95, bf16[512,512]{1,0:T(8,128)(2,1)} %get-tuple-element.96, bf16[512,512]{1,0:T(8,128)(2,1)} %get-tuple-element.97, ...), kind=kOutput, calls=%fused_computation.2 | convolution fusion | flops 4324327424 | bytes 20971520 | tf_op jit(solution)/shard_map/dot_general | solution.py:1392
  473.3 3.9 copy-done.14
  479.6 13.9 %fusion = f32[2,256,2048]{2,1,0:T(8,128)} fusion(bf16[2,256,4096]{2,1,0:T(8,128)(2,1)S(1)} %bitcast.208, bf16[4096,2048]{1,0:T(8,128)(2,1)} %all-gather.2.cloned.1.call-done), kind=kOutput, calls=%fused_computation | convolution fusion | flops 8589934592 | bytes 25165824 | tf_op jit(solution)/shard_map/tf,td->fd/dot_general | solution.py:1406
  493.4 36.6 %line_gather.3 = bf16[4,128,2048]{2,1,0:T(8,128)(2,1)S(1)} custom-call(bf16[128,2048]{1,0:T(8,128)(2,1)S(1)} %fusion.52.refs_0_), custom_call_target="tpu_custom_call" | custom-call | tf_op jit(solution)/shard_map/line_gather/pallas_call | solution.py:514
  532.6 1.8 copy-done.6
  534.5 2.2 convolution_convert_fusion.7
  536.6 1.6 multiply_reduce_fusion
  538.3 3.9 fusion.31
  548.9 5.5 line_total.3
  557.4 8.6 %convolution_convert_fusion.1 = bf16[2048,1536]{1,0:T(8,128)(2,1)} fusion(bf16[512,2048]{1,0:T(8,128)(2,1)} %bitcast.191, bf16[512,512]{0,1:T(8,128)(2,1)} %bitcast.247, bf16[512,512]{0,1:T(8,128)(2,1)} %multiply_convert_fusion.1, bf16[512,512]{0,1:T(8,128)(2,1)} %multiply_convert_fusion.2), kind=kOutput, calls=%fused_computation.4 | convolution fusion | flops 3229089792 | bytes 9961472 | tf_op jit(solution)/shard_map/sd,sf->df/dot_general | solution.py:1599
  566.0 2.6 convolution_convert_fusion.3
  570.0 4.8 fusion.9
  574.8 3.4 fusion.28
  578.2 1.5 pad_maximum_fusion.4.e_ref
  579.7 106.0 %finish_sums.1 = (bf16[16,128,512]{2,1,0:T(8,128)(2,1)}, bf16[16,128,512]{2,1,0:T(8,128)(2,1)}, bf16[16,128,512]{2,1,0:T(8,128)(2,1)}, bf16[16,128,512]{2,1,0:T(...) custom-call(bf16[16,128,1536]{2,1,0:T(8,128)(2,1)} %bitcast.207, ...), custom_call_target="tpu_custom_call" | custom-call | tf_op jit(solution)/shard_map/finish_sums/pallas_call | solution.py:1126
  687.3 1.6 slice.126
  688.9 1.6 slice_bitcast_fusion.8
  690.5 1.7 multiply_reduce_fusion.1
  692.7 4.2 bitcast_convert_fusion.3
  696.9 2.7 bitcast_convert_fusion.2
  699.7 2.7 bitcast_convert_fusion.1
  702.4 2.7 bitcast_convert_fusion
  705.2 5.3 copy.66
  710.5 3.6 add_convert_fusion.5
  (219 shorter events, 36.8 us)
Async XLA Ops:
  7.2 101.9 %copy-start = (bf16[512,2048]{1,0:T(8,128)(2,1)S(1)}, bf16[512,2048]{1,0:T(8,128)(2,1)}, u32[]{:S(2)}) copy-start(bf16[512,2048]{1,0:T(8,128)(2,1)} %param.25) | copy-start | bytes 6291460
  7.2 169.9 %all-gather.2.cloned.1.call-start = ((), (), s32[]{:S(2)}) async-start(), calls=%async_computation | async-start | bytes 17301504 | tf_op jit(solution)/shard_map/all_gather | solution.py:1483
  7.9 677.8 %all-reduce.2.cloned.1.call-start = ((), (), s32[]{:S(2)}) async-start(), calls=%async_computation.1 | async-start | bytes 393216 | tf_op jit(solution)/shard_map/psum | solution.py:1537
  8.0 76.3 %copy-start.69 = (bf16[2048,512]{1,0:T(8,128)(2,1)S(1)}, bf16[2048,512]{1,0:T(8,128)(2,1)}, u32[]{:S(2)}) copy-start(bf16[2048,512]{1,0:T(8,128)(2,1)} %param.20) | copy-start | bytes 6291460
  9.4 74.9 %copy-start.62 = (f32[128]{0:T(128)}, f32[128]{0:T(128)S(1)}, u32[]{:S(2)}) copy-start(f32[128]{0:T(128)S(1)} %add_rsqrt_fusion.3) | copy-start | bytes 1540
  88.2 13.1 %copy-start.10 = (f32[512,512]{0,1:T(8,128)}, f32[512,512]{0,1:T(8,128)S(1)}, u32[]{:S(2)}) copy-start(f32[512,512]{0,1:T(8,128)S(1)} %get-tuple-element.139) | copy-start | bytes 3145732
  88.2 11.1 %copy-start.61 = (s32[1,512]{1,0:T(1,128)S(1)}, s32[1,512]{1,0:T(1,128)}, u32[]{:S(2)}) copy-start(s32[1,512]{1,0:T(1,128)} %param.17) | copy-start | bytes 6148
  88.2 11.4 %copy-start.57 = (f32[512]{0:T(512)S(1)}, f32[512]{0:T(512)}, u32[]{:S(2)}) copy-start(f32[512]{0:T(512)} %param.23) | copy-start | bytes 6148
  88.2 12.9 %copy-start.59 = (f32[512]{0:T(512)S(1)}, f32[512]{0:T(512)}, u32[]{:S(2)}) copy-start(f32[512]{0:T(512)} %param.24) | copy-start | bytes 6148
  99.5 8.1 %copy-start.15 = (pred[512,512]{0,1:T(8,128)(4,1)}, pred[512,512]{0,1:T(8,128)(4,1)S(1)}, u32[]{:S(2)}) copy-start(pred[512,512]{0,1:T(8,128)(4,1)S(1)} %fusion.40) | copy-start | bytes 786436
  102.2 4.1 copy-start.65
  103.2 4.4 copy-start.5
  107.6 2.7 copy-start.43
  110.3 61.0 %copy-start.49 = (f32[2048]{0:T(1024)S(1)}, f32[2048]{0:T(1024)}, u32[]{:S(2)}) copy-start(f32[2048]{0:T(1024)} %param.26) | copy-start | bytes 24580
  110.4 61.1 %copy-start.48 = (bf16[2048,16]{0,1:T(8,128)(2,1)S(1)}, bf16[2048,16]{0,1:T(8,128)(2,1)}, u32[]{:S(2)}) copy-start(bf16[2048,16]{0,1:T(8,128)(2,1)} %param.27) | copy-start | bytes 196612
  110.4 61.4 %copy-start.64 = (s32[128,8]{0,1:T(8,128)S(1)}, s32[128,8]{0,1:T(8,128)}, u32[]{:S(2)}) copy-start(s32[128,8]{0,1:T(8,128)} %param.18) | copy-start | bytes 12292
  168.9 3.5 copy-start.35
  168.9 3.5 copy-start.36
  282.1 2.8 copy-start.27
  282.1 3.1 copy-start.29
  284.7 24.2 %copy-start.7 = (bf16[4,4,2,128,512]{4,3,1,2,0:T(8,128)(2,1)}, bf16[4,4,2,128,512]{4,3,1,2,0:T(8,128)(2,1)S(1)}, u32[]{:S(2)}) copy-start(bf16[4,4,2,128,512]{4,3,1,2,0:T(8,128)(2,1)S(1)} %copy.60) | copy-start | bytes 12582916
  423.6 40.2 %collective-permute-start = (bf16[2048,2048]{1,0:T(8,128)(2,1)}, bf16[2048,2048]{1,0:T(8,128)(2,1)}, u32[]{:S(2)}, u32[]{:S(2)}) collective-permute-start(bf16[2048,2048]{1,0:T(8,128)(2,1)} %convolution_convert_fusion.2), channel_id=1, source_target_pairs={{0,4},{4,0},{8,12},{12,8},{16,20},{20,16},{24,28},{28,24},{1,5},{5... | collective-permute-start | bytes 25165832 | tf_op jit(solution)/shard_map/ppermute | solution.py:1163
  423.7 8.6 %copy-start.9 = (f32[128,2048]{1,0:T(8,128)S(1)}, f32[128,2048]{1,0:T(8,128)}, u32[]{:S(2)}) copy-start(f32[128,2048]{1,0:T(8,128)} %copy-done.8) | copy-start | bytes 3145732
  473.0 4.2 copy-start.14
  473.1 6.4 copy-start.23
  477.4 52.7 %collective-permute-start.1 = (bf16[2,2,128,2048]{3,2,1,0:T(8,128)(2,1)S(1)}, bf16[2,2,128,2048]{3,2,1,0:T(8,128)(2,1)S(1)}, u32[]{:S(2)}, u32[]{:S(2)}) collective-permute-start(bf16[2,2,128,2048]{3,2,1,0:T(8,128)(2,1)S(1)} %pad_maximum_fusion.3), channel_id=1, source_target_pairs={{0,8},{4,12},{8,0},{12,4},{16,24},{20,28},{24,16},{28,20},{1,9},{5... | collective-permute-start | bytes 6291464 | tf_op jit(solution)/shard_map/ppermute | solution.py:1163
  478.6 51.5 %collective-permute-start.2 = (bf16[2,2,128,2048]{3,2,1,0:T(8,128)(2,1)S(1)}, bf16[2,2,128,2048]{3,2,1,0:T(8,128)(2,1)S(1)}, u32[]{:S(2)}, u32[]{:S(2)}) collective-permute-start(bf16[2,2,128,2048]{3,2,1,0:T(8,128)(2,1)S(1)} %stack.60), channel_id=1, source_target_pairs={{0,16},{4,20},{8,24},{12,28},{16,0},{20,4},{24,8},{28,12},{1,17},{... | collective-permute-start | bytes 6291464 | tf_op jit(solution)/shard_map/ppermute | solution.py:1163
  530.0 4.4 copy-start.6
  530.0 4.4 copy-start.16
  530.0 4.4 copy-start.52
  530.1 8.2 %copy-start.37 = (bf16[2,2,128,2048]{3,2,1,0:T(8,128)(2,1)}, bf16[2,2,128,2048]{3,2,1,0:T(8,128)(2,1)S(1)}, u32[]{:S(2)}) copy-start(bf16[2,2,128,2048]{3,2,1,0:T(8,128)(2,1)S(1)} %collective-permute-done.1) | copy-start | bytes 6291460
  530.1 8.2 %copy-start.39 = (bf16[2,2,128,2048]{3,2,1,0:T(8,128)(2,1)}, bf16[2,2,128,2048]{3,2,1,0:T(8,128)(2,1)S(1)}, u32[]{:S(2)}) copy-start(bf16[2,2,128,2048]{3,2,1,0:T(8,128)(2,1)S(1)} %collective-permute-done.2) | copy-start | bytes 6291460
  532.6 4.0 copy-start.44
  542.2 32.6 %collective-permute-start.3 = (bf16[2,128,2048]{2,1,0:T(8,128)(2,1)}, bf16[2,128,2048]{2,1,0:T(8,128)(2,1)}, u32[]{:S(2)}, u32[]{:S(2)}) collective-permute-start(bf16[2,128,2048]{2,1,0:T(8,128)(2,1)} %get-tuple-element.90), channel_id=1, source_target_pairs={{0,16},{4,20},{8,24},{12,28},{16,0},{20,4},{24,8},{28,12},{1,17},{... | collective-permute-start | bytes 3145736 | tf_op jit(solution)/shard_map/ppermute | solution.py:1163
  543.3 31.5 %collective-permute-start.4 = (bf16[2,128,2048]{2,1,0:T(8,128)(2,1)}, bf16[2,128,2048]{2,1,0:T(8,128)(2,1)}, u32[]{:S(2)}, u32[]{:S(2)}) collective-permute-start(bf16[2,128,2048]{2,1,0:T(8,128)(2,1)} %get-tuple-element.91), channel_id=1, source_target_pairs={{0,8},{4,12},{8,0},{12,4},{16,24},{20,28},{24,16},{28,20},{1,9},{5... | collective-permute-start | bytes 3145736 | tf_op jit(solution)/shard_map/ppermute | solution.py:1163
  557.4 8.6 %copy-start.4 = (bf16[4,128,2048]{2,1,0:T(8,128)(2,1)S(1)}, bf16[4,128,2048]{2,1,0:T(8,128)(2,1)}, u32[]{:S(2)}) copy-start(bf16[4,128,2048]{2,1,0:T(8,128)(2,1)} %copy-done.3) | copy-start | bytes 6291460
  557.4 8.6 %copy-start.72 = (bf16[4,128,512]{2,1,0:T(8,128)(2,1)S(1)}, bf16[4,128,512]{2,1,0:T(8,128)(2,1)}, u32[]{:S(2)}) copy-start(bf16[4,128,512]{2,1,0:T(8,128)(2,1)} %copy-done.71) | copy-start | bytes 1572868
  566.0 2.7 copy-start.45
  566.0 2.9 copy-start.68
  566.0 3.9 copy-start.70
  566.0 3.9 copy-start.73
  570.0 4.8 copy-start.38
  570.0 4.8 copy-start.40
  579.7 110.8 %copy-start.50 = (f32[2048]{0:T(1024)S(1)}, f32[2048]{0:T(1024)}, u32[]{:S(2)}) copy-start(f32[2048]{0:T(1024)} %param.19) | copy-start | bytes 24580
  579.7 110.8 %copy-start.63 = (f32[128]{0:T(128)S(1)}, f32[128]{0:T(128)}, u32[]{:S(2)}) copy-start(f32[128]{0:T(128)} %copy-done.62) | copy-start | bytes 1540
  687.3 9.6 %copy-start.33 = (bf16[16,128,512]{2,1,0:T(8,128)(2,1)S(1)}, bf16[16,128,512]{2,1,0:T(8,128)(2,1)}, u32[]{:S(2)}) copy-start(bf16[16,128,512]{2,1,0:T(8,128)(2,1)} %get-tuple-element.70) | copy-start | bytes 6291460
  696.9 2.7 copy-start.32
  699.7 2.7 copy-start.31
  (33 other events, 59.3 us)
Sparse Core Ops, SparseCore 0:
  11.0 148.6 all-gather.1
  435.9 123.7 all-reduce.1

commit v5 on v4

--- a/solution.py
+++ b/solution.py
@@ -89,7 +89,7 @@
     )
 
 
-def experts_kernel(nz, x_ref, t_ref, g_ref, wide_ref, down_ref, rows_ref, slopes_ref, gated_ref, tiles_ref, land, tags, g_buf, pre, back, gate_at, grad_at, local_sem, s_rows, s_g, sz, sx, sy, sda, sdb, sc, rz, rx, ry, rda, rdb, rc):
+def experts_kernel(nz, x_ref, t_ref, g_ref, gate_ref, up_ref, down_ref, rows_ref, slopes_ref, gated_ref, tiles_ref, land, tags, g_buf, pre, back, gate_at, grad_at, local_sem, s_rows, s_g, sz, sx, sy, sda, sdb, sc, rz, rx, ry, rda, rdb, rc):
     dp, z = lax.axis_index("dp"), lax.axis_index("tensor")
     count, width = x_ref.shape
     half = count // 2
@@ -222,12 +222,11 @@
             load_g(chip, zz, c).start()
         x = land.at[chip, zz]
 
-        def product(k, carry):
-            at = pl.ds(pl.multiple_of(k * 256, 256), 256)
-            pre[:, at] = jnp.dot(x[...], wide_ref[:, at], preferred_element_type=jnp.float32)
-            return carry
-
-        lax.fori_loop(0, 2 * both // 256, product, 0, unroll=True)
+        for k, ref in enumerate((gate_ref, up_ref)):
+            for j in range(gate_at.shape[0]):
+                pre[:, pl.ds(k * both + j * each, each)] = jnp.dot(
+                    x[...], ref[j], preferred_element_type=jnp.float32
+                )
         for j in range(gate_at.shape[0]):
             for c in range(2):
                 row = tags[(2 * chip + c) * nz + zz, pl.ds(dp * gate_at.shape[0] + j, 1), :]
@@ -236,15 +235,14 @@
         for c in range(2):
             load_g(chip, zz, c).wait()
 
-        def back_product(k, carry):
-            at = pl.ds(pl.multiple_of(k * 256, 256), 256)
-            back[:, at] = jnp.dot(g_buf[...], down_ref[:, at], preferred_element_type=jnp.float32)
-            return carry
-
-        lax.fori_loop(0, both // 256, back_product, 0, unroll=True)
+        for j in range(gate_at.shape[0]):
+            back[:, pl.ds(j * each, each)] = lax.dot_general(
+                g_buf[...], down_ref[j], (((1,), (1,)), ((), ())), preferred_element_type=jnp.float32
+            )
 
         def elementwise(k, carry):
             at = pl.ds(pl.multiple_of(k * 64, 64), 64)
+            place, inner = 2 * chip + k // (count // 64), pl.ds(pl.multiple_of(k % (count // 64) * 64, 64), 64)
             for j in range(gate_at.shape[0]):
                 cols, up_cols = pl.ds(j * each, each), pl.ds(both + j * each, each)
                 gate = jnp.concatenate([gate_at[j, at, :]] * (each // 128), axis=1)
@@ -252,7 +250,7 @@
                 sigmoid = 1.0 / (1.0 + jnp.exp(-gate_pre))
                 silu = gate_pre * sigmoid
                 hidden = silu * up_pre
-                gated_ref[chip, zz, at, cols] = (gate * hidden).astype(gated_ref.dtype)
+                gated_ref[place, zz, inner, cols] = (gate * hidden).astype(gated_ref.dtype)
                 share = jnp.sum(hidden * grad, axis=1, keepdims=True)
                 grad_at[j, at, :] = jnp.broadcast_to(share, (64, 128))
                 slope = gate * grad
@@ -337,9 +335,10 @@
             store_rows(chip, zz).wait()
 
 
-def gather_experts(x, gates, cotangents, wide, down, experts_here, nz, collective_id):
+def gather_experts(x, gates, cotangents, w_gate, w_up, w_down, nz, collective_id):
     rows, width = x.shape
-    both = down.shape[1]
+    experts_here, each, _ = w_down.shape
+    both = experts_here * each
     dma, vmem = pltpu.SemaphoreType.DMA, pl.BlockSpec(memory_space=pltpu.VMEM)
     any_place = pl.BlockSpec(memory_space=pl.ANY)
     group = (4, nz, 2 * rows)
@@ -350,10 +349,10 @@
         out_shape=(
             jax.ShapeDtypeStruct(group + (width,), x.dtype),
             jax.ShapeDtypeStruct(group + (2 * both,), x.dtype),
-            jax.ShapeDtypeStruct(group + (both,), x.dtype),
+            jax.ShapeDtypeStruct((8, nz, rows, both), x.dtype),
             jax.ShapeDtypeStruct((8 * nz, 8, rows), jnp.float32),
         ),
-        in_specs=[vmem, vmem, any_place, vmem, vmem],
+        in_specs=[vmem, vmem, any_place, vmem, vmem, vmem],
         out_specs=(any_place, vmem, vmem, vmem),
         scratch_shapes=[
             pltpu.VMEM(group + (width,), x.dtype),
@@ -373,7 +372,7 @@
             collective_id=collective_id, has_side_effects=True, vmem_limit_bytes=VMEM_LIMIT
         ),
         cost_estimate=pl.CostEstimate(flops=flops, bytes_accessed=64 * 2**20, transcendentals=0),
-    )(x, gates, cotangents, wide, down)
+    )(x, gates, cotangents, w_gate, w_up, w_down)
 
 
 def greet_line(dp, z, nz):
@@ -696,10 +695,15 @@
     return [sorted(range(nz), key=lambda zz: (-abs(zz - z), zz if z >= nz // 2 else -zz)) for z in range(nz)]
 
 
-def scatter_kernel(nz, p_ref, t_ref, out_ref, tiles_ref, acc, rc, ra, rb, rx, ry, ru, rd, s_tile, r_tile, s_keep, s_local, s_core, r_core, s_a, r_a, s_b, r_b, s_x, r_x, s_y, r_y, s_u, r_u, s_d, r_d):
+def scatter_kernel(nz, p_ref, gate_ref, up_ref, t_ref, out_ref, tiles_ref, parts, weights, rc, ra, rb, rx, ry, ru, rd, s_weight, s_tile, r_tile, s_keep, s_core, r_core, s_a, r_a, s_b, r_b, s_x, r_x, s_y, r_y, s_u, r_u, s_d, r_d):
     dp, z = lax.axis_index("dp"), lax.axis_index("tensor")
-    rows = acc.shape[2]
+    rows = parts.shape[3]
     half = rows // 2
+    core = dp % 2
+
+    def acc(kind, zz):
+        return parts.at[kind, zz, core]
+
     order = z_order(nz)
 
     def place(i):
@@ -708,56 +712,66 @@
             zz = jnp.where(z == zv, order[zv][i], zz)
         return zz
 
-    def block_of(place, zz):
-        return p_ref.at[(place // 2 * nz + zz) * 2 + place % 2]
-
     flips = (0, 2, 4, 6)
-
-    def load(kind, zz):
-        return pltpu.make_async_copy(
-            block_of(dp ^ flips[kind], zz), acc.at[kind, zz], s_local.at[kind, zz]
-        )
 
     def core_copy(kind, zz):
         return remote(
-            block_of(dp ^ flips[kind] ^ 1, zz), rc.at[kind, zz], s_core.at[kind, zz], r_core.at[kind, zz], (dp ^ 1, z)
+            parts.at[kind, zz, 1 - core], rc.at[kind, zz], s_core.at[kind, zz], r_core.at[kind, zz], (dp ^ 1, z)
         )
 
+    def product(kind, zz):
+        slopes = p_ref.at[(dp ^ (2 * kind)) // 2, zz]
+
+        def tile(n, carry):
+            at = pl.ds(pl.multiple_of(n * 256, 256), 256)
+            total = lax.dot_general(
+                slopes[...], weights[at, :], (((1,), (1,)), ((), ())), preferred_element_type=jnp.float32
+            ).astype(parts.dtype)
+            parts[kind, zz, 0, :, at] = total[:rows]
+            parts[kind, zz, 1, :, at] = total[rows:]
+            return carry
+
+        lax.fori_loop(0, parts.shape[4] // 256, tile, 0, unroll=2)
+
     def a_copy(zz):
-        return remote(acc.at[3, zz, pl.ds(0, half)], ra.at[zz], s_a.at[zz], r_a.at[zz], (dp ^ 2, z))
+        return remote(acc(3, zz).at[pl.ds(0, half)], ra.at[zz], s_a.at[zz], r_a.at[zz], (dp ^ 2, z))
 
     def b_copy(zz):
-        return remote(acc.at[3, zz, pl.ds(half, half)], rb.at[zz], s_b.at[zz], r_b.at[zz], (dp ^ 4, z))
+        return remote(acc(3, zz).at[pl.ds(half, half)], rb.at[zz], s_b.at[zz], r_b.at[zz], (dp ^ 4, z))
 
     def x_copy(zz):
-        return remote(acc.at[1, zz], rx.at[zz], s_x.at[zz], r_x.at[zz], (dp ^ 2, z))
+        return remote(acc(1, zz), rx.at[zz], s_x.at[zz], r_x.at[zz], (dp ^ 2, z))
 
     def y_copy(zz):
-        return remote(acc.at[2, zz], ry.at[zz], s_y.at[zz], r_y.at[zz], (dp ^ 4, z))
+        return remote(acc(2, zz), ry.at[zz], s_y.at[zz], r_y.at[zz], (dp ^ 4, z))
 
     def up_copy(zz):
-        return remote(acc.at[0, zz], ru.at[zz], s_u.at[zz], r_u.at[zz], (dp, z + 1))
+        return remote(acc(0, zz), ru.at[zz], s_u.at[zz], r_u.at[zz], (dp, z + 1))
 
     def down_copy(zz):
-        return remote(acc.at[0, zz], rd.at[zz], s_d.at[zz], r_d.at[zz], (dp, z - 1))
+        return remote(acc(0, zz), rd.at[zz], s_d.at[zz], r_d.at[zz], (dp, z - 1))
 
     def add(dst, *others, start=0, count=rows):
         add_rows(dst, *others, start=start, count=count)
 
     def wave(i):
         zz = place(i)
-        for kind in (3, 1, 2, 0):
+
+        def one(k, carry):
+            kind = 3 - k
+            product(kind, zz)
             core_copy(kind, zz).start()
-            load(kind, zz).start()
+            return carry
+
+        lax.fori_loop(0, 4, one, 0)
 
     def paired(kind, zz):
-        load(kind, zz).wait()
         core_copy(kind, zz).wait_recv()
 
     def stage_diagonal(i):
         zz = place(i)
         paired(3, zz)
-        add(acc.at[3, zz], (rc.at[3, zz], 0))
+        add(acc(3, zz), (rc.at[3, zz], 0))
         a_copy(zz).start()
         b_copy(zz).start()
 
@@ -766,12 +780,12 @@
         paired(1, zz)
         paired(2, zz)
         a_copy(zz).wait_recv()
-        add(acc.at[2, zz], (rc.at[2, zz], 0), (ra.at[zz], 0), start=0, count=half)
-        add(acc.at[2, zz], (rc.at[2, zz], half), start=half, count=half)
+        add(acc(2, zz), (rc.at[2, zz], 0), (ra.at[zz], 0), start=0, count=half)
+        add(acc(2, zz), (rc.at[2, zz], half), start=half, count=half)
         y_copy(zz).start()
         b_copy(zz).wait_recv()
-        add(acc.at[1, zz], (rc.at[1, zz], half), (rb.at[zz], 0), start=half, count=half)
-        add(acc.at[1, zz], (rc.at[1, zz], 0), start=0, count=half)
+        add(acc(1, zz), (rc.at[1, zz], half), (rb.at[zz], 0), start=half, count=half)
+        add(acc(1, zz), (rc.at[1, zz], 0), start=0, count=half)
         x_copy(zz).start()
 
     def stage_column(i):
@@ -779,7 +793,7 @@
         paired(0, zz)
         x_copy(zz).wait_recv()
         y_copy(zz).wait_recv()
-        add(acc.at[0, zz], (rc.at[0, zz], 0), (rx.at[zz], 0), (ry.at[zz], 0))
+        add(acc(0, zz), (rc.at[0, zz], 0), (rx.at[zz], 0), (ry.at[zz], 0))
 
         @pl.when((zz > z) & (z == 0))
         def _():
@@ -795,13 +809,13 @@
         @pl.when((zz > z) & (z > 0))
         def _():
             up_copy(zz).wait_recv()
-            add(acc.at[0, zz], (ru.at[zz], 0))
+            add(acc(0, zz), (ru.at[zz], 0))
             up_copy(zz).start()
 
         @pl.when((zz < z) & (z < nz - 1))
         def _():
             down_copy(zz).wait_recv()
-            add(acc.at[0, zz], (rd.at[zz], 0))
+            add(acc(0, zz), (rd.at[zz], 0))
             down_copy(zz).start()
 
     def peers():
@@ -816,20 +830,33 @@
             t_ref.at[peer * nz + line], tiles_ref.at[here], s_tile.at[flip, turn], r_tile.at[flip, turn], (peer, line)
         )
 
+    each = gate_ref.shape[2]
+    here = gate_ref.shape[0]
+    fetch = [
+        pltpu.make_async_copy(
+            ref.at[j], weights.at[:, pl.ds((k * here + j) * each, each)], s_weight.at[k, j]
+        )
+        for k, ref in enumerate((gate_ref, up_ref))
+        for j in range(here)
+    ]
+    for copy in fetch:
+        copy.start()
     barrier = pltpu.get_barrier_semaphore()
     for _, _, peer, line in peers():
         pl.semaphore_signal(barrier, 1, device_id=(peer, line), device_id_type=MESH)
     pl.semaphore_wait(barrier, 8 * nz - 1)
+    for copy in fetch:
+        copy.wait()
     wave(0)
     keep = pltpu.make_async_copy(t_ref.at[dp * nz + z], tiles_ref.at[dp * nz + z], s_keep)
     keep.start()
     for peer in peers():
         tile_copy(*peer).start()
     for i in range(nz + 3):
+        if i < nz:
+            stage_diagonal(i)
         if i + 1 < nz:
             wave(i + 1)
-        if i < nz:
-            stage_diagonal(i)
         if 0 <= i - 1 < nz:
             stage_side(i - 1)
         if 0 <= i - 2 < nz:
@@ -853,7 +880,7 @@
 
     def finish(k, carry):
         at = pl.ds(k * CHUNK, CHUNK)
-        total = acc[0, z, at, :].astype(jnp.float32)
+        total = parts[0, z, core, at, :].astype(jnp.float32)
         zero = jnp.zeros_like(total)
         total = total + jnp.where(z > 0, ru[z, at, :].astype(jnp.float32), zero)
         total = total + jnp.where(z < nz - 1, rd[z, at, :].astype(jnp.float32), zero)
@@ -878,8 +905,8 @@
             down_copy(zz).wait_send()
 
 
-def scatter_all(p, tiles, nz, collective_id):
-    _, rows, width = p.shape
+def scatter_all(p, w_gate, w_up, tiles, nz, collective_id):
+    rows, width = p.shape[2] // 2, w_gate.shape[1]
     dma, vmem = pltpu.SemaphoreType.DMA, functools.partial(pltpu.VMEM, dtype=p.dtype)
     half = rows // 2
     return pl.pallas_call(
@@ -889,18 +916,22 @@
             jax.ShapeDtypeStruct((rows, width), jnp.float32),
             jax.ShapeDtypeStruct(tiles.shape, tiles.dtype),
         ),
-        in_specs=[pl.BlockSpec(memory_space=pl.ANY), pl.BlockSpec(memory_space=pltpu.VMEM)],
+        in_specs=[
+            pl.BlockSpec(memory_space=pltpu.VMEM),
+            *[pl.BlockSpec(memory_space=pl.ANY)] * 2,
+            pl.BlockSpec(memory_space=pltpu.VMEM),
+        ],
         out_specs=(pl.BlockSpec(memory_space=pltpu.VMEM), pl.BlockSpec(memory_space=pltpu.VMEM)),
-        scratch_shapes=[vmem((4, nz, rows, width)), vmem((4, nz, rows, width))]
+        scratch_shapes=[vmem((4, nz, 2, rows, width)), vmem((width, p.shape[3])), vmem((4, nz, rows, width))]
         + [vmem((nz, half, width)) for _ in range(2)]
         + [vmem((nz, rows, width)) for _ in range(4)]
-        + [dma((8, nz)), dma((8, nz)), dma(())]
-        + [dma((4, nz)), dma((4, nz)), dma((4, nz))]
+        + [dma((2, w_gate.shape[0])), dma((8, nz)), dma((8, nz)), dma(())]
+        + [dma((4, nz)), dma((4, nz))]
         + [dma((nz,)) for _ in range(12)],
         compiler_params=pltpu.CompilerParams(
             collective_id=collective_id, has_side_effects=True, vmem_limit_bytes=VMEM_LIMIT
         ),
-    )(p, tiles)
+    )(p, w_gate, w_up, tiles)
 
 
 def finish_kernel(nz, nc, g_ref, h_ref, p_ref, e_ref, unit_ref, small_ref, sum_q, sum_k, sum_v, sum_o, out_ref, routed_ref, total_ref, buf, acc, rc, ra, rb, rx, ry, line_acc, up, down, more_acc, more_got, *sems):
@@ -1367,22 +1398,20 @@
     gates = jnp.where(chosen, route_probs, 0.0).T
 
     down_rows = w_down.reshape(exp_dev * width, d_model)
-    wide = jnp.concatenate([w_gate[e] for e in range(exp_dev)] + [w_up[e] for e in range(exp_dev)], axis=1)
     both = exp_dev * width
-    all_rows, grad_pre, gated, tiles = gather_experts(
+    all_rows, slopes, gated, tiles = gather_experts(
         second_normalized,
         gates,
         all_cotangents.reshape(devices, tok_count, d_model),
-        wide,
-        down_rows.T,
-        exp_dev,
+        w_gate,
+        w_up,
+        w_down,
         n_tensor,
         0,
     )
-    all_rows, grad_pre = all_rows.reshape(all_count, d_model), grad_pre.reshape(all_count, 2 * both)
-    lines = gated.reshape(n_dp // 2, n_tensor, 2, tok_count, both).transpose(0, 2, 1, 3, 4)
-    gated_hidden = lines.reshape(all_count, both)
-    lines = lines.reshape(n_dp, n_tensor * tok_count, both)
+    all_rows, grad_pre = all_rows.reshape(all_count, d_model), slopes.reshape(all_count, 2 * both)
+    gated_hidden = gated.reshape(all_count, both)
+    lines = gated.reshape(n_dp, n_tensor * tok_count, both)
 
     def out_rows(places):
         picked = [
@@ -1393,13 +1422,9 @@
             jnp.concatenate(picked), down_rows, preferred_element_type=jnp.float32
         ).astype(jnp.bfloat16)
 
-    in_part = jnp.einsum("tf,df->td", grad_pre, wide, preferred_element_type=jnp.float32).astype(jnp.bfloat16)
     spread = Spread(n_tensor, (tok_count, d_model))
     partner_rows = out_rows((1, 3, 5, 7))
-    in_part, partner_rows = hold(in_part, partner_rows)
-    grad_in, gate_tiles = scatter_all(
-        in_part.reshape(devices, tok_count, d_model), tiles, n_tensor, 1
-    )
+    grad_in, gate_tiles = scatter_all(slopes, w_gate, w_up, tiles, n_tensor, 1)
     grad_in, partner_rows = hold(grad_in, partner_rows)
     theirs = spread.pair(out_rows((0, 2, 4, 6)), partner_rows)
     sides = spread.sides(theirs)

time: 733 us -> 710 us (0.969)
  matrix products: 114 us -> 87.4 us
  Pallas kernels: 493 us -> 511 us
  other arithmetic: 51.5 us -> 42.9 us
    dot_general x1 -> x0, matrix products: 23.7 us -> none  [experts_dense(): jnp.einsum('tf,df->td', grad_pre, wide, preferred_element_type=jnp.float32)]
    pallas_call x1, Pallas kernels: 103 us -> 115 us  [scatter_all(): pl.pallas_call(functools.partial(scatter_kernel, nz), name='scatter_all',...]
    unnamed x152 -> x130, local copies, waits for them, and re-layouts: 17.1 us -> 15.4 us
  transfers between devices with their start and end apart: 7 -> 7, of which waited for: 0 -> 2; matrix products, arithmetic and copies ran while one was open for 18% -> 16% of each run, Pallas kernels for 39% -> 41%
where the time goes in v5:
time: 710 us; the launch traced here: 700 us
  Pallas kernels  511 us (72%)
  matrix products  87.4 us (12%)
  other arithmetic  42.9 us (6%)
  local copies, waits for them, and re-layouts  37.1 us (5%)
  between operations  15.6 us (2%)
    pallas_call x1, Pallas kernels, scatter_all(): pl.pallas_call(functools.partial(scatter_kernel, nz), name='scatter_all',...  115 us
    pallas_call x2, Pallas kernels, line_gather(): pl.pallas_call(kernel, name='line_gather', out_shape=blocks, in_specs=[vm...  110 us
    pallas_call x1, Pallas kernels, finish_sums(): pl.pallas_call(functools.partial(finish_kernel, nz, nc), name='finish_sum...  106 us
    pallas_call x1, Pallas kernels, gather_experts(): pl.pallas_call(functools.partial(experts_kernel, nz), name='gather_expert...  105 us
    pallas_call x1, Pallas kernels, line_scatter(): pl.pallas_call(functools.partial(line_scatter_kernel, nz), name='line_sca...  63.8 us
    dot_general x1, matrix products, experts_dense(): jnp.einsum('td,tf->df', all_rows, grad_pre, preferred_element_type=jnp.fl...  22.6 us
    dot_general x2, matrix products, out_rows(): jnp.dot(jnp.concatenate(picked), down_rows, preferred_element_type=jnp.fl...  18.7 us
    unnamed x130, local copies, waits for them, and re-layouts  15.4 us
  transfers between devices with their start and end apart: 7, of which 2 were waited for; matrix products, arithmetic and copies ran while one was open for 16% of the time, Pallas kernels for 41%

profile of v5, /device:TPU:0, one launch (start us, length us, event | category | flops | bytes accessed | tf_op | source)
XLA Modules:
  0.0 700.2 jit_solution(17105279688538223753)
XLA Ops:
  8.0 1.4 fusion.29
  9.4 2.2 convert_multiply_fusion
  11.7 72.7 %line_gather.2 = bf16[4,128,2048]{2,1,0:T(8,128)(2,1)S(1)} custom-call(bf16[128,2048]{1,0:T(8,128)(2,1)S(1)} %get-tuple-element.109.refs_0_), custom_call_target="tpu_custom_call" | custom-call | tf_op jit(solution)/shard_map/line_gather/pallas_call | solution.py:513
  84.4 1.3 multiply_reduce_fusion.8
  86.7 1.3 multiply_reduce_fusion.7
  88.1 5.6 line_total.2
  98.6 2.1 copy-done.54
  100.8 1.3 convolution_convert_fusion.5
  102.1 1.4 convolution_convert_fusion.7
  103.5 1.3 convolution_convert_fusion.3
  104.8 63.8 %line_scatter.1 = f32[128,2048]{1,0:T(8,128)S(1)} custom-call(bf16[4,128,2048]{2,1,0:T(8,128)(2,1)S(1)} %bitcast.179), custom_call_target="tpu_custom_call" | custom-call | tf_op jit(solution)/shard_map/line_scatter/pallas_call | solution.py:679
  168.7 1.3 multiply_reduce_fusion.6
  172.0 105.3 %gather_experts.1 = (bf16[4,4,256,2048]{3,2,1,0:T(8,128)(2,1)}, bf16[4,4,256,1024]{3,2,1,0:T(8,128)(2,1)}, bf16[8,4,128,512]{3,2,1,0:T(8,128)(2,1)}, f32[32,8,128]{2,1,0:T(8,128)}) custom-call(bf16[128,2048]{1,0:T(8,128)(2,1)} %copy-done.23, f32[16,128]{1,0:T(8,128)} %select_bitcast_fusion.2.t_ref, bf16[32,128,2048]{2,1,0:T(8,128)(2,1)} %bitcast.221, ...), custom_call_target="tpu_custom_call" | custom-call | flops 25769803776 | bytes 67108864 | tf_op jit(solution)/shard_map/gather_experts/pallas_call | solution.py:346
  277.3 115.1 %scatter_all.1 = (f32[128,2048]{1,0:T(8,128)}, f32[32,8,128]{2,1,0:T(8,128)}) custom-call(bf16[4,4,256,1024]{3,2,1,0:T(8,128)(2,1)} %get-tuple-element.43.p_ref, bf16[2,2048,256]{2,1,0:T(8,128)(2,1)} %gate_ref.3, bf16[2,2048,256]{2,1,0:T(8,128)(2,1)} %up_ref.3, f32[32,8,128]{2,1,0:T(8,128)} %get-tuple-element.44.t_ref), custom_call_target="tpu_custom_call" | custom-call | tf_op jit(solution)/shard_map/scatter_all/pallas_call | solution.py:912
  392.5 3.8 dynamic-slice_bitcast_fusion.3
  396.3 9.7 %convolution_convert_fusion.1 = bf16[2048,2048]{1,0:T(8,128)(2,1)} fusion(bf16[512,2048]{1,0:T(8,128)(2,1)S(1)} %bitcast.223, bf16[512,512]{1,0:T(8,128)(2,1)S(1)} %get-tuple-element.94, bf16[512,512]{1,0:T(8,128)(2,1)S(1)} %get-tuple-element.95, bf16[512,512]{1,0:T(8,128)(2,1)S(1)} %get-tuple-element.96, bf16[512,512]{1,0:T(8,128)(2,1)S(1)} %get-tuple-element.97), kind=kOutput, calls=%fused_computation.4 | convolution fusion | flops 4307550208 | bytes 12582912 | tf_op jit(solution)/shard_map/dot_general | solution.py:1421
  408.2 2.6 multiply_reduce_fusion.2
  411.6 6.3 copy.52
  417.9 22.6 %convolution_bitcast_fusion = f32[2048,1024]{1,0:T(8,128)S(1)} fusion(bf16[4,4,256,2048]{3,2,1,0:T(8,128)(2,1)} %get-tuple-element.71, bf16[4,4,256,1024]{3,2,1,0:T(8,128)(2,1)} %get-tuple-element.43.p_ref), kind=kOutput, calls=%fused_computation.11 | convolution fusion | flops 17179869184 | bytes 33554432 | tf_op jit(solution)/shard_map/td,tf->df/dot_general | solution.py:1434
  441.4 2.3 pad_maximum_fusion.1
  443.7 2.3 pad_maximum_fusion
  447.0 9.1 %add_convert_fusion = bf16[2048,2048]{1,0:T(8,128)(2,1)S(1)} fusion(bf16[2048,2048]{1,0:T(8,128)(2,1)} %collective-permute-done, bf16[512,2048]{1,0:T(8,128)(2,1)} %bitcast.222, bf16[512,512]{1,0:T(8,128)(2,1)} %get-tuple-element.91, bf16[512,512]{1,0:T(8,128)(2,1)} %get-tuple-element.92, bf16[512,512]{1,0:T(8,128)(2,1)} %get-tuple-element.93, ...), kind=kOutput, calls=%fused_computation.2 | convolution fusion | flops 4324327424 | bytes 20971520 | tf_op jit(solution)/shard_map/dot_general | solution.py:1421
  456.4 3.0 copy-done.22
  459.6 1.8 collective-permute-start.2
  461.5 13.8 %fusion = f32[2,256,2048]{2,1,0:T(8,128)} fusion(bf16[2,256,4096]{2,1,0:T(8,128)(2,1)S(1)} %bitcast.192, bf16[4096,2048]{1,0:T(8,128)(2,1)} %all-gather.2.cloned.1.call-done), kind=kOutput, calls=%fused_computation | convolution fusion | flops 8589934592 | bytes 25165824 | tf_op jit(solution)/shard_map/tf,td->fd/dot_general | solution.py:1431
  475.4 37.3 %line_gather.3 = bf16[4,128,2048]{2,1,0:T(8,128)(2,1)S(1)} custom-call(bf16[128,2048]{1,0:T(8,128)(2,1)S(1)} %fusion.52.refs_0_), custom_call_target="tpu_custom_call" | custom-call | tf_op jit(solution)/shard_map/line_gather/pallas_call | solution.py:513
  512.7 1.3 convolution_convert_fusion.4
  515.8 1.3 copy-done.6
  517.2 1.6 multiply_reduce_fusion
  518.8 2.2 convolution_convert_fusion.6
  527.7 3.1 fusion.31
  531.0 1.8 collective-permute-start.4
  532.7 5.5 line_total.3
  538.9 6.6 convolution_convert_fusion
  545.6 2.6 convolution_convert_fusion.2
  549.2 4.8 fusion.9
  554.0 1.7 collective-permute-done.3
  555.8 2.8 fusion.28
  558.6 1.5 pad_maximum_fusion.3.e_ref
  560.1 105.7 %finish_sums.1 = (bf16[16,128,512]{2,1,0:T(8,128)(2,1)}, bf16[16,128,512]{2,1,0:T(8,128)(2,1)}, bf16[16,128,512]{2,1,0:T(8,128)(2,1)}, bf16[16,128,512]{2,1,0:T(...) custom-call(bf16[16,128,1536]{2,1,0:T(8,128)(2,1)} %bitcast.190, ...), custom_call_target="tpu_custom_call" | custom-call | tf_op jit(solution)/shard_map/finish_sums/pallas_call | solution.py:1157
  667.3 1.6 slice_bitcast_fusion.4
  668.9 1.4 slice.110
  670.4 4.2 bitcast_convert_fusion
  674.6 5.3 copy.50
  679.9 4.3 bitcast_convert_fusion.1
  684.2 2.7 bitcast_convert_fusion.2
  687.0 2.7 bitcast_convert_fusion.3
  690.7 1.6 add_convert_fusion.5
  (192 shorter events, 27.5 us)
Async XLA Ops:
  7.2 96.3 %copy-start = (bf16[512,2048]{1,0:T(8,128)(2,1)S(1)}, bf16[512,2048]{1,0:T(8,128)(2,1)}, u32[]{:S(2)}) copy-start(bf16[512,2048]{1,0:T(8,128)(2,1)} %param.25) | copy-start | bytes 6291460
  7.2 164.8 %all-gather.2.cloned.1.call-start = ((), (), s32[]{:S(2)}) async-start(), calls=%async_computation | async-start | bytes 17301504 | tf_op jit(solution)/shard_map/all_gather | solution.py:1508
  7.9 657.9 %all-reduce.2.cloned.1.call-start = ((), (), s32[]{:S(2)}) async-start(), calls=%async_computation.1 | async-start | bytes 393216 | tf_op jit(solution)/shard_map/psum | solution.py:1562
  8.0 76.4 %copy-start.58 = (bf16[2048,512]{1,0:T(8,128)(2,1)S(1)}, bf16[2048,512]{1,0:T(8,128)(2,1)}, u32[]{:S(2)}) copy-start(bf16[2048,512]{1,0:T(8,128)(2,1)} %param.20) | copy-start | bytes 6291460
  9.4 75.0 %copy-start.50 = (f32[128]{0:T(128)}, f32[128]{0:T(128)S(1)}, u32[]{:S(2)}) copy-start(f32[128]{0:T(128)S(1)} %add_rsqrt_fusion.3) | copy-start | bytes 1540
  84.3 14.3 %copy-start.1 = (bf16[4,128,2048]{2,1,0:T(8,128)(2,1)}, bf16[4,128,2048]{2,1,0:T(8,128)(2,1)S(1)}, u32[]{:S(2)}) copy-start(bf16[4,128,2048]{2,1,0:T(8,128)(2,1)S(1)} %line_gather.2) | copy-start | bytes 6291460
  86.7 8.7 %copy-start.17 = (f32[512,512]{0,1:T(8,128)}, f32[512,512]{0,1:T(8,128)S(1)}, u32[]{:S(2)}) copy-start(f32[512,512]{0,1:T(8,128)S(1)} %get-tuple-element.133) | copy-start | bytes 3145732
  86.7 8.4 %copy-start.49 = (s32[1,512]{1,0:T(1,128)S(1)}, s32[1,512]{1,0:T(1,128)}, u32[]{:S(2)}) copy-start(s32[1,512]{1,0:T(1,128)} %param.17) | copy-start | bytes 6148
  86.7 8.7 %copy-start.47 = (f32[512]{0:T(512)S(1)}, f32[512]{0:T(512)}, u32[]{:S(2)}) copy-start(f32[512]{0:T(512)} %param.23) | copy-start | bytes 6148
  88.0 8.0 %copy-start.14 = (f32[512,512]{0,1:T(8,128)}, f32[512,512]{0,1:T(8,128)S(1)}, u32[]{:S(2)}) copy-start(f32[512,512]{0,1:T(8,128)S(1)} %get-tuple-element.131) | copy-start | bytes 3145732
  88.0 7.5 %copy-start.48 = (f32[512]{0:T(512)S(1)}, f32[512]{0:T(512)}, u32[]{:S(2)}) copy-start(f32[512]{0:T(512)} %param.24) | copy-start | bytes 6148
  97.6 4.4 copy-start.5
  97.7 3.1 copy-start.54
  104.8 66.1 %copy-start.45 = (f32[2048]{0:T(1024)S(1)}, f32[2048]{0:T(1024)}, u32[]{:S(2)}) copy-start(f32[2048]{0:T(1024)} %param.26) | copy-start | bytes 24580
  104.8 66.3 %copy-start.44 = (bf16[2048,16]{0,1:T(8,128)(2,1)S(1)}, bf16[2048,16]{0,1:T(8,128)(2,1)}, u32[]{:S(2)}) copy-start(bf16[2048,16]{0,1:T(8,128)(2,1)} %param.27) | copy-start | bytes 196612
  168.6 2.8 copy-start.52
  392.5 3.8 copy-start.53
  396.3 11.9 %copy-start.8 = (f32[128,2048]{1,0:T(8,128)S(1)}, f32[128,2048]{1,0:T(8,128)}, u32[]{:S(2)}) copy-start(f32[128,2048]{1,0:T(8,128)} %copy-done.7) | copy-start | bytes 3145732
  406.0 40.3 %collective-permute-start = (bf16[2048,2048]{1,0:T(8,128)(2,1)}, bf16[2048,2048]{1,0:T(8,128)(2,1)}, u32[]{:S(2)}, u32[]{:S(2)}) collective-permute-start(bf16[2048,2048]{1,0:T(8,128)(2,1)} %convolution_convert_fusion.1), channel_id=1, source_target_pairs={{0,4},{4,0},{8,12},{12,8},{16,20},{20,16},{24,28},{28,24},{1,5},{5... | collective-permute-start | bytes 25165832 | tf_op jit(solution)/shard_map/ppermute | solution.py:1194
  456.1 3.3 copy-start.22
  459.5 53.1 %collective-permute-start.1 = (bf16[2,2,128,2048]{3,2,1,0:T(8,128)(2,1)S(1)}, bf16[2,2,128,2048]{3,2,1,0:T(8,128)(2,1)S(1)}, u32[]{:S(2)}, u32[]{:S(2)}) collective-permute-start(bf16[2,2,128,2048]{3,2,1,0:T(8,128)(2,1)S(1)} %pad_maximum_fusion.2), channel_id=1, source_target_pairs={{0,8},{4,12},{8,0},{12,4},{16,24},{20,28},{24,16},{28,20},{1,9},{5... | collective-permute-start | bytes 6291464 | tf_op jit(solution)/shard_map/ppermute | solution.py:1194
  459.6 53.1 %collective-permute-start.2 = (bf16[2,2,128,2048]{3,2,1,0:T(8,128)(2,1)S(1)}, bf16[2,2,128,2048]{3,2,1,0:T(8,128)(2,1)S(1)}, u32[]{:S(2)}, u32[]{:S(2)}) collective-permute-start(bf16[2,2,128,2048]{3,2,1,0:T(8,128)(2,1)S(1)} %stack.60), channel_id=1, source_target_pairs={{0,16},{4,20},{8,24},{12,28},{16,0},{20,4},{24,8},{28,12},{1,17},{... | collective-permute-start | bytes 6291464 | tf_op jit(solution)/shard_map/ppermute | solution.py:1194
  512.7 3.1 copy-start.36
  512.7 4.4 copy-start.6
  512.7 4.5 copy-start.42
  527.7 10.6 %copy-start.13 = (f32[512,4,128]{0,2,1:T(8,128)S(1)}, f32[512,4,128]{0,2,1:T(8,128)}, u32[]{:S(2)}) copy-start(f32[512,4,128]{0,2,1:T(8,128)} %copy-done.12) | copy-start | bytes 3145732
  527.7 10.6 %copy-start.19 = (f32[512,512]{0,1:T(8,128)S(1)}, f32[512,512]{0,1:T(8,128)}, u32[]{:S(2)}) copy-start(f32[512,512]{0,1:T(8,128)} %copy-done.17) | copy-start | bytes 3145732
  527.7 10.8 %copy-start.11 = (f32[512,4,128]{0,2,1:T(8,128)S(1)}, f32[512,4,128]{0,2,1:T(8,128)}, u32[]{:S(2)}) copy-start(f32[512,4,128]{0,2,1:T(8,128)} %copy-done.10) | copy-start | bytes 3145732
  527.7 10.8 %copy-start.16 = (f32[512,512]{0,1:T(8,128)S(1)}, f32[512,512]{0,1:T(8,128)}, u32[]{:S(2)}) copy-start(f32[512,512]{0,1:T(8,128)} %copy-done.14) | copy-start | bytes 3145732
  530.9 8.0 %copy-start.2 = (bf16[4,128,2048]{2,1,0:T(8,128)(2,1)S(1)}, bf16[4,128,2048]{2,1,0:T(8,128)(2,1)}, u32[]{:S(2)}) copy-start(bf16[4,128,2048]{2,1,0:T(8,128)(2,1)} %copy-done.1) | copy-start | bytes 6291460
  530.9 8.0 %copy-start.62 = (bf16[4,128,512]{2,1,0:T(8,128)(2,1)S(1)}, bf16[4,128,512]{2,1,0:T(8,128)(2,1)}, u32[]{:S(2)}) copy-start(bf16[4,128,512]{2,1,0:T(8,128)(2,1)} %convolution_convert_fusion.6) | copy-start | bytes 1572868
  530.9 24.8 %collective-permute-start.3 = (bf16[2,128,2048]{2,1,0:T(8,128)(2,1)S(1)}, bf16[2,128,2048]{2,1,0:T(8,128)(2,1)S(1)}, u32[]{:S(2)}, u32[]{:S(2)}) collective-permute-start(bf16[2,128,2048]{2,1,0:T(8,128)(2,1)S(1)} %get-tuple-element.86), channel_id=1, source_target_pairs={{0,16},{4,20},{8,24},{12,28},{16,0},{20,4},{24,8},{28,12},{1,17},{... | collective-permute-start | bytes 3145736 | tf_op jit(solution)/shard_map/ppermute | solution.py:1194
  531.0 24.8 %collective-permute-start.4 = (bf16[2,128,2048]{2,1,0:T(8,128)(2,1)S(1)}, bf16[2,128,2048]{2,1,0:T(8,128)(2,1)S(1)}, u32[]{:S(2)}, u32[]{:S(2)}) collective-permute-start(bf16[2,128,2048]{2,1,0:T(8,128)(2,1)S(1)} %get-tuple-element.87), channel_id=1, source_target_pairs={{0,8},{4,12},{8,0},{12,4},{16,24},{20,28},{24,16},{28,20},{1,9},{5... | collective-permute-start | bytes 3145736 | tf_op jit(solution)/shard_map/ppermute | solution.py:1194
  538.8 6.7 copy-start.4
  538.9 6.7 copy-start.61
  545.5 2.7 copy-start.55
  545.6 3.6 copy-start.59
  549.2 6.6 copy-start.35
  549.2 6.6 copy-start.37
  679.9 4.4 copy-start.33
  684.2 2.7 copy-start.32
  687.0 2.8 copy-start.9
  687.0 2.8 copy-start.31
  687.0 2.8 copy-start.46
  687.0 2.8 copy-start.51
  687.0 3.7 copy-start.21
  687.0 3.7 copy-start.25
  687.0 3.7 copy-start.40
  (22 other events, 34.7 us)
Sparse Core Ops, SparseCore 0:
  11.0 154.3 all-gather.1
  411.7 123.8 all-reduce.1

commit v6 on v5

--- a/solution.py
+++ b/solution.py
@@ -247,7 +247,7 @@
                 cols, up_cols = pl.ds(j * each, each), pl.ds(both + j * each, each)
                 gate = jnp.concatenate([gate_at[j, at, :]] * (each // 128), axis=1)
                 gate_pre, up_pre, grad = pre[at, cols], pre[at, up_cols], back[at, cols]
-                sigmoid = 1.0 / (1.0 + jnp.exp(-gate_pre))
+                sigmoid = 0.5 + 0.5 * jnp.tanh(0.5 * gate_pre)
                 silu = gate_pre * sigmoid
                 hidden = silu * up_pre
                 gated_ref[place, zz, inner, cols] = (gate * hidden).astype(gated_ref.dtype)
@@ -271,7 +271,7 @@
 
     def job(step, k):
         kind, sign = k // 2, 1 - 2 * (k % 2)
-        distance = step - 1 - (kind + 1) // 2
+        distance = step - 1 - jnp.where(kind == 0, 0, 1)
         zz = z + sign * distance
         flip = 2 * kind
 
@@ -309,7 +309,7 @@
         lax.fori_loop(0, 8, inner, 0)
         return carry
 
-    lax.fori_loop(0, nz + 3, step_body, 0)
+    lax.fori_loop(0, nz + 2, step_body, 0)
 
     def sent(copies):
         for copy in copies:
@@ -565,12 +565,16 @@
     )(x)
 
 
-CHUNK = 16
+CHUNK = 32
 
 
 def add_rows(dst, *others, start=0, count):
     def body(k, carry):
         at = pl.ds(start + k * CHUNK, CHUNK)
+        if len(others) == 1:
+            ref, base = others[0]
+            dst[at, :] = dst[at, :] + ref[pl.ds(base + k * CHUNK, CHUNK), :]
+            return carry
         total = dst[at, :].astype(jnp.float32)
         for ref, base in others:
             total = total + ref[pl.ds(base + k * CHUNK, CHUNK), :].astype(jnp.float32)
@@ -1113,7 +1117,8 @@
         lax.fori_loop(0, routed_ref.shape[0] // CHUNK, body, 0)
 
     side = [functools.partial(line.step, distance) for distance in range(1, nz - 1)] + [line_end, more_start]
-    late = [functools.partial(total.step, k, total_ref) for k in range(3)] + [more_end]
+    side += [functools.partial(total.step, 0, total_ref)]
+    late = [functools.partial(total.step, k, total_ref) for k in range(1, 3)] + [more_end]
     late += [functools.partial(total.step, k, total_ref) for k in range(3, Total.steps)]
     stages = (stage_diagonal, stage_side, stage_own, stage_relay, stage_corner)
     for i in range(nc + len(stages) - 1):

time: 710 us -> 703 us (level)
  transfers between devices with their start and end apart: 7 -> 7, of which waited for: 2 -> 2; matrix products, arithmetic and copies ran while one was open for 16% -> 16% of each run, Pallas kernels for 41% -> 42%
where the time goes in v6:
time: 703 us; the launch traced here: 694 us
  Pallas kernels  505 us (72%)
  matrix products  87.4 us (12%)
  other arithmetic  42.9 us (6%)
  local copies, waits for them, and re-layouts  37 us (5%)
  between operations  15.6 us (2%)
    pallas_call x1, Pallas kernels, scatter_all(): pl.pallas_call(functools.partial(scatter_kernel, nz), name='scatter_all',...  115 us
    pallas_call x2, Pallas kernels, line_gather(): pl.pallas_call(kernel, name='line_gather', out_shape=blocks, in_specs=[vm...  110 us
    pallas_call x1, Pallas kernels, finish_sums(): pl.pallas_call(functools.partial(finish_kernel, nz, nc), name='finish_sum...  104 us
    pallas_call x1, Pallas kernels, gather_experts(): pl.pallas_call(functools.partial(experts_kernel, nz), name='gather_expert...  102 us
    pallas_call x1, Pallas kernels, line_scatter(): pl.pallas_call(functools.partial(line_scatter_kernel, nz), name='line_sca...  63.8 us
    dot_general x1, matrix products, experts_dense(): jnp.einsum('td,tf->df', all_rows, grad_pre, preferred_element_type=jnp.fl...  22.6 us
    dot_general x2, matrix products, out_rows(): jnp.dot(jnp.concatenate(picked), down_rows, preferred_element_type=jnp.fl...  18.7 us
    unnamed x130, local copies, waits for them, and re-layouts  15.4 us
  transfers between devices with their start and end apart: 7, of which 2 were waited for; matrix products, arithmetic and copies ran while one was open for 16% of the time, Pallas kernels for 42%

profile of v6, /device:TPU:0, one launch (start us, length us, event | category | flops | bytes accessed | tf_op | source)
XLA Modules:
  0.0 693.9 jit_solution(14432668759559439177)
XLA Ops:
  8.0 1.4 fusion.29
  9.4 2.2 convert_multiply_fusion
  11.7 72.7 %line_gather.2 = bf16[4,128,2048]{2,1,0:T(8,128)(2,1)S(1)} custom-call(bf16[128,2048]{1,0:T(8,128)(2,1)S(1)} %get-tuple-element.109.refs_0_), custom_call_target="tpu_custom_call" | custom-call | tf_op jit(solution)/shard_map/line_gather/pallas_call | solution.py:513
  84.4 1.3 multiply_reduce_fusion.8
  86.7 1.3 multiply_reduce_fusion.7
  88.1 5.6 line_total.2
  98.6 2.1 copy-done.54
  100.8 1.3 convolution_convert_fusion.5
  102.1 1.4 convolution_convert_fusion.7
  103.5 1.3 convolution_convert_fusion.3
  104.8 63.8 %line_scatter.1 = f32[128,2048]{1,0:T(8,128)S(1)} custom-call(bf16[4,128,2048]{2,1,0:T(8,128)(2,1)S(1)} %bitcast.179), custom_call_target="tpu_custom_call" | custom-call | tf_op jit(solution)/shard_map/line_scatter/pallas_call | solution.py:683
  168.7 1.3 multiply_reduce_fusion.6
  172.0 101.6 %gather_experts.1 = (bf16[4,4,256,2048]{3,2,1,0:T(8,128)(2,1)}, bf16[4,4,256,1024]{3,2,1,0:T(8,128)(2,1)}, bf16[8,4,128,512]{3,2,1,0:T(8,128)(2,1)}, f32[32,8,128]{2,1,0:T(8,128)}) custom-call(bf16[128,2048]{1,0:T(8,128)(2,1)} %copy-done.23, f32[16,128]{1,0:T(8,128)} %select_bitcast_fusion.2.t_ref, bf16[32,128,2048]{2,1,0:T(8,128)(2,1)} %bitcast.221, ...), custom_call_target="tpu_custom_call" | custom-call | flops 25769803776 | bytes 67108864 | tf_op jit(solution)/shard_map/gather_experts/pallas_call | solution.py:346
  273.6 114.5 %scatter_all.1 = (f32[128,2048]{1,0:T(8,128)}, f32[32,8,128]{2,1,0:T(8,128)}) custom-call(bf16[4,4,256,1024]{3,2,1,0:T(8,128)(2,1)} %get-tuple-element.43.p_ref, bf16[2,2048,256]{2,1,0:T(8,128)(2,1)} %gate_ref.3, bf16[2,2048,256]{2,1,0:T(8,128)(2,1)} %up_ref.3, f32[32,8,128]{2,1,0:T(8,128)} %get-tuple-element.44.t_ref), custom_call_target="tpu_custom_call" | custom-call | tf_op jit(solution)/shard_map/scatter_all/pallas_call | solution.py:916
  388.2 3.8 dynamic-slice_bitcast_fusion.3
  392.0 9.7 %convolution_convert_fusion.1 = bf16[2048,2048]{1,0:T(8,128)(2,1)} fusion(bf16[512,2048]{1,0:T(8,128)(2,1)S(1)} %bitcast.223, bf16[512,512]{1,0:T(8,128)(2,1)S(1)} %get-tuple-element.94, bf16[512,512]{1,0:T(8,128)(2,1)S(1)} %get-tuple-element.95, bf16[512,512]{1,0:T(8,128)(2,1)S(1)} %get-tuple-element.96, bf16[512,512]{1,0:T(8,128)(2,1)S(1)} %get-tuple-element.97), kind=kOutput, calls=%fused_computation.4 | convolution fusion | flops 4307550208 | bytes 12582912 | tf_op jit(solution)/shard_map/dot_general | solution.py:1426
  403.9 2.6 multiply_reduce_fusion.2
  407.2 6.3 copy.52
  413.6 22.6 %convolution_bitcast_fusion = f32[2048,1024]{1,0:T(8,128)S(1)} fusion(bf16[4,4,256,2048]{3,2,1,0:T(8,128)(2,1)} %get-tuple-element.71, bf16[4,4,256,1024]{3,2,1,0:T(8,128)(2,1)} %get-tuple-element.43.p_ref), kind=kOutput, calls=%fused_computation.11 | convolution fusion | flops 17179869184 | bytes 33554432 | tf_op jit(solution)/shard_map/td,tf->df/dot_general | solution.py:1439
  437.0 2.3 pad_maximum_fusion.1
  439.3 2.3 pad_maximum_fusion
  442.7 9.1 %add_convert_fusion = bf16[2048,2048]{1,0:T(8,128)(2,1)S(1)} fusion(bf16[2048,2048]{1,0:T(8,128)(2,1)} %collective-permute-done, bf16[512,2048]{1,0:T(8,128)(2,1)} %bitcast.222, bf16[512,512]{1,0:T(8,128)(2,1)} %get-tuple-element.91, bf16[512,512]{1,0:T(8,128)(2,1)} %get-tuple-element.92, bf16[512,512]{1,0:T(8,128)(2,1)} %get-tuple-element.93, ...), kind=kOutput, calls=%fused_computation.2 | convolution fusion | flops 4324327424 | bytes 20971520 | tf_op jit(solution)/shard_map/dot_general | solution.py:1426
  452.0 3.0 copy-done.22
  455.3 1.8 collective-permute-start.2
  457.2 13.8 %fusion = f32[2,256,2048]{2,1,0:T(8,128)} fusion(bf16[2,256,4096]{2,1,0:T(8,128)(2,1)S(1)} %bitcast.192, bf16[4096,2048]{1,0:T(8,128)(2,1)} %all-gather.2.cloned.1.call-done), kind=kOutput, calls=%fused_computation | convolution fusion | flops 8589934592 | bytes 25165824 | tf_op jit(solution)/shard_map/tf,td->fd/dot_general | solution.py:1436
  471.0 37.3 %line_gather.3 = bf16[4,128,2048]{2,1,0:T(8,128)(2,1)S(1)} custom-call(bf16[128,2048]{1,0:T(8,128)(2,1)S(1)} %fusion.52.refs_0_), custom_call_target="tpu_custom_call" | custom-call | tf_op jit(solution)/shard_map/line_gather/pallas_call | solution.py:513
  508.4 1.3 convolution_convert_fusion.4
  511.4 1.3 copy-done.6
  512.9 1.6 multiply_reduce_fusion
  514.5 2.2 convolution_convert_fusion.6
  523.4 3.1 fusion.31
  526.6 1.8 collective-permute-start.4
  528.5 5.5 line_total.3
  534.6 6.6 convolution_convert_fusion
  541.3 2.7 convolution_convert_fusion.2
  544.9 4.8 fusion.9
  549.7 1.7 collective-permute-done.3
  551.5 2.8 fusion.28
  554.2 1.5 pad_maximum_fusion.3.e_ref
  555.7 103.7 %finish_sums.1 = (bf16[16,128,512]{2,1,0:T(8,128)(2,1)}, bf16[16,128,512]{2,1,0:T(8,128)(2,1)}, bf16[16,128,512]{2,1,0:T(8,128)(2,1)}, bf16[16,128,512]{2,1,0:T(...) custom-call(bf16[16,128,1536]{2,1,0:T(8,128)(2,1)} %bitcast.190, ...), custom_call_target="tpu_custom_call" | custom-call | tf_op jit(solution)/shard_map/finish_sums/pallas_call | solution.py:1162
  661.0 1.6 slice_bitcast_fusion.4
  662.5 1.4 slice.110
  664.0 4.2 bitcast_convert_fusion
  668.2 5.3 copy.50
  673.5 4.3 bitcast_convert_fusion.1
  677.9 2.7 bitcast_convert_fusion.2
  680.7 2.7 bitcast_convert_fusion.3
  684.4 1.6 add_convert_fusion.5
  (192 shorter events, 27.4 us)
Async XLA Ops:
  7.2 96.3 %copy-start = (bf16[512,2048]{1,0:T(8,128)(2,1)S(1)}, bf16[512,2048]{1,0:T(8,128)(2,1)}, u32[]{:S(2)}) copy-start(bf16[512,2048]{1,0:T(8,128)(2,1)} %param.25) | copy-start | bytes 6291460
  7.2 164.8 %all-gather.2.cloned.1.call-start = ((), (), s32[]{:S(2)}) async-start(), calls=%async_computation | async-start | bytes 17301504 | tf_op jit(solution)/shard_map/all_gather | solution.py:1513
  7.9 651.5 %all-reduce.2.cloned.1.call-start = ((), (), s32[]{:S(2)}) async-start(), calls=%async_computation.1 | async-start | bytes 393216 | tf_op jit(solution)/shard_map/psum | solution.py:1567
  8.0 76.4 %copy-start.58 = (bf16[2048,512]{1,0:T(8,128)(2,1)S(1)}, bf16[2048,512]{1,0:T(8,128)(2,1)}, u32[]{:S(2)}) copy-start(bf16[2048,512]{1,0:T(8,128)(2,1)} %param.20) | copy-start | bytes 6291460
  9.4 75.0 %copy-start.50 = (f32[128]{0:T(128)}, f32[128]{0:T(128)S(1)}, u32[]{:S(2)}) copy-start(f32[128]{0:T(128)S(1)} %add_rsqrt_fusion.3) | copy-start | bytes 1540
  84.3 14.3 %copy-start.1 = (bf16[4,128,2048]{2,1,0:T(8,128)(2,1)}, bf16[4,128,2048]{2,1,0:T(8,128)(2,1)S(1)}, u32[]{:S(2)}) copy-start(bf16[4,128,2048]{2,1,0:T(8,128)(2,1)S(1)} %line_gather.2) | copy-start | bytes 6291460
  86.7 8.7 %copy-start.17 = (f32[512,512]{0,1:T(8,128)}, f32[512,512]{0,1:T(8,128)S(1)}, u32[]{:S(2)}) copy-start(f32[512,512]{0,1:T(8,128)S(1)} %get-tuple-element.133) | copy-start | bytes 3145732
  86.7 8.4 %copy-start.49 = (s32[1,512]{1,0:T(1,128)S(1)}, s32[1,512]{1,0:T(1,128)}, u32[]{:S(2)}) copy-start(s32[1,512]{1,0:T(1,128)} %param.17) | copy-start | bytes 6148
  86.7 8.7 %copy-start.47 = (f32[512]{0:T(512)S(1)}, f32[512]{0:T(512)}, u32[]{:S(2)}) copy-start(f32[512]{0:T(512)} %param.23) | copy-start | bytes 6148
  88.0 8.0 %copy-start.14 = (f32[512,512]{0,1:T(8,128)}, f32[512,512]{0,1:T(8,128)S(1)}, u32[]{:S(2)}) copy-start(f32[512,512]{0,1:T(8,128)S(1)} %get-tuple-element.131) | copy-start | bytes 3145732
  88.0 7.5 %copy-start.48 = (f32[512]{0:T(512)S(1)}, f32[512]{0:T(512)}, u32[]{:S(2)}) copy-start(f32[512]{0:T(512)} %param.24) | copy-start | bytes 6148
  97.6 4.4 copy-start.5
  97.7 3.1 copy-start.54
  104.8 66.1 %copy-start.45 = (f32[2048]{0:T(1024)S(1)}, f32[2048]{0:T(1024)}, u32[]{:S(2)}) copy-start(f32[2048]{0:T(1024)} %param.26) | copy-start | bytes 24580
  104.8 66.3 %copy-start.44 = (bf16[2048,16]{0,1:T(8,128)(2,1)S(1)}, bf16[2048,16]{0,1:T(8,128)(2,1)}, u32[]{:S(2)}) copy-start(bf16[2048,16]{0,1:T(8,128)(2,1)} %param.27) | copy-start | bytes 196612
  168.6 2.8 copy-start.52
  388.1 3.8 copy-start.53
  392.0 11.9 %copy-start.8 = (f32[128,2048]{1,0:T(8,128)S(1)}, f32[128,2048]{1,0:T(8,128)}, u32[]{:S(2)}) copy-start(f32[128,2048]{1,0:T(8,128)} %copy-done.7) | copy-start | bytes 3145732
  401.7 40.3 %collective-permute-start = (bf16[2048,2048]{1,0:T(8,128)(2,1)}, bf16[2048,2048]{1,0:T(8,128)(2,1)}, u32[]{:S(2)}, u32[]{:S(2)}) collective-permute-start(bf16[2048,2048]{1,0:T(8,128)(2,1)} %convolution_convert_fusion.1), channel_id=1, source_target_pairs={{0,4},{4,0},{8,12},{12,8},{16,20},{20,16},{24,28},{28,24},{1,5},{5... | collective-permute-start | bytes 25165832 | tf_op jit(solution)/shard_map/ppermute | solution.py:1199
  451.7 3.3 copy-start.22
  455.2 53.1 %collective-permute-start.1 = (bf16[2,2,128,2048]{3,2,1,0:T(8,128)(2,1)S(1)}, bf16[2,2,128,2048]{3,2,1,0:T(8,128)(2,1)S(1)}, u32[]{:S(2)}, u32[]{:S(2)}) collective-permute-start(bf16[2,2,128,2048]{3,2,1,0:T(8,128)(2,1)S(1)} %pad_maximum_fusion.2), channel_id=1, source_target_pairs={{0,8},{4,12},{8,0},{12,4},{16,24},{20,28},{24,16},{28,20},{1,9},{5... | collective-permute-start | bytes 6291464 | tf_op jit(solution)/shard_map/ppermute | solution.py:1199
  455.3 53.1 %collective-permute-start.2 = (bf16[2,2,128,2048]{3,2,1,0:T(8,128)(2,1)S(1)}, bf16[2,2,128,2048]{3,2,1,0:T(8,128)(2,1)S(1)}, u32[]{:S(2)}, u32[]{:S(2)}) collective-permute-start(bf16[2,2,128,2048]{3,2,1,0:T(8,128)(2,1)S(1)} %stack.60), channel_id=1, source_target_pairs={{0,16},{4,20},{8,24},{12,28},{16,0},{20,4},{24,8},{28,12},{1,17},{... | collective-permute-start | bytes 6291464 | tf_op jit(solution)/shard_map/ppermute | solution.py:1199
  508.4 3.1 copy-start.36
  508.4 4.4 copy-start.6
  508.4 4.5 copy-start.42
  523.4 10.6 %copy-start.13 = (f32[512,4,128]{0,2,1:T(8,128)S(1)}, f32[512,4,128]{0,2,1:T(8,128)}, u32[]{:S(2)}) copy-start(f32[512,4,128]{0,2,1:T(8,128)} %copy-done.12) | copy-start | bytes 3145732
  523.4 10.6 %copy-start.19 = (f32[512,512]{0,1:T(8,128)S(1)}, f32[512,512]{0,1:T(8,128)}, u32[]{:S(2)}) copy-start(f32[512,512]{0,1:T(8,128)} %copy-done.17) | copy-start | bytes 3145732
  523.4 10.9 %copy-start.11 = (f32[512,4,128]{0,2,1:T(8,128)S(1)}, f32[512,4,128]{0,2,1:T(8,128)}, u32[]{:S(2)}) copy-start(f32[512,4,128]{0,2,1:T(8,128)} %copy-done.10) | copy-start | bytes 3145732
  523.4 10.9 %copy-start.16 = (f32[512,512]{0,1:T(8,128)S(1)}, f32[512,512]{0,1:T(8,128)}, u32[]{:S(2)}) copy-start(f32[512,512]{0,1:T(8,128)} %copy-done.14) | copy-start | bytes 3145732
  526.5 8.0 %copy-start.2 = (bf16[4,128,2048]{2,1,0:T(8,128)(2,1)S(1)}, bf16[4,128,2048]{2,1,0:T(8,128)(2,1)}, u32[]{:S(2)}) copy-start(bf16[4,128,2048]{2,1,0:T(8,128)(2,1)} %copy-done.1) | copy-start | bytes 6291460
  526.6 8.0 %copy-start.62 = (bf16[4,128,512]{2,1,0:T(8,128)(2,1)S(1)}, bf16[4,128,512]{2,1,0:T(8,128)(2,1)}, u32[]{:S(2)}) copy-start(bf16[4,128,512]{2,1,0:T(8,128)(2,1)} %convolution_convert_fusion.6) | copy-start | bytes 1572868
  526.6 24.8 %collective-permute-start.3 = (bf16[2,128,2048]{2,1,0:T(8,128)(2,1)S(1)}, bf16[2,128,2048]{2,1,0:T(8,128)(2,1)S(1)}, u32[]{:S(2)}, u32[]{:S(2)}) collective-permute-start(bf16[2,128,2048]{2,1,0:T(8,128)(2,1)S(1)} %get-tuple-element.86), channel_id=1, source_target_pairs={{0,16},{4,20},{8,24},{12,28},{16,0},{20,4},{24,8},{28,12},{1,17},{... | collective-permute-start | bytes 3145736 | tf_op jit(solution)/shard_map/ppermute | solution.py:1199
  526.6 24.8 %collective-permute-start.4 = (bf16[2,128,2048]{2,1,0:T(8,128)(2,1)S(1)}, bf16[2,128,2048]{2,1,0:T(8,128)(2,1)S(1)}, u32[]{:S(2)}, u32[]{:S(2)}) collective-permute-start(bf16[2,128,2048]{2,1,0:T(8,128)(2,1)S(1)} %get-tuple-element.87), channel_id=1, source_target_pairs={{0,8},{4,12},{8,0},{12,4},{16,24},{20,28},{24,16},{28,20},{1,9},{5... | collective-permute-start | bytes 3145736 | tf_op jit(solution)/shard_map/ppermute | solution.py:1199
  534.6 6.7 copy-start.4
  534.6 6.7 copy-start.61
  541.3 2.7 copy-start.55
  541.3 3.6 copy-start.59
  544.9 6.6 copy-start.35
  544.9 6.6 copy-start.37
  673.5 4.4 copy-start.33
  677.9 2.7 copy-start.32
  680.6 2.8 copy-start.9
  680.6 2.8 copy-start.31
  680.6 2.8 copy-start.46
  680.6 2.8 copy-start.51
  680.6 3.7 copy-start.21
  680.7 3.7 copy-start.25
  680.7 3.7 copy-start.40
  (22 other events, 34.7 us)
Sparse Core Ops, SparseCore 0:
  11.0 154.3 all-gather.1
  407.4 123.8 all-reduce.1
